TPU v7x, 32 devices: a whole 2x2x4 slice. The times are simulated.
32 devices in a mesh: row: 8 (over z, y), col: 4 (over x, core).
Axes of the slice: x: 2, y: 2, z: 4, core: 2. Of those that a mesh axis runs over, the one named last changes fastest.
Arguments:
- upper: bfloat16 [4096, 8, 4, 128], P('row', None, 'col'), as said below
- signs: int32 [4096, 512], P(('row', 'col')), may hold values from 0 to 1
- weights: float32 [4096], P(('row', 'col')), may hold values from 0.5 to 2
- components: float32 [2], replicated, may hold values from 0.3 to 3
Outputs:
- applied: float32 [4096, 512], P(('row', 'col'))
Inputs may be any that keep to these rules, and one draw needn't show every extreme that they name: upper's first dimension and its flattened column index count the same samples in the same order.
All inputs are finite; a program needn't handle non-finite values.
Results may differ from a plain program's by a relative error of at most 0.0055.
Values may be sent and summed in bfloat16 or wider, within the bound.
No kernel may reach another device: no remote copies, remote signals or barrier semaphores. Data moves between devices by JAX's collectives and lax.ppermute only.
A program may use at most 128 MiB of HBM per device.

v0:
```python
import jax
import jax.numpy as jnp
from jax import lax
from jax.sharding import PartitionSpec as P


def body(upper, signs, weights, components):
    rows, ntiles, single, fine = upper.shape
    row_index = lax.axis_index("row")
    col_index = lax.axis_index("col")
    flat = upper.reshape(rows, ntiles * fine)
    probes = ((2 * signs - 1).astype(jnp.float32) * weights[:, None]).astype(jnp.bfloat16)
    q_rows = lax.all_gather(probes, "col", axis=0, tiled=True)
    zero = jnp.zeros((), jnp.bfloat16)
    rowpos = lax.broadcasted_iota(jnp.int32, (rows, ntiles, fine), 0)
    tilepos = lax.broadcasted_iota(jnp.int32, (rows, ntiles, fine), 1)
    colpos = col_index * fine + lax.broadcasted_iota(jnp.int32, (rows, ntiles, fine), 2)
    beyond = tilepos > row_index
    onside = tilepos == row_index
    keep_up = (beyond | onside & (colpos >= rowpos)).reshape(rows, ntiles * fine)
    keep_strict = (beyond | onside & (colpos > rowpos)).reshape(rows, ntiles * fine)
    masked_a = jnp.where(keep_up, flat, zero)
    masked_b = jnp.where(keep_strict, flat, zero)
    columns = masked_a
    direct = jnp.dot(
        columns,
        lax.all_gather(probes, "row", axis=0, tiled=True),
        preferred_element_type=jnp.float32,
    )
    columns = masked_b
    mirrored = lax.psum_scatter(
        lax.dot_general(
            columns, q_rows, (((0,), (0,)), ((), ())), preferred_element_type=jnp.float32
        ).astype(jnp.bfloat16),
        "row",
        scatter_dimension=0,
        tiled=True,
    ).astype(jnp.float32)
    summed = lax.psum_scatter(direct, "col", scatter_dimension=0, tiled=True)
    return components[0] * (summed + mirrored) + components[1] * probes.astype(jnp.float32)


def solution(mesh):
    return jax.shard_map(
        body,
        mesh=mesh,
        in_specs=(P("row", None, "col", None), P(("row", "col"), None), P(("row", "col")), P()),
        out_specs=P(("row", "col"), None),
        check_vma=False,
    )
```

profile of v0, /device:TPU:0, one launch (start us, length us, event | category | flops | bytes accessed | tf_op | source)
XLA Modules:
  0.0 154.1 jit_solution(2603484826157275666)
XLA Ops:
  6.5 0.0 copy-start.3
  6.5 0.0 all-gather.2.cloned.1.call-start
  6.5 1.8 %multiply_convert_fusion = bf16[128,512]{1,0:T(8,128)(2,1)} fusion(s32[128,512]{1,0:T(8,128)} %param.5, f32[128]{0:T(128)} %param.6), kind=kLoop, calls=%fused_computation.23 | loop fusion | flops 327680 | bytes 393728 | tf_op jit(solution)/shard_map/convert_element_type | solution.py:12
  8.3 0.0 all-gather.2.cloned.1.call-update
  8.3 0.0 reduce-scatter.5.cloned.1.call-start
  8.4 8.8 %all_gather.7 = bf16[512,512]{1,0:T(8,128)(2,1)S(1)} all-gather(bf16[128,512]{1,0:T(8,128)(2,1)} %multiply_convert_fusion), channel_id=1, replica_groups=mesh['row'=8,'col'=4] {'col'}, dimensions={0}, use_global_device_ids=true | all-gather | bytes 655360 | tf_op jit(solution)/shard_map/all_gather | solution.py:13
  17.3 0.1 broadcast_bitcast_fusion.1
  17.3 0.1 broadcast_bitcast_fusion.2
  17.4 0.0 copy-done.3
  17.4 1.8 %convolution_convert_fusion = bf16[1024,512]{1,0:T(8,128)(2,1)} fusion(bf16[512,512]{1,0:T(8,128)(2,1)S(1)} %all_gather.7, s32[1024]{0:T(1024)S(1)} %broadcast_bitcast_fusion, pred[1024]{0:T(1024)(128)(4,1)S(1)} %broadcast_bitcast_fusion.1, pred[1024]{0:T(1024)(128)(4,1)S(1)} %broadcast_bitcast_fusion.2, bf16[64,8,8,128]{3,2,1,0:T(8,128)(2,1)S(1)} %bitcast.22), kind=kOutput, calls=%fused_computation.8 | convolution fusion | flops 539492352 | bytes 2627584 | tf_op jit(solution)/shard_map/dot_general | solution.py:32
  19.2 0.0 reduce-scatter.5.cloned.1.call-update
  19.2 0.0 reduce-scatter.3.cloned.1.call-start
  19.3 33.1 %all-gather.2.cloned.1.call-done = bf16[1024,512]{1,0:T(8,128)(2,1)} async-done(((bf16[128,512]{1,0:T(8,128)(2,1)}), bf16[1024,512]{1,0:T(8,128)(2,1)}) %all-gather.2.cloned.1.call-update) | async-done | bytes 1048592 | tf_op jit(solution)/shard_map/all_gather | solution.py:27
  52.4 3.0 %fusion.7 = f32[512,512]{1,0:T(8,128)} fusion(bf16[1024,512]{1,0:T(8,128)(2,1)} %all-gather.2.cloned.1.call-done, s32[1024]{0:T(1024)S(1)} %broadcast_bitcast_fusion, pred[1024]{0:T(1024)(128)(4,1)S(1)} %broadcast_bitcast_fusion.1, pred[1024]{0:T(1024)(128)(4,1)S(1)} %broadcast_bitcast_fusion.2, bf16[64,8,8,128]{3,2,1,0:T(8,128)(2,1)S(1)} %bitcast.23), kind=kOutput, calls=%fused_computation.9 | convolution fusion | flops 538968064 | bytes 3151872 | tf_op jit(solution)/shard_map/dot_general | solution.py:25
  55.3 0.0 copy-start.2
  55.3 0.0 copy-start
  55.3 0.0 reduce-scatter.3.cloned.1.call-update
  55.4 0.6 copy-done.2
  56.0 0.6 fusion.23
  56.6 61.3 %reduce-scatter.5.cloned.1.call-done = bf16[128,512]{1,0:T(8,128)(2,1)} async-done(((bf16[1024,512]{1,0:T(8,128)(2,1)}), bf16[128,512]{1,0:T(8,128)(2,1)}) %reduce-scatter.5.cloned.1.call-update) | async-done | bytes 131088 | tf_op jit(solution)/shard_map/reduce_scatter | solution.py:31
  117.9 26.6 %reduce-scatter.3.cloned.1.call-done = f32[128,512]{1,0:T(8,128)} async-done(((f32[512,512]{1,0:T(8,128)}), f32[128,512]{1,0:T(8,128)}) %reduce-scatter.3.cloned.1.call-update) | async-done | bytes 262160 | tf_op jit(solution)/shard_map/reduce_scatter | solution.py:39
  144.5 0.0 copy-done
  144.5 0.0 copy-done.1
  144.5 3.1 %multiply_add_fusion = f32[128,512]{1,0:T(8,128)} fusion(f32[128,512]{1,0:T(8,128)} %reduce-scatter.3.cloned.1.call-done, bf16[128,512]{1,0:T(8,128)(2,1)} %reduce-scatter.5.cloned.1.call-done, f32[]{:T(128)} %bitcast.4, f32[]{:T(128)} %bitcast, f32[128]{0:T(128)S(1)} %copy-done.1, s32[128,512]{1,0:T(8,128)S(1)} %copy-done), kind=kLoop, calls=%fused_computation.22 | loop fusion | flops 720896 | bytes 918024 | tf_op jit(solution)/shard_map/add | solution.py:40
  (4 shorter events, 0.0 us)
Async XLA Ops:
  6.5 10.9 %copy-start.3 = (bf16[512,8,1,128]{3,1,2,0:T(8,128)(2,1)S(1)}, bf16[512,8,1,128]{3,1,2,0:T(8,128)(2,1)}, u32[]{:S(2)}) copy-start(bf16[512,8,1,128]{3,1,2,0:T(8,128)(2,1)} %param.4) | copy-start | bytes 3145732
  6.5 45.8 %all-gather.2.cloned.1.call-start = ((), (), s32[]{:S(2)}) async-start(), calls=%async_computation.2 | async-start | bytes 1179648 | tf_op jit(solution)/shard_map/all_gather | solution.py:27
  8.3 109.5 %reduce-scatter.5.cloned.1.call-start = ((), (), s32[]{:S(2)}) async-start(), calls=%async_computation.4 | async-start | bytes 1179648 | tf_op jit(solution)/shard_map/reduce_scatter | solution.py:31
  19.2 125.3 %reduce-scatter.3.cloned.1.call-start = ((), (), s32[]{:S(2)}) async-start(), calls=%async_computation.3 | async-start | bytes 1310720 | tf_op jit(solution)/shard_map/reduce_scatter | solution.py:39
  55.3 0.7 copy-start.2
  55.3 89.2 %copy-start = (s32[128,512]{1,0:T(8,128)S(1)}, s32[128,512]{1,0:T(8,128)}, u32[]{:S(2)}) copy-start(s32[128,512]{1,0:T(8,128)} %param.5) | copy-start | bytes 786436
  55.3 89.2 %copy-start.1 = (f32[128]{0:T(128)S(1)}, f32[128]{0:T(128)}, u32[]{:S(2)}) copy-start(f32[128]{0:T(128)} %param.6) | copy-start | bytes 1540
Sparse Core Ops, SparseCore 0:
  9.5 42.8 all-gather.1
  55.8 62.0 reduce-scatter.4
  120.6 23.8 reduce-scatter.2
where the time goes:
time: 154 us
  waiting for transfers between devices  121 us (79%)
  between operations  13.1 us (9%)
  blocking collectives  8.83 us (6%)
  other arithmetic  4.85 us (3%)
  matrix products  4.75 us (3%)
    reduce_scatter x1, waiting for transfers between devices, body(): lax.psum_scatter(lax.dot_general(columns, q_rows, (((0,), (0,)), ((), ())...  61.3 us
    all_gather x1, waiting for transfers between devices, body(): lax.all_gather(probes, 'row', axis=0, tiled=True)  33.1 us
    reduce_scatter x1, waiting for transfers between devices, body(): summed = lax.psum_scatter(direct, 'col', scatter_dimension=0, tiled=True)  26.6 us
    all_gather x1, blocking collectives, body(): q_rows = lax.all_gather(probes, 'col', axis=0, tiled=True)  8.83 us
  transfers between devices with their start and end apart: 3, of which 3 were waited for; matrix products, arithmetic and copies ran while one was open for 4% of the time, Pallas kernels for 0%

commit v1 on v0

v1 whole, which is shorter than its diff:
```python
import jax
import jax.numpy as jnp
from jax import lax
from jax.sharding import PartitionSpec as P


def solution(mesh):
    nrow, ncol = mesh.shape["row"], mesh.shape["col"]
    ny, nk = 2, 2
    nz, nx = nrow // ny, ncol // nk
    both = ("row", "col")

    def place(z, y, x, k):
        return ((z * ny + y) * nx + x) * nk + k

    spots = [(z, y, x, k) for z in range(nz) for y in range(ny) for x in range(nx) for k in range(nk)]

    def down(d):
        return [(place(z, y, x, k), place(z - d, y, x, k)) for z, y, x, k in spots if z >= d]

    def up(d):
        return [(place(z, y, x, k), place(z + d, y, x, k)) for z, y, x, k in spots if z + d < nz]

    def shift(s, e):
        return [(place(z, y, x, k), place(z, y ^ s, (x + e) % nx, k)) for z, y, x, k in spots]

    other_core = [(place(z, y, x, k), place(z, y, x, 1 - k)) for z, y, x, k in spots]
    away = [(s, e) for s in range(ny) for e in range(nx) if (s, e) != (0, 0)]

    def body(upper, signs, weights, components):
        rows, ntiles, _, fine = upper.shape
        npro = signs.shape[1]
        r, c = lax.axis_index("row"), lax.axis_index("col")
        z, y, x, k = r // ny, r % ny, c // nk, c % nk
        f32, bf16 = jnp.float32, jnp.bfloat16
        probes = ((2 * signs - 1).astype(f32) * weights[:, None]).astype(bf16)
        flat = upper.reshape(rows, ntiles * fine)

        def column(d, side):
            tile = ((z + d) % nz) * ny + side
            return lax.dynamic_slice_in_dim(flat, tile * fine, fine, 1)

        rowpos = lax.broadcasted_iota(jnp.int32, (rows, fine), 0)
        colpos = c * fine + lax.broadcasted_iota(jnp.int32, (rows, fine), 1)
        zero = jnp.zeros((), bf16)
        diag_block = column(0, y)
        own = jnp.concatenate(
            [jnp.where(colpos > rowpos, diag_block, zero)] + [column(d, y) for d in range(1, nz)], axis=1
        )
        give = jnp.concatenate(
            [jnp.where(y == 0, column(0, 1 - y), zero)] + [column(d, 1 - y) for d in range(1, nz)], axis=1
        )
        oth = lax.ppermute(give, both, shift(1, 0))
        diag = jnp.sum(jnp.where(colpos == rowpos, diag_block.astype(f32), 0.0), axis=0)

        mine = {(0, 0): probes}
        for s, e in away:
            mine[s, e] = lax.ppermute(probes, both, shift(s, (nx - e) % nx))
        pcat = jnp.concatenate([probes] + [lax.ppermute(probes, both, down(d)) for d in range(1, nz)], axis=0)

        stack = jnp.stack([jnp.stack([mine[s, e] for e in range(nx)]) for s in range(ny)])
        got = lax.ppermute(stack, both, other_core)
        pair = jnp.where(k == 0, jnp.stack([stack, got], axis=2), jnp.stack([got, stack], axis=2))
        pair = lax.dynamic_slice_in_dim(jnp.concatenate([pair, pair], axis=1), (nx - x) % nx, nx, 1)
        q_own = pair[0].reshape(rows, npro)
        q_oth = pair[1].reshape(rows, npro)

        def tdot(a, b):
            return lax.dot_general(a, b, (((0,), (0,)), ((), ())), preferred_element_type=f32)

        mirrored = tdot(own, q_own) + tdot(oth, q_oth)
        m0 = mirrored[:fine]
        ms = mirrored[fine:].astype(bf16)
        total = m0
        for d in range(nz - 1, 0, -1):
            total = total + lax.ppermute(ms[(d - 1) * fine : d * fine], both, up(d)).astype(f32)

        d_own = jnp.dot(own, pcat, preferred_element_type=f32).reshape(nx, nk, fine, npro)
        d_oth = jnp.dot(oth, pcat, preferred_element_type=f32).reshape(nx, nk, fine, npro)
        d_all = jnp.stack([d_own, d_oth])
        keep = lax.dynamic_index_in_dim(d_all, k, 2, keepdims=False)
        part = keep + lax.ppermute(
            lax.dynamic_index_in_dim(d_all, 1 - k, 2, keepdims=False).astype(bf16), both, other_core
        ).astype(f32)
        total = total + lax.dynamic_index_in_dim(part[0], x, 0, keepdims=False)
        for s, e in away:
            piece = lax.dynamic_index_in_dim(part[s], (x + e) % nx, 0, keepdims=False).astype(bf16)
            total = total + lax.ppermute(piece, both, shift(s, e)).astype(f32)
        pf = probes.astype(f32)
        total = total + diag[:, None] * pf
        return components[0] * total + components[1] * pf

    return jax.shard_map(
        body,
        mesh=mesh,
        in_specs=(P("row", None, "col", None), P(both, None), P(both), P()),
        out_specs=P(both, None),
        check_vma=False,
    )
```

time: 154 us -> 53.1 us (0.34)
  waiting for transfers between devices: 121 us -> 13.8 us
  starting transfers between devices: 0.09 us -> 24.1 us
  between operations: 13.1 us -> 0.44 us
  blocking collectives: 8.83 us -> 0 us
  local copies, waits for them, and re-layouts: 1.39 us -> 4.47 us
    reduce_scatter x2 -> x0, waiting for transfers between devices: 87.9 us -> none  [the longest x1 61.3 us: body(): lax.psum_scatter(lax.dot_general(columns, q_rows, (((0,), (0,)), ((), ())...]
    all_gather x1 -> x0, waiting for transfers between devices: 33.1 us -> none  [body(): lax.all_gather(probes, 'row', axis=0, tiled=True)]
    ppermute x0 -> x15, starting transfers between devices: none -> 24.1 us  [the longest x3 9.96 us: body(): lax.ppermute(ms[(d - 1) * fine:d * fine], both, up(d)).astype(f32)]
    ppermute x0 -> x15, waiting for transfers between devices: none -> 13.8 us  [the longest x3 8.29 us: body(): lax.ppermute(probes, both, down(d))]
    all_gather x1 -> x0, blocking collectives: 8.83 us -> none  [body(): q_rows = lax.all_gather(probes, 'col', axis=0, tiled=True)]
    dot_general x2 -> x4, matrix products: 4.75 us -> 3.61 us  [the longest x1 1.34 us: body(): jnp.dot(own, pcat, preferred_element_type=f32).reshape(nx, nk, fine, npro)]
    add x2 -> x3, other arithmetic: 3.06 us -> 3.29 us  [the longest x1 3.1 us: body(): return components[0] * total + components[1] * pf]
  transfers between devices with their start and end apart: 3 -> 15, of which waited for: 3 -> 3; matrix products, arithmetic and copies ran while one was open for 4% -> 19% of each run, Pallas kernels for 0% -> 0%
where the time goes in v1:
time: 53.1 us; the launch traced here: 52.8 us
  starting transfers between devices  24.1 us (45%)
  waiting for transfers between devices  13.8 us (26%)
  other arithmetic  6.3 us (12%)
  local copies, waits for them, and re-layouts  4.47 us (8%)
  matrix products  3.61 us (7%)
    ppermute x3, starting transfers between devices, body(): lax.ppermute(ms[(d - 1) * fine:d * fine], both, up(d)).astype(f32)  9.96 us
    ppermute x3, waiting for transfers between devices, body(): lax.ppermute(probes, both, down(d))  8.29 us
    ppermute x3, waiting for transfers between devices, body(): total = total + lax.ppermute(piece, both, shift(s, e)).astype(f32)  5.51 us
    ppermute x3, starting transfers between devices, body(): mine[s, e] = lax.ppermute(probes, both, shift(s, (nx - e) % nx))  4.6 us
    ppermute x3, starting transfers between devices, body(): lax.ppermute(probes, both, down(d))  3.88 us
    ppermute x3, starting transfers between devices, body(): total = total + lax.ppermute(piece, both, shift(s, e)).astype(f32)  3.55 us
    add x1, other arithmetic, body(): return components[0] * total + components[1] * pf  3.1 us
    ppermute x1, starting transfers between devices, body(): oth = lax.ppermute(give, both, shift(1, 0))  1.98 us
  transfers between devices with their start and end apart: 15, of which 3 were waited for; matrix products, arithmetic and copies ran while one was open for 19% of the time, Pallas kernels for 0%

profile of v1, /device:TPU:0, one launch (start us, length us, event | category | flops | bytes accessed | tf_op | source)
XLA Modules:
  0.0 52.8 jit_solution(10530717623297910304)
XLA Ops:
  0.0 1.0 %multiply_convert_fusion = bf16[128,512]{1,0:T(8,128)(2,1)S(1)} fusion(s32[128,512]{1,0:T(8,128)} %param.5, f32[128]{0:T(128)} %param.6), kind=kLoop, calls=%fused_computation.40 | loop fusion | flops 327680 | bytes 393728 | tf_op jit(solution)/shard_map/convert_element_type | solution.py:36
  1.0 1.3 %collective-permute-start.10 = (bf16[128,512]{1,0:T(8,128)(2,1)S(1)}, bf16[128,512]{1,0:T(8,128)(2,1)}, u32[]{:S(2)}, u32[]{:S(2)}) collective-permute-start(bf16[128,512]{1,0:T(8,128)(2,1)S(1)} %multiply_convert_fusion), channel_id=1, source_target_pairs={{24,0},{25,1},{26,2},{27,3},{28,4},{29,5},{30,6},{31,7}} | collective-permute-start | bytes 393224 | tf_op jit(solution)/shard_map/ppermute | solution.py:59
  2.3 4.0 %collective-permute-start.2 = (bf16[128,512]{1,0:T(8,128)(2,1)S(1)}, bf16[128,512]{1,0:T(8,128)(2,1)S(1)}, u32[]{:S(2)}, u32[]{:S(2)}) collective-permute-start(bf16[128,512]{1,0:T(8,128)(2,1)S(1)} %multiply_convert_fusion), channel_id=1, source_target_pairs={{0,6},{1,7},{2,4},{3,5},{4,2},{5,3},{6,0},{7,1},{8,14},{9,15},{10,... | collective-permute-start | bytes 393224 | tf_op jit(solution)/shard_map/ppermute | solution.py:58
  6.9 1.5 %copy.14 = bf16[64,8,8,128]{3,1,2,0:T(8,128)(2,1)S(1)} copy(bf16[64,8,8,128]{3,2,1,0:T(8,128)(2,1)} %bitcast.57) | data formatting | bytes 2097152
  8.5 1.0 %dynamic-slice_select_fusion = (bf16[512,128]{1,0:T(8,128)(2,1)S(1)}, bf16[512,128]{1,0:T(8,128)(2,1)S(1)}, bf16[512,128]{1,0:T(8,128)(2,1)S(1)}, bf16[512,128]{...) fusion(bf16[512,1024]{1,0:T(8,128)(2,1)S(1)} %bitcast.50, ...), kind=kLoop, calls=%fused_computation.46 | loop fusion | flops 196608 | bytes 2097697 | tf_op jit(solution)/shard_map/jit(_where)/select_n | solution.py:51
  9.5 2.0 %collective-permute-start.4 = (bf16[512,512]{1,0:T(8,128)(2,1)S(1)}, bf16[512,512]{1,0:T(8,128)(2,1)S(1)}, u32[]{:S(2)}, u32[]{:S(2)}) collective-permute-start(bf16[512,512]{1,0:T(8,128)(2,1)S(1)} %pad_maximum_fusion.2), channel_id=1, source_target_pairs={{0,4},{1,5},{2,6},{3,7},{4,0},{5,1},{6,2},{7,3},{8,12},{9,13},{10,... | collective-permute-start | bytes 1572872 | tf_op jit(solution)/shard_map/ppermute | solution.py:53
  11.7 1.3 %collective-permute-start.9 = (bf16[128,512]{1,0:T(8,128)(2,1)S(1)}, bf16[128,512]{1,0:T(8,128)(2,1)S(1)}, u32[]{:S(2)}, u32[]{:S(2)}) collective-permute-start(bf16[128,512]{1,0:T(8,128)(2,1)S(1)} %multiply_convert_fusion), channel_id=1, source_target_pairs={{16,0},{17,1},{18,2},{19,3},{20,4},{21,5},{22,6},{23,7},{24,8},{25... | collective-permute-start | bytes 393224 | tf_op jit(solution)/shard_map/ppermute | solution.py:59
  13.0 1.3 %collective-permute-start.8 = (bf16[128,512]{1,0:T(8,128)(2,1)S(1)}, bf16[128,512]{1,0:T(8,128)(2,1)S(1)}, u32[]{:S(2)}, u32[]{:S(2)}) collective-permute-start(bf16[128,512]{1,0:T(8,128)(2,1)S(1)} %multiply_convert_fusion), channel_id=1, source_target_pairs={{8,0},{9,1},{10,2},{11,3},{12,4},{13,5},{14,6},{15,7},{16,8},{17,9... | collective-permute-start | bytes 393224 | tf_op jit(solution)/shard_map/ppermute | solution.py:59
  14.6 8.3 %collective-permute-done.9 = bf16[128,512]{1,0:T(8,128)(2,1)S(1)} collective-permute-done((bf16[128,512]{1,0:T(8,128)(2,1)S(1)}, bf16[128,512]{1,0:T(8,128)(2,1)S(1)}, u32[]{:S(2)}, u32[]{:S(2)}) %collective-permute-start.9) | collective-permute-done | bytes 131104 | tf_op jit(solution)/shard_map/ppermute | solution.py:59
  22.9 1.3 %fusion.22 = f32[512,512]{1,0:T(8,128)S(1)} fusion(bf16[128,512]{1,0:T(8,128)(2,1)} %collective-permute-done.10, bf16[128,512]{1,0:T(8,128)(2,1)S(1)} %collective-permute-done.9, bf16[128,512]{1,0:T(8,128)(2,1)S(1)} %collective-permute-done.8, bf16[128,512]{1,0:T(8,128)(2,1)S(1)} %multiply_convert_fusion, bf16[512,128]{1,0:T(8,128)(2,1)S(1)} %get-tuple-element.11, ...), kind=kOutput, calls=%fused_computation.48 | convolution fusion | flops 272629760 | bytes 2097152 | tf_op jit(solution)/shard_map/dot_general | solution.py:78
  24.3 1.3 %fusion.21 = f32[512,512]{1,0:T(8,128)S(1)} fusion(bf16[512,512]{1,0:T(8,128)(2,1)S(1)} %collective-permute-done.4, bf16[128,512]{1,0:T(8,128)(2,1)} %collective-permute-done.10, bf16[128,512]{1,0:T(8,128)(2,1)S(1)} %collective-permute-done.9, bf16[128,512]{1,0:T(8,128)(2,1)S(1)} %collective-permute-done.8, bf16[128,512]{1,0:T(8,128)(2,1)S(1)} %multiply_convert_fusion), kind=kOutput, calls=%fused_computation.47 | convolution fusion | flops 270532608 | bytes 2097152 | tf_op jit(solution)/shard_map/dot_general | solution.py:79
  27.5 0.7 %fusion.29 = (bf16[128,512]{1,0:T(8,128)(2,1)S(1)}, bf16[128,512]{1,0:T(8,128)(2,1)}, bf16[128,512]{1,0:T(8,128)(2,1)}) fusion(bf16[512,512]{1,0:T(8,128)(2,1)S(1)} %get-tuple-element.24), kind=kLoop, calls=%fused_computation.62 | loop fusion | bytes 786432 | tf_op jit(solution)/shard_map/slice | solution.py:76
  28.2 6.2 %collective-permute-start.5 = (bf16[128,512]{1,0:T(8,128)(2,1)S(1)}, bf16[128,512]{1,0:T(8,128)(2,1)S(1)}, u32[]{:S(2)}, u32[]{:S(2)}) collective-permute-start(bf16[128,512]{1,0:T(8,128)(2,1)S(1)} %get-tuple-element.15), channel_id=1, source_target_pairs={{0,24},{1,25},{2,26},{3,27},{4,28},{5,29},{6,30},{7,31}} | collective-permute-start | bytes 393224 | tf_op jit(solution)/shard_map/ppermute | solution.py:76
  34.4 1.3 %collective-permute-start.7 = (bf16[128,512]{1,0:T(8,128)(2,1)}, bf16[128,512]{1,0:T(8,128)(2,1)S(1)}, u32[]{:S(2)}, u32[]{:S(2)}) collective-permute-start(bf16[128,512]{1,0:T(8,128)(2,1)} %get-tuple-element.16), channel_id=1, source_target_pairs={{0,8},{1,9},{2,10},{3,11},{4,12},{5,13},{6,14},{7,15},{8,16},{9,17... | collective-permute-start | bytes 393224 | tf_op jit(solution)/shard_map/ppermute | solution.py:76
  35.7 2.5 %collective-permute-start.6 = (bf16[128,512]{1,0:T(8,128)(2,1)}, bf16[128,512]{1,0:T(8,128)(2,1)S(1)}, u32[]{:S(2)}, u32[]{:S(2)}) collective-permute-start(bf16[128,512]{1,0:T(8,128)(2,1)} %get-tuple-element.17), channel_id=1, source_target_pairs={{0,16},{1,17},{2,18},{3,19},{4,20},{5,21},{6,22},{7,23},{8,24},{9,... | collective-permute-start | bytes 393224 | tf_op jit(solution)/shard_map/ppermute | solution.py:76
  38.4 0.7 %fusion.18 = bf16[128,512]{1,0:T(8,128)(2,1)} fusion(f32[1,2,128,512]{3,2,1,0:T(8,128)S(1)} %slice.53, s32[]{:T(128)S(6)} %select_n.152), kind=kLoop, calls=%fused_computation.43 | loop fusion | bytes 262148 | tf_op jit(solution)/shard_map/convert_element_type | solution.py:87
  39.1 1.7 %collective-permute-start.12 = (bf16[128,512]{1,0:T(8,128)(2,1)}, bf16[128,512]{1,0:T(8,128)(2,1)S(1)}, u32[]{:S(2)}, u32[]{:S(2)}) collective-permute-start(bf16[128,512]{1,0:T(8,128)(2,1)} %fusion.18), channel_id=1, source_target_pairs={{0,2},{1,3},{2,0},{3,1},{4,6},{5,7},{6,4},{7,5},{8,10},{9,11},{10,... | collective-permute-start | bytes 393224 | tf_op jit(solution)/shard_map/ppermute | solution.py:88
  40.9 0.7 %fusion.19 = (bf16[128,512]{1,0:T(8,128)(2,1)}, bf16[128,512]{1,0:T(8,128)(2,1)}) fusion(bf16[1,2,128,512]{3,2,1,0:T(8,128)(2,1)S(1)} %slice.54, s32[]{:T(128)S(6)} %select_n.154, s32[]{:T(128)S(6)} %select_n.152), kind=kLoop, calls=%fused_computation.44 | loop fusion | bytes 524296 | tf_op jit(solution)/shard_map/convert_element_type | solution.py:87
  41.6 0.6 %collective-permute-start.13 = (bf16[128,512]{1,0:T(8,128)(2,1)}, bf16[128,512]{1,0:T(8,128)(2,1)S(1)}, u32[]{:S(2)}, u32[]{:S(2)}) collective-permute-start(bf16[128,512]{1,0:T(8,128)(2,1)} %get-tuple-element.20), channel_id=1, source_target_pairs={{0,4},{1,5},{2,6},{3,7},{4,0},{5,1},{6,2},{7,3},{8,12},{9,13},{10,... | collective-permute-start | bytes 393224 | tf_op jit(solution)/shard_map/ppermute | solution.py:88
  42.2 1.2 %collective-permute-start.14 = (bf16[128,512]{1,0:T(8,128)(2,1)}, bf16[128,512]{1,0:T(8,128)(2,1)}, u32[]{:S(2)}, u32[]{:S(2)}) collective-permute-start(bf16[128,512]{1,0:T(8,128)(2,1)} %get-tuple-element.21), channel_id=1, source_target_pairs={{0,6},{1,7},{2,4},{3,5},{4,2},{5,3},{6,0},{7,1},{8,14},{9,15},{10,... | collective-permute-start | bytes 393224 | tf_op jit(solution)/shard_map/ppermute | solution.py:88
  43.4 0.6 %fusion.30 = (f32[1]{0:T(128)}, f32[1]{0:T(128)}) fusion(f32[2]{0:T(128)S(1)} %copy-done.5), kind=kLoop, calls=%fused_computation.63 | loop fusion | bytes 16 | tf_op jit(solution)/shard_map/slice | solution.py:91
  44.1 0.8 %collective-permute-done.12 = bf16[128,512]{1,0:T(8,128)(2,1)S(1)} collective-permute-done((bf16[128,512]{1,0:T(8,128)(2,1)}, bf16[128,512]{1,0:T(8,128)(2,1)S(1)}, u32[]{:S(2)}, u32[]{:S(2)}) %collective-permute-start.12) | collective-permute-done | bytes 131104 | tf_op jit(solution)/shard_map/ppermute | solution.py:88
  44.9 4.8 %collective-permute-done.13 = bf16[128,512]{1,0:T(8,128)(2,1)S(1)} collective-permute-done((bf16[128,512]{1,0:T(8,128)(2,1)}, bf16[128,512]{1,0:T(8,128)(2,1)S(1)}, u32[]{:S(2)}, u32[]{:S(2)}) %collective-permute-start.13) | collective-permute-done | bytes 131104 | tf_op jit(solution)/shard_map/ppermute | solution.py:88
  49.7 3.1 %fusion.10 = f32[128,512]{1,0:T(8,128)} fusion(f32[512,512]{1,0:T(8,128)S(1)} %get-tuple-element.25, bf16[128,512]{1,0:T(8,128)(2,1)} %collective-permute-done.14, bf16[128,512]{1,0:T(8,128)(2,1)S(1)} %collective-permute-done.13, bf16[128,512]{1,0:T(8,128)(2,1)S(1)} %collective-permute-done.12, f32[1,2,128,512]{3,2,1,0:T(8,128)S(1)} %slice.53, ...), kind=kLoop, calls=%fused_computation.25 | loop fusion | flops 1572864 | bytes 1836044 | tf_op jit(solution)/shard_map/add | solution.py:91
  (46 shorter events, 3.2 us)
Async XLA Ops:
  1.0 13.6 %collective-permute-start.10 = (bf16[128,512]{1,0:T(8,128)(2,1)S(1)}, bf16[128,512]{1,0:T(8,128)(2,1)}, u32[]{:S(2)}, u32[]{:S(2)}) collective-permute-start(bf16[128,512]{1,0:T(8,128)(2,1)S(1)} %multiply_convert_fusion), channel_id=1, source_target_pairs={{24,0},{25,1},{26,2},{27,3},{28,4},{29,5},{30,6},{31,7}} | collective-permute-start | bytes 393224 | tf_op jit(solution)/shard_map/ppermute | solution.py:59
  2.3 9.4 %collective-permute-start.2 = (bf16[128,512]{1,0:T(8,128)(2,1)S(1)}, bf16[128,512]{1,0:T(8,128)(2,1)S(1)}, u32[]{:S(2)}, u32[]{:S(2)}) collective-permute-start(bf16[128,512]{1,0:T(8,128)(2,1)S(1)} %multiply_convert_fusion), channel_id=1, source_target_pairs={{0,6},{1,7},{2,4},{3,5},{4,2},{5,3},{6,0},{7,1},{8,14},{9,15},{10,... | collective-permute-start | bytes 393224 | tf_op jit(solution)/shard_map/ppermute | solution.py:58
  6.3 6.7 %collective-permute-start.1 = (bf16[128,512]{1,0:T(8,128)(2,1)S(1)}, bf16[128,512]{1,0:T(8,128)(2,1)S(1)}, u32[]{:S(2)}, u32[]{:S(2)}) collective-permute-start(bf16[128,512]{1,0:T(8,128)(2,1)S(1)} %multiply_convert_fusion), channel_id=1, source_target_pairs={{0,4},{1,5},{2,6},{3,7},{4,0},{5,1},{6,2},{7,3},{8,12},{9,13},{10,... | collective-permute-start | bytes 393224 | tf_op jit(solution)/shard_map/ppermute | solution.py:58
  6.8 7.6 %collective-permute-start = (bf16[128,512]{1,0:T(8,128)(2,1)S(1)}, bf16[128,512]{1,0:T(8,128)(2,1)S(1)}, u32[]{:S(2)}, u32[]{:S(2)}) collective-permute-start(bf16[128,512]{1,0:T(8,128)(2,1)S(1)} %multiply_convert_fusion), channel_id=1, source_target_pairs={{0,2},{1,3},{2,0},{3,1},{4,6},{5,7},{6,4},{7,5},{8,10},{9,11},{10,... | collective-permute-start | bytes 393224 | tf_op jit(solution)/shard_map/ppermute | solution.py:58
  9.5 2.1 %copy-start = (s32[128,512]{1,0:T(8,128)S(1)}, s32[128,512]{1,0:T(8,128)}, u32[]{:S(2)}) copy-start(s32[128,512]{1,0:T(8,128)} %param.5) | copy-start | bytes 786436
  9.5 2.1 %copy-start.4 = (f32[128]{0:T(128)S(1)}, f32[128]{0:T(128)}, u32[]{:S(2)}) copy-start(f32[128]{0:T(128)} %param.6) | copy-start | bytes 1540
  9.5 14.7 %collective-permute-start.4 = (bf16[512,512]{1,0:T(8,128)(2,1)S(1)}, bf16[512,512]{1,0:T(8,128)(2,1)S(1)}, u32[]{:S(2)}, u32[]{:S(2)}) collective-permute-start(bf16[512,512]{1,0:T(8,128)(2,1)S(1)} %pad_maximum_fusion.2), channel_id=1, source_target_pairs={{0,4},{1,5},{2,6},{3,7},{4,0},{5,1},{6,2},{7,3},{8,12},{9,13},{10,... | collective-permute-start | bytes 1572872 | tf_op jit(solution)/shard_map/ppermute | solution.py:53
  11.7 11.2 %collective-permute-start.9 = (bf16[128,512]{1,0:T(8,128)(2,1)S(1)}, bf16[128,512]{1,0:T(8,128)(2,1)S(1)}, u32[]{:S(2)}, u32[]{:S(2)}) collective-permute-start(bf16[128,512]{1,0:T(8,128)(2,1)S(1)} %multiply_convert_fusion), channel_id=1, source_target_pairs={{16,0},{17,1},{18,2},{19,3},{20,4},{21,5},{22,6},{23,7},{24,8},{25... | collective-permute-start | bytes 393224 | tf_op jit(solution)/shard_map/ppermute | solution.py:59
  13.0 9.9 %collective-permute-start.8 = (bf16[128,512]{1,0:T(8,128)(2,1)S(1)}, bf16[128,512]{1,0:T(8,128)(2,1)S(1)}, u32[]{:S(2)}, u32[]{:S(2)}) collective-permute-start(bf16[128,512]{1,0:T(8,128)(2,1)S(1)} %multiply_convert_fusion), channel_id=1, source_target_pairs={{8,0},{9,1},{10,2},{11,3},{12,4},{13,5},{14,6},{15,7},{16,8},{17,9... | collective-permute-start | bytes 393224 | tf_op jit(solution)/shard_map/ppermute | solution.py:59
  14.4 8.5 %copy-start.1 = (bf16[512,128]{1,0:T(8,128)(2,1)S(1)}, bf16[512,128]{1,0:T(8,128)(2,1)}, u32[]{:S(2)}) copy-start(bf16[512,128]{1,0:T(8,128)(2,1)} %get-tuple-element.12) | copy-start | bytes 393220
  14.4 8.5 %copy-start.2 = (bf16[512,128]{1,0:T(8,128)(2,1)S(1)}, bf16[512,128]{1,0:T(8,128)(2,1)}, u32[]{:S(2)}) copy-start(bf16[512,128]{1,0:T(8,128)(2,1)} %get-tuple-element.13) | copy-start | bytes 393220
  14.4 8.5 %copy-start.3 = (bf16[512,128]{1,0:T(8,128)(2,1)S(1)}, bf16[512,128]{1,0:T(8,128)(2,1)}, u32[]{:S(2)}) copy-start(bf16[512,128]{1,0:T(8,128)(2,1)} %get-tuple-element.14) | copy-start | bytes 393220
  14.5 11.3 %collective-permute-start.3 = (bf16[2,2,128,512]{3,2,1,0:T(8,128)(2,1)S(1)}, bf16[2,2,128,512]{3,2,1,0:T(8,128)(2,1)S(1)}, u32[]{:S(2)}, u32[]{:S(2)}) collective-permute-start(bf16[2,2,128,512]{3,2,1,0:T(8,128)(2,1)S(1)} %get-tuple-element.19), channel_id=1, source_target_pairs={{0,1},{1,0},{2,3},{3,2},{4,5},{5,4},{6,7},{7,6},{8,9},{9,8},{10,11... | collective-permute-start | bytes 1572872 | tf_op jit(solution)/shard_map/ppermute | solution.py:62
  25.7 12.5 %collective-permute-start.11 = (bf16[2,2,128,512]{3,2,1,0:T(8,128)(2,1)S(1)}, bf16[2,2,128,512]{3,2,1,0:T(8,128)(2,1)S(1)}, u32[]{:S(2)}, u32[]{:S(2)}) collective-permute-start(bf16[2,2,128,512]{3,2,1,0:T(8,128)(2,1)S(1)} %fusion.7), channel_id=1, source_target_pairs={{0,1},{1,0},{2,3},{3,2},{4,5},{5,4},{6,7},{7,6},{8,9},{9,8},{10,11... | collective-permute-start | bytes 1572872 | tf_op jit(solution)/shard_map/ppermute | solution.py:82
  28.2 14.0 %collective-permute-start.5 = (bf16[128,512]{1,0:T(8,128)(2,1)S(1)}, bf16[128,512]{1,0:T(8,128)(2,1)S(1)}, u32[]{:S(2)}, u32[]{:S(2)}) collective-permute-start(bf16[128,512]{1,0:T(8,128)(2,1)S(1)} %get-tuple-element.15), channel_id=1, source_target_pairs={{0,24},{1,25},{2,26},{3,27},{4,28},{5,29},{6,30},{7,31}} | collective-permute-start | bytes 393224 | tf_op jit(solution)/shard_map/ppermute | solution.py:76
  34.4 9.7 %collective-permute-start.7 = (bf16[128,512]{1,0:T(8,128)(2,1)}, bf16[128,512]{1,0:T(8,128)(2,1)S(1)}, u32[]{:S(2)}, u32[]{:S(2)}) collective-permute-start(bf16[128,512]{1,0:T(8,128)(2,1)} %get-tuple-element.16), channel_id=1, source_target_pairs={{0,8},{1,9},{2,10},{3,11},{4,12},{5,13},{6,14},{7,15},{8,16},{9,17... | collective-permute-start | bytes 393224 | tf_op jit(solution)/shard_map/ppermute | solution.py:76
  35.7 8.4 %collective-permute-start.6 = (bf16[128,512]{1,0:T(8,128)(2,1)}, bf16[128,512]{1,0:T(8,128)(2,1)S(1)}, u32[]{:S(2)}, u32[]{:S(2)}) collective-permute-start(bf16[128,512]{1,0:T(8,128)(2,1)} %get-tuple-element.17), channel_id=1, source_target_pairs={{0,16},{1,17},{2,18},{3,19},{4,20},{5,21},{6,22},{7,23},{8,24},{9,... | collective-permute-start | bytes 393224 | tf_op jit(solution)/shard_map/ppermute | solution.py:76
  38.4 5.0 %copy-start.5 = (f32[2]{0:T(128)S(1)}, f32[2]{0:T(128)}, u32[]{:S(2)}) copy-start(f32[2]{0:T(128)} %param.7) | copy-start | bytes 28
  39.1 5.8 %collective-permute-start.12 = (bf16[128,512]{1,0:T(8,128)(2,1)}, bf16[128,512]{1,0:T(8,128)(2,1)S(1)}, u32[]{:S(2)}, u32[]{:S(2)}) collective-permute-start(bf16[128,512]{1,0:T(8,128)(2,1)} %fusion.18), channel_id=1, source_target_pairs={{0,2},{1,3},{2,0},{3,1},{4,6},{5,7},{6,4},{7,5},{8,10},{9,11},{10,... | collective-permute-start | bytes 393224 | tf_op jit(solution)/shard_map/ppermute | solution.py:88
  41.6 8.1 %collective-permute-start.13 = (bf16[128,512]{1,0:T(8,128)(2,1)}, bf16[128,512]{1,0:T(8,128)(2,1)S(1)}, u32[]{:S(2)}, u32[]{:S(2)}) collective-permute-start(bf16[128,512]{1,0:T(8,128)(2,1)} %get-tuple-element.20), channel_id=1, source_target_pairs={{0,4},{1,5},{2,6},{3,7},{4,0},{5,1},{6,2},{7,3},{8,12},{9,13},{10,... | collective-permute-start | bytes 393224 | tf_op jit(solution)/shard_map/ppermute | solution.py:88
  42.2 7.4 %collective-permute-start.14 = (bf16[128,512]{1,0:T(8,128)(2,1)}, bf16[128,512]{1,0:T(8,128)(2,1)}, u32[]{:S(2)}, u32[]{:S(2)}) collective-permute-start(bf16[128,512]{1,0:T(8,128)(2,1)} %get-tuple-element.21), channel_id=1, source_target_pairs={{0,6},{1,7},{2,4},{3,5},{4,2},{5,3},{6,0},{7,1},{8,14},{9,15},{10,... | collective-permute-start | bytes 393224 | tf_op jit(solution)/shard_map/ppermute | solution.py:88

commit v2 on v1

v2 whole, which is shorter than its diff:
```python
import functools

import jax
import jax.numpy as jnp
from jax import lax
from jax.experimental import pallas as pl
from jax.experimental.pallas import tpu as pltpu
from jax.sharding import PartitionSpec as P

F32, BF16, I32 = jnp.float32, jnp.bfloat16, jnp.int32
VMEM_LIMIT = 56 * 1024 * 1024


def iota(shape, dim):
    return lax.broadcasted_iota(I32, shape, dim)


def call(kernel, outs, *args, vmem=None):
    specs = [pl.BlockSpec(memory_space=pltpu.SMEM)] + [pl.BlockSpec(memory_space=pltpu.VMEM)] * (len(args) - 1)
    return pl.pallas_call(
        kernel,
        out_shape=[jax.ShapeDtypeStruct(s, d) for s, d in outs],
        in_specs=specs,
        out_specs=[pl.BlockSpec(memory_space=pltpu.VMEM)] * len(outs),
        scratch_shapes=vmem or [],
        compiler_params=pltpu.CompilerParams(vmem_limit_bytes=VMEM_LIMIT),
    )(*args)


def tdot(a, b):
    return lax.dot_general(a, b, (((0,), (0,)), ((), ())), preferred_element_type=F32)


def dot(a, b):
    return jnp.dot(a, b, preferred_element_type=F32)


def prep_kernel(at, u, signs, weights, probes, own, give, diag, *, nz, ny, fine, rows):
    z, y, c = at[0], at[1], at[2]
    ntiles = nz * ny
    take = 256 // ntiles
    eye = iota((fine, fine), 0) == iota((fine, fine), 1)
    wcol = jnp.sum(jnp.where(eye, weights[...], 0.0), axis=1, keepdims=True)
    probes[...] = ((2 * signs[...] - 1).astype(F32) * wcol).astype(BF16)
    j, m = iota((256, 256), 0), iota((256, 256), 1)
    slot, i = j // take, j % take
    d = slot % nz
    side = jnp.where(slot < nz, y, 1 - y)
    tile = ((z + d) % nz) * ny + side
    pick = jnp.where(m == i * ntiles + tile, 1.0, 0.0).astype(BF16)
    for h in range(rows // (2 * take)):
        x = jnp.concatenate([u[h * 512 : h * 512 + 256, :], u[h * 512 + 256 : h * 512 + 512, :]], axis=1)
        o = dot(pick, x).astype(BF16)
        for g in range(2):
            r0 = h * 2 * take + g * take
            og = o[:, g * fine : (g + 1) * fine]
            for s in range(nz):
                part = og[s * take : (s + 1) * take]
                mirror = og[(nz + s) * take : (nz + s + 1) * take]
                if s == 0:
                    col = c * fine + iota((take, fine), 1)
                    row = r0 + iota((take, fine), 0)
                    own[r0 : r0 + take, 0:fine] = jnp.where(col > row, part.astype(F32), 0.0).astype(BF16)
                    own[r0 : r0 + take, nz * fine : (nz + 1) * fine] = jnp.where(
                        y == 0, mirror.astype(F32), 0.0
                    ).astype(BF16)
                else:
                    own[r0 : r0 + take, s * fine : (s + 1) * fine] = part
                    give[r0 : r0 + take, (s - 1) * fine : s * fine] = mirror
    base = c * fine * ntiles
    t = z * ny + y
    blk = u[pl.ds(pl.multiple_of(base, 128), fine * ntiles), :].astype(F32)
    a, b = iota((fine * ntiles, fine), 0), iota((fine * ntiles, fine), 1)
    picked = jnp.where(a == b * ntiles + t, blk, 0.0)
    row = jnp.sum(picked, axis=0, keepdims=True)
    diag[...] = jnp.broadcast_to(jnp.sum(jnp.where(eye, row, 0.0), axis=1, keepdims=True), (fine, fine))


def mirror_kernel(at, own, oth, near, far, m0, mx, ms, q, *, nz, ny, nx, nk, fine):
    x, k = at[3], at[4]
    rows = nx * nk * fine
    for s in range(ny):
        for e in range(nx):
            xx = (x + e) % nx
            i = s * nx + e
            q[s, pl.ds(pl.multiple_of((xx * nk + k) * fine, fine), fine), :] = near[i]
            q[s, pl.ds(pl.multiple_of((xx * nk + 1 - k) * fine, fine), fine), :] = far[i]
    q0, q1 = q[0], q[1]
    m0[...] = tdot(own[:, :fine], q0)
    mx[...] = tdot(own[:, nz * fine :], q0)
    ms[...] = (tdot(own[:, fine : nz * fine], q0) + tdot(oth[...], q1)).astype(BF16).reshape(ms.shape)


def direct_kernel(at, own, oth, mx, *refs, nz, ny, nx, nk, fine):
    ps, (keep, send), (p, d) = refs[: nz + 1], refs[nz + 1 : nz + 3], refs[nz + 3 :]
    k = at[4]
    x = at[3]
    npro = p.shape[1]
    for n in range(nz + 1):
        p[n * fine : (n + 1) * fine, :] = ps[n][...]
    d[0] = dot(own[...], p[...])
    d[1] = dot(oth[...], p[fine : nz * fine, :])
    mine = pl.ds(pl.multiple_of((x * nk + k) * fine, fine), fine)
    d[1, mine, :] = d[1, mine, :] + mx[...]
    for s in range(ny):
        for e in range(nx):
            xx = (x + e) % nx
            i = s * nx + e
            keep[i] = d[s, pl.ds(pl.multiple_of((xx * nk + k) * fine, fine), fine), :]
            send[i] = d[s, pl.ds(pl.multiple_of((xx * nk + 1 - k) * fine, fine), fine), :].astype(BF16)


def fold_kernel(at, keep, got, home, *pieces, nx, ny):
    home[...] = keep[0] + got[0].astype(F32)
    for i in range(1, nx * ny):
        pieces[i - 1][...] = (keep[i] + got[i].astype(F32)).astype(BF16)


def last_kernel(comp, probes, diag, m0, home, *refs):
    out = refs[-1]
    total = m0[...] + home[...]
    for r in refs[:-1]:
        total = total + r[...].astype(F32)
    pf = probes[...].astype(F32)
    total = total + diag[:, 0:1] * pf
    out[...] = comp[0] * total + comp[1] * pf


def solution(mesh):
    nrow, ncol = mesh.shape["row"], mesh.shape["col"]
    ny, nk = 2, 2
    nz, nx = nrow // ny, ncol // nk
    both = ("row", "col")

    def place(z, y, x, k):
        return ((z * ny + y) * nx + x) * nk + k

    spots = [(z, y, x, k) for z in range(nz) for y in range(ny) for x in range(nx) for k in range(nk)]

    def down(d):
        return [(place(z, y, x, k), place(z - d, y, x, k)) for z, y, x, k in spots if z >= d]

    def up(d):
        return [(place(z, y, x, k), place(z + d, y, x, k)) for z, y, x, k in spots if z + d < nz]

    def shift(s, e):
        return [(place(z, y, x, k), place(z, y ^ s, (x + e) % nx, k)) for z, y, x, k in spots]

    other_core = [(place(z, y, x, k), place(z, y, x, 1 - k)) for z, y, x, k in spots]
    away = [(s, e) for s in range(ny) for e in range(nx) if (s, e) != (0, 0)]

    def body(upper, signs, weights, components):
        rows, ntiles, _, fine = upper.shape
        npro = signs.shape[1]
        r, c = lax.axis_index("row"), lax.axis_index("col")
        z, y, x, k = r // ny, r % ny, c // nk, c % nk
        at = jnp.stack([z, y, c, x, k]).astype(I32)
        blk = (fine, npro)
        nblk = nx * ny

        probes, own, give, diag = call(
            functools.partial(prep_kernel, nz=nz, ny=ny, fine=fine, rows=rows),
            [(blk, BF16), ((rows, (nz + 1) * fine), BF16), ((rows, (nz - 1) * fine), BF16), ((fine, fine), F32)],
            at, upper.reshape(rows * ntiles, fine), signs, weights.reshape(1, fine),
        )
        downs = {d: lax.ppermute(probes, both, down(d)) for d in range(nz - 1, 0, -1)}
        oth = lax.ppermute(give, both, shift(1, 0))
        near = [probes] + [lax.ppermute(probes, both, shift(s, (nx - e) % nx)) for s, e in away]
        near = jnp.stack(near)
        far = lax.ppermute(near, both, other_core)
        m0, mx, ms = call(
            functools.partial(mirror_kernel, nz=nz, ny=ny, nx=nx, nk=nk, fine=fine),
            [(blk, F32), (blk, F32), ((nz - 1, *blk), BF16)],
            at, own, oth, near, far,
            vmem=[pltpu.VMEM((ny, rows, npro), BF16)],
        )
        ups = [lax.ppermute(ms[d - 1], both, up(d)) for d in range(nz - 1, 0, -1)]
        keep, send = call(
            functools.partial(direct_kernel, nz=nz, ny=ny, nx=nx, nk=nk, fine=fine),
            [((nblk, *blk), F32), ((nblk, *blk), BF16)],
            at, own, oth, mx, probes, *[downs[d] for d in range(1, nz)], near[nx],
            vmem=[pltpu.VMEM(((nz + 1) * fine, npro), BF16), pltpu.VMEM((ny, rows, npro), F32)],
        )
        got = lax.ppermute(send, both, other_core)
        home, *pieces = call(
            functools.partial(fold_kernel, nx=nx, ny=ny),
            [(blk, F32)] + [(blk, BF16)] * (nblk - 1),
            at, keep, got,
        )
        cross = [lax.ppermute(p, both, shift(s, e)) for p, (s, e) in zip(pieces, away)]
        (out,) = call(last_kernel, [(blk, F32)], components, probes, diag, m0, home, *cross, *ups)
        return out

    return jax.shard_map(
        body,
        mesh=mesh,
        in_specs=(P("row", None, "col", None), P(both, None), P(both), P()),
        out_specs=P(both, None),
        check_vma=False,
    )
```

time: 53.1 us -> 60.7 us (1.14)
  Pallas kernels: 0 us -> 14.1 us
  waiting for transfers between devices: 13.8 us -> 19.3 us
  other arithmetic: 6.3 us -> 1.04 us
  matrix products: 3.61 us -> 0 us
  starting transfers between devices: 24.1 us -> 21.8 us
  local copies, waits for them, and re-layouts: 4.47 us -> 3.8 us
    pallas_call x0 -> x5, Pallas kernels: none -> 14.1 us  [call(): pl.pallas_call(kernel, out_shape=[jax.ShapeDtypeStruct(s, d) for s, d in...]
    ppermute x3, waiting for transfers between devices: 8.29 us -> 0.9 us  [body(): lax.ppermute(probes, both, down(d))]
    ppermute x11, waiting for transfers between devices: 5.53 us -> 12.3 us  [the longest x3 6.19 us: body(): lax.ppermute(probes, both, shift(s, (nx - e) % nx))]
    ppermute x1, waiting for transfers between devices: 0.01 us -> 6.1 us  [body(): oth = lax.ppermute(give, both, shift(1, 0))]
    dot_general x4 -> x0, matrix products: 3.61 us -> none  [the longest x1 1.34 us: body(): jnp.dot(own, pcat, preferred_element_type=f32).reshape(nx, nk, fine, npro)]
    add x3 -> x0, other arithmetic: 3.29 us -> none  [the longest x1 3.1 us: body(): return components[0] * total + components[1] * pf]
    ppermute x11, starting transfers between devices: 18.3 us -> 16.5 us  [the longest x3 8.43 us: body(): ups = [lax.ppermute(ms[d - 1], both, up(d)) for d in range(nz - 1, 0, -1)]]
    unnamed x13 -> x34, local copies, waits for them, and re-layouts: 1.52 us -> 3.11 us
  transfers between devices with their start and end apart: 15 -> 15, of which waited for: 3 -> 7; matrix products, arithmetic and copies ran while one was open for 19% -> 0% of each run, Pallas kernels for 0% -> 9%
where the time goes in v2:
time: 60.7 us; the launch traced here: 60.3 us
  starting transfers between devices  21.8 us (36%)
  waiting for transfers between devices  19.3 us (32%)
  Pallas kernels  14.1 us (23%)
  local copies, waits for them, and re-layouts  3.8 us (6%)
  other arithmetic  1.04 us (2%)
    pallas_call x5, Pallas kernels, call(): pl.pallas_call(kernel, out_shape=[jax.ShapeDtypeStruct(s, d) for s, d in...  14.1 us
    ppermute x3, starting transfers between devices, body(): ups = [lax.ppermute(ms[d - 1], both, up(d)) for d in range(nz - 1, 0, -1)]  8.43 us
    ppermute x3, waiting for transfers between devices, body(): lax.ppermute(probes, both, shift(s, (nx - e) % nx))  6.19 us
    ppermute x3, waiting for transfers between devices, body(): lax.ppermute(p, both, shift(s, e))  6.1 us
    ppermute x1, waiting for transfers between devices, body(): oth = lax.ppermute(give, both, shift(1, 0))  6.1 us
    ppermute x3, starting transfers between devices, body(): lax.ppermute(probes, both, shift(s, (nx - e) % nx))  4.46 us
    ppermute x3, starting transfers between devices, body(): lax.ppermute(probes, both, down(d))  3.86 us
    ppermute x3, starting transfers between devices, body(): lax.ppermute(p, both, shift(s, e))  3.49 us
  transfers between devices with their start and end apart: 15, of which 7 were waited for; matrix products, arithmetic and copies ran while one was open for 0% of the time, Pallas kernels for 9%

profile of v2, /device:TPU:0, one launch (start us, length us, event | category | flops | bytes accessed | tf_op | source)
XLA Modules:
  0.0 60.3 jit_solution(1604566007647845474)
XLA Ops:
  0.7 2.9 %shard_map.46 = (bf16[128,512]{1,0:T(8,128)(2,1)}, bf16[512,640]{1,0:T(8,128)(2,1)}, bf16[512,384]{1,0:T(8,128)(2,1)}, f32[128,128]{1,0:T(8,128)}) custom-call(s32[5]{0:T(128)} %stack.38.at, bf16[4096,128]{1,0:T(8,128)(2,1)} %bitcast.18, s32[128,512]{1,0:T(8,128)} %signs.1, f32[1,128]{1,0:T(1,128)} %bitcast.22), custom_call_target="tpu_custom_call" | custom-call | tf_op jit(solution)/shard_map/pallas_call | solution.py:20
  3.5 3.9 %collective-permute-start.3 = (bf16[128,512]{1,0:T(8,128)(2,1)}, bf16[128,512]{1,0:T(8,128)(2,1)S(1)}, u32[]{:S(2)}, u32[]{:S(2)}) collective-permute-start(bf16[128,512]{1,0:T(8,128)(2,1)} %get-tuple-element.18.refs_0_.probes), channel_id=1, source_target_pairs={{0,6},{1,7},{2,4},{3,5},{4,2},{5,3},{6,0},{7,1},{8,14},{9,15},{10,... | collective-permute-start | bytes 393224 | tf_op jit(solution)/shard_map/ppermute | solution.py:168
  8.0 3.6 %collective-permute-done.3 = bf16[128,512]{1,0:T(8,128)(2,1)S(1)} collective-permute-done((bf16[128,512]{1,0:T(8,128)(2,1)}, bf16[128,512]{1,0:T(8,128)(2,1)S(1)}, u32[]{:S(2)}, u32[]{:S(2)}) %collective-permute-start.3) | collective-permute-done | bytes 131104 | tf_op jit(solution)/shard_map/ppermute | solution.py:168
  11.7 2.3 %collective-permute-done.2.refs_4_ = bf16[128,512]{1,0:T(8,128)(2,1)S(1)} collective-permute-done((bf16[128,512]{1,0:T(8,128)(2,1)}, bf16[128,512]{1,0:T(8,128)(2,1)S(1)}, u32[]{:S(2)}, u32[]{:S(2)}) %collective-permute-start.2) | collective-permute-done | bytes 131104 | tf_op jit(solution)/shard_map/ppermute | solution.py:168
  14.2 1.0 %pad_maximum_fusion.near = bf16[4,128,512]{2,1,0:T(8,128)(2,1)S(1)} fusion(bf16[1,128,512]{2,1,0:T(8,128)(2,1)S(1)} %bitcast.20, bf16[1,128,512]{2,1,0:T(8,128)(2,1)S(1)} %bitcast.19, bf16[1,128,512]{2,1,0:T(8,128)(2,1)S(1)} %bitcast.21, bf16[1,128,512]{2,1,0:T(8,128)(2,1)} %bitcast.17), kind=kLoop, calls=%fused_computation | loop fusion | flops 786432 | bytes 1048576 | tf_op jit(solution)/shard_map/stack | solution.py:169
  15.4 1.5 %collective-permute-start = (bf16[512,384]{1,0:T(8,128)(2,1)S(1)}, bf16[512,384]{1,0:T(8,128)(2,1)S(1)}, u32[]{:S(2)}, u32[]{:S(2)}) collective-permute-start(bf16[512,384]{1,0:T(8,128)(2,1)S(1)} %copy-done.16), channel_id=1, source_target_pairs={{0,4},{1,5},{2,6},{3,7},{4,0},{5,1},{6,2},{7,3},{8,12},{9,13},{10,... | collective-permute-start | bytes 1179656 | tf_op jit(solution)/shard_map/ppermute | solution.py:167
  16.9 1.3 %collective-permute-start.7 = (bf16[128,512]{1,0:T(8,128)(2,1)S(1)}, bf16[128,512]{1,0:T(8,128)(2,1)S(1)}, u32[]{:S(2)}, u32[]{:S(2)}) collective-permute-start(bf16[128,512]{1,0:T(8,128)(2,1)S(1)} %copy-done.2), channel_id=1, source_target_pairs={{24,0},{25,1},{26,2},{27,3},{28,4},{29,5},{30,6},{31,7}} | collective-permute-start | bytes 393224 | tf_op jit(solution)/shard_map/ppermute | solution.py:166
  18.2 1.3 %collective-permute-start.6 = (bf16[128,512]{1,0:T(8,128)(2,1)S(1)}, bf16[128,512]{1,0:T(8,128)(2,1)S(1)}, u32[]{:S(2)}, u32[]{:S(2)}) collective-permute-start(bf16[128,512]{1,0:T(8,128)(2,1)S(1)} %copy-done.2), channel_id=1, source_target_pairs={{16,0},{17,1},{18,2},{19,3},{20,4},{21,5},{22,6},{23,7},{24,8},{25... | collective-permute-start | bytes 393224 | tf_op jit(solution)/shard_map/ppermute | solution.py:166
  19.5 1.3 %collective-permute-start.5 = (bf16[128,512]{1,0:T(8,128)(2,1)S(1)}, bf16[128,512]{1,0:T(8,128)(2,1)S(1)}, u32[]{:S(2)}, u32[]{:S(2)}) collective-permute-start(bf16[128,512]{1,0:T(8,128)(2,1)S(1)} %copy-done.2), channel_id=1, source_target_pairs={{8,0},{9,1},{10,2},{11,3},{12,4},{13,5},{14,6},{15,7},{16,8},{17,9... | collective-permute-start | bytes 393224 | tf_op jit(solution)/shard_map/ppermute | solution.py:166
  20.8 6.1 %collective-permute-done.oth = bf16[512,384]{1,0:T(8,128)(2,1)S(1)} collective-permute-done((bf16[512,384]{1,0:T(8,128)(2,1)S(1)}, bf16[512,384]{1,0:T(8,128)(2,1)S(1)}, u32[]{:S(2)}, u32[]{:S(2)}) %collective-permute-start) | collective-permute-done | bytes 393248 | tf_op jit(solution)/shard_map/ppermute | solution.py:167
  26.9 0.7 %copy-done.1 = bf16[512,384]{1,0:T(8,128)(2,1)} copy-done((bf16[512,384]{1,0:T(8,128)(2,1)}, bf16[512,384]{1,0:T(8,128)(2,1)S(1)}, u32[]{:S(2)}) %copy-start.1) | copy-done | bytes 393240
  27.8 3.1 %shard_map.47 = (f32[128,512]{1,0:T(8,128)}, f32[128,512]{1,0:T(8,128)}, bf16[3,128,512]{2,1,0:T(8,128)(2,1)}) custom-call(s32[5]{0:T(128)} %stack.38.at, bf16[512,640]{1,0:T(8,128)(2,1)} %get-tuple-element.20.own, bf16[512,384]{1,0:T(8,128)(2,1)} %copy-done.1, bf16[4,128,512]{2,1,0:T(8,128)(2,1)} %copy-done, bf16[4,128,512]{2,1,0:T(8,128)(2,1)} %copy-done.3), custom_call_target="tpu_custom_call" | custom-call | tf_op jit(solution)/shard_map/pallas_call | solution.py:20
  30.9 0.9 %collective-permute-done.6.refs_2_ = bf16[128,512]{1,0:T(8,128)(2,1)S(1)} collective-permute-done((bf16[128,512]{1,0:T(8,128)(2,1)S(1)}, bf16[128,512]{1,0:T(8,128)(2,1)S(1)}, u32[]{:S(2)}, u32[]{:S(2)}) %collective-permute-start.6) | collective-permute-done | bytes 131104 | tf_op jit(solution)/shard_map/ppermute | solution.py:166
  32.5 3.6 %shard_map.48 = (f32[4,128,512]{2,1,0:T(8,128)}, bf16[4,128,512]{2,1,0:T(8,128)(2,1)}) custom-call(s32[5]{0:T(128)} %stack.38.at, bf16[512,640]{1,0:T(8,128)(2,1)} %get-tuple-element.20.own, bf16[512,384]{1,0:T(8,128)(2,1)} %copy-done.1, f32[128,512]{1,0:T(8,128)} %get-tuple-element.23.mx, bf16[128,512]{1,0:T(8,128)(2,1)} %get-tuple-element.18.refs_0_.probes, ...), custom_call_target="tpu_custom_call" | custom-call | tf_op jit(solution)/shard_map/pallas_call | solution.py:20
  36.2 5.2 %collective-permute-start.14 = (bf16[128,512]{1,0:T(8,128)(2,1)S(1)}, bf16[128,512]{1,0:T(8,128)(2,1)S(1)}, u32[]{:S(2)}, u32[]{:S(2)}) collective-permute-start(bf16[128,512]{1,0:T(8,128)(2,1)S(1)} %get-tuple-element.31), channel_id=1, source_target_pairs={{0,8},{1,9},{2,10},{3,11},{4,12},{5,13},{6,14},{7,15},{8,16},{9,17... | collective-permute-start | bytes 393224 | tf_op jit(solution)/shard_map/ppermute | solution.py:177
  41.4 1.9 %collective-permute-start.13 = (bf16[128,512]{1,0:T(8,128)(2,1)S(1)}, bf16[128,512]{1,0:T(8,128)(2,1)S(1)}, u32[]{:S(2)}, u32[]{:S(2)}) collective-permute-start(bf16[128,512]{1,0:T(8,128)(2,1)S(1)} %get-tuple-element.32), channel_id=1, source_target_pairs={{0,16},{1,17},{2,18},{3,19},{4,20},{5,21},{6,22},{7,23},{8,24},{9,... | collective-permute-start | bytes 393224 | tf_op jit(solution)/shard_map/ppermute | solution.py:177
  43.3 1.3 %collective-permute-start.12 = (bf16[128,512]{1,0:T(8,128)(2,1)S(1)}, bf16[128,512]{1,0:T(8,128)(2,1)S(1)}, u32[]{:S(2)}, u32[]{:S(2)}) collective-permute-start(bf16[128,512]{1,0:T(8,128)(2,1)S(1)} %get-tuple-element.33), channel_id=1, source_target_pairs={{0,24},{1,25},{2,26},{3,27},{4,28},{5,29},{6,30},{7,31}} | collective-permute-start | bytes 393224 | tf_op jit(solution)/shard_map/ppermute | solution.py:177
  44.7 0.8 %copy-done.4 = bf16[4,128,512]{2,1,0:T(8,128)(2,1)} copy-done((bf16[4,128,512]{2,1,0:T(8,128)(2,1)}, bf16[4,128,512]{2,1,0:T(8,128)(2,1)S(1)}, u32[]{:S(2)}) %copy-start.4) | copy-done | bytes 524312
  45.4 2.2 %shard_map.49 = (f32[128,512]{1,0:T(8,128)}, bf16[128,512]{1,0:T(8,128)(2,1)}, bf16[128,512]{1,0:T(8,128)(2,1)}, bf16[128,512]{1,0:T(8,128)(2,1)}) custom-call(s32[5]{0:T(128)} %stack.38.at, f32[4,128,512]{2,1,0:T(8,128)} %get-tuple-element.24.keep, bf16[4,128,512]{2,1,0:T(8,128)(2,1)} %copy-done.4), custom_call_target="tpu_custom_call" | custom-call | tf_op jit(solution)/shard_map/pallas_call | solution.py:20
  47.7 1.5 %collective-permute-start.9 = (bf16[128,512]{1,0:T(8,128)(2,1)}, bf16[128,512]{1,0:T(8,128)(2,1)S(1)}, u32[]{:S(2)}, u32[]{:S(2)}) collective-permute-start(bf16[128,512]{1,0:T(8,128)(2,1)} %get-tuple-element.27), channel_id=1, source_target_pairs={{0,2},{1,3},{2,0},{3,1},{4,6},{5,7},{6,4},{7,5},{8,10},{9,11},{10,... | collective-permute-start | bytes 393224 | tf_op jit(solution)/shard_map/ppermute | solution.py:190
  49.9 1.2 %collective-permute-start.11 = (bf16[128,512]{1,0:T(8,128)(2,1)}, bf16[128,512]{1,0:T(8,128)(2,1)S(1)}, u32[]{:S(2)}, u32[]{:S(2)}) collective-permute-start(bf16[128,512]{1,0:T(8,128)(2,1)} %get-tuple-element.29), channel_id=1, source_target_pairs={{0,6},{1,7},{2,4},{3,5},{4,2},{5,3},{6,0},{7,1},{8,14},{9,15},{10,... | collective-permute-start | bytes 393224 | tf_op jit(solution)/shard_map/ppermute | solution.py:190
  51.2 2.3 %collective-permute-done.9.refs_0_ = bf16[128,512]{1,0:T(8,128)(2,1)S(1)} collective-permute-done((bf16[128,512]{1,0:T(8,128)(2,1)}, bf16[128,512]{1,0:T(8,128)(2,1)S(1)}, u32[]{:S(2)}, u32[]{:S(2)}) %collective-permute-start.9) | collective-permute-done | bytes 131104 | tf_op jit(solution)/shard_map/ppermute | solution.py:190
  53.5 3.8 %collective-permute-done.10.refs_1_ = bf16[128,512]{1,0:T(8,128)(2,1)S(1)} collective-permute-done((bf16[128,512]{1,0:T(8,128)(2,1)}, bf16[128,512]{1,0:T(8,128)(2,1)S(1)}, u32[]{:S(2)}, u32[]{:S(2)}) %collective-permute-start.10) | collective-permute-done | bytes 131104 | tf_op jit(solution)/shard_map/ppermute | solution.py:190
  58.0 2.3 %shard_map.50 = f32[128,512]{1,0:T(8,128)} custom-call(f32[2]{0:T(128)} %comp.1, bf16[128,512]{1,0:T(8,128)(2,1)} %get-tuple-element.18.refs_0_.probes, f32[128,128]{1,0:T(8,128)} %get-tuple-element.19.diag, f32[128,512]{1,0:T(8,128)} %get-tuple-element.22.m0, f32[128,512]{1,0:T(8,128)} %get-tuple-element.26.home, bf16[128,512]{1,0:T(8,128)(2,1)} %copy-done.13, ...), custom_call_target="tpu_custom_call" | custom-call | tf_op jit(solution)/shard_map/pallas_call | solution.py:20
  (48 shorter events, 3.9 us)
Async XLA Ops:
  3.5 8.1 %collective-permute-start.3 = (bf16[128,512]{1,0:T(8,128)(2,1)}, bf16[128,512]{1,0:T(8,128)(2,1)S(1)}, u32[]{:S(2)}, u32[]{:S(2)}) collective-permute-start(bf16[128,512]{1,0:T(8,128)(2,1)} %get-tuple-element.18.refs_0_.probes), channel_id=1, source_target_pairs={{0,6},{1,7},{2,4},{3,5},{4,2},{5,3},{6,0},{7,1},{8,14},{9,15},{10,... | collective-permute-start | bytes 393224 | tf_op jit(solution)/shard_map/ppermute | solution.py:168
  7.4 6.5 %collective-permute-start.2 = (bf16[128,512]{1,0:T(8,128)(2,1)}, bf16[128,512]{1,0:T(8,128)(2,1)S(1)}, u32[]{:S(2)}, u32[]{:S(2)}) collective-permute-start(bf16[128,512]{1,0:T(8,128)(2,1)} %get-tuple-element.18.refs_0_.probes), channel_id=1, source_target_pairs={{0,4},{1,5},{2,6},{3,7},{4,0},{5,1},{6,2},{7,3},{8,12},{9,13},{10,... | collective-permute-start | bytes 393224 | tf_op jit(solution)/shard_map/ppermute | solution.py:168
  7.9 6.3 %collective-permute-start.1 = (bf16[128,512]{1,0:T(8,128)(2,1)}, bf16[128,512]{1,0:T(8,128)(2,1)S(1)}, u32[]{:S(2)}, u32[]{:S(2)}) collective-permute-start(bf16[128,512]{1,0:T(8,128)(2,1)} %get-tuple-element.18.refs_0_.probes), channel_id=1, source_target_pairs={{0,2},{1,3},{2,0},{3,1},{4,6},{5,7},{6,4},{7,5},{8,10},{9,11},{10,... | collective-permute-start | bytes 393224 | tf_op jit(solution)/shard_map/ppermute | solution.py:168
  13.9 1.3 %copy-start.5 = (bf16[128,512]{1,0:T(8,128)(2,1)}, bf16[128,512]{1,0:T(8,128)(2,1)S(1)}, u32[]{:S(2)}) copy-start(bf16[128,512]{1,0:T(8,128)(2,1)S(1)} %collective-permute-done.2.refs_4_) | copy-start | bytes 393220
  14.2 1.2 %copy-start.16 = (bf16[512,384]{1,0:T(8,128)(2,1)S(1)}, bf16[512,384]{1,0:T(8,128)(2,1)}, u32[]{:S(2)}) copy-start(bf16[512,384]{1,0:T(8,128)(2,1)} %get-tuple-element.21) | copy-start | bytes 1179652
  14.2 2.7 %copy-start.2 = (bf16[128,512]{1,0:T(8,128)(2,1)S(1)}, bf16[128,512]{1,0:T(8,128)(2,1)}, u32[]{:S(2)}) copy-start(bf16[128,512]{1,0:T(8,128)(2,1)} %get-tuple-element.18.refs_0_.probes) | copy-start | bytes 393220
  15.3 11.6 %copy-start = (bf16[4,128,512]{2,1,0:T(8,128)(2,1)}, bf16[4,128,512]{2,1,0:T(8,128)(2,1)S(1)}, u32[]{:S(2)}) copy-start(bf16[4,128,512]{2,1,0:T(8,128)(2,1)S(1)} %pad_maximum_fusion.near) | copy-start | bytes 1572868
  15.3 11.6 %collective-permute-start.4 = (bf16[4,128,512]{2,1,0:T(8,128)(2,1)S(1)}, bf16[4,128,512]{2,1,0:T(8,128)(2,1)S(1)}, u32[]{:S(2)}, u32[]{:S(2)}) collective-permute-start(bf16[4,128,512]{2,1,0:T(8,128)(2,1)S(1)} %pad_maximum_fusion.near), channel_id=1, source_target_pairs={{0,1},{1,0},{2,3},{3,2},{4,5},{5,4},{6,7},{7,6},{8,9},{9,8},{10,11... | collective-permute-start | bytes 1572872 | tf_op jit(solution)/shard_map/ppermute | solution.py:170
  15.4 11.5 %collective-permute-start = (bf16[512,384]{1,0:T(8,128)(2,1)S(1)}, bf16[512,384]{1,0:T(8,128)(2,1)S(1)}, u32[]{:S(2)}, u32[]{:S(2)}) collective-permute-start(bf16[512,384]{1,0:T(8,128)(2,1)S(1)} %copy-done.16), channel_id=1, source_target_pairs={{0,4},{1,5},{2,6},{3,7},{4,0},{5,1},{6,2},{7,3},{8,12},{9,13},{10,... | collective-permute-start | bytes 1179656 | tf_op jit(solution)/shard_map/ppermute | solution.py:167
  16.9 14.0 %collective-permute-start.7 = (bf16[128,512]{1,0:T(8,128)(2,1)S(1)}, bf16[128,512]{1,0:T(8,128)(2,1)S(1)}, u32[]{:S(2)}, u32[]{:S(2)}) collective-permute-start(bf16[128,512]{1,0:T(8,128)(2,1)S(1)} %copy-done.2), channel_id=1, source_target_pairs={{24,0},{25,1},{26,2},{27,3},{28,4},{29,5},{30,6},{31,7}} | collective-permute-start | bytes 393224 | tf_op jit(solution)/shard_map/ppermute | solution.py:166
  18.2 13.6 %collective-permute-start.6 = (bf16[128,512]{1,0:T(8,128)(2,1)S(1)}, bf16[128,512]{1,0:T(8,128)(2,1)S(1)}, u32[]{:S(2)}, u32[]{:S(2)}) collective-permute-start(bf16[128,512]{1,0:T(8,128)(2,1)S(1)} %copy-done.2), channel_id=1, source_target_pairs={{16,0},{17,1},{18,2},{19,3},{20,4},{21,5},{22,6},{23,7},{24,8},{25... | collective-permute-start | bytes 393224 | tf_op jit(solution)/shard_map/ppermute | solution.py:166
  19.5 12.3 %collective-permute-start.5 = (bf16[128,512]{1,0:T(8,128)(2,1)S(1)}, bf16[128,512]{1,0:T(8,128)(2,1)S(1)}, u32[]{:S(2)}, u32[]{:S(2)}) collective-permute-start(bf16[128,512]{1,0:T(8,128)(2,1)S(1)} %copy-done.2), channel_id=1, source_target_pairs={{8,0},{9,1},{10,2},{11,3},{12,4},{13,5},{14,6},{15,7},{16,8},{17,9... | collective-permute-start | bytes 393224 | tf_op jit(solution)/shard_map/ppermute | solution.py:166
  32.5 3.6 %copy-start.6 = (bf16[3,128,512]{2,1,0:T(8,128)(2,1)S(1)}, bf16[3,128,512]{2,1,0:T(8,128)(2,1)}, u32[]{:S(2)}) copy-start(bf16[3,128,512]{2,1,0:T(8,128)(2,1)} %get-tuple-element.30) | copy-start | bytes 1179652
  36.2 8.5 %collective-permute-start.8 = (bf16[4,128,512]{2,1,0:T(8,128)(2,1)}, bf16[4,128,512]{2,1,0:T(8,128)(2,1)S(1)}, u32[]{:S(2)}, u32[]{:S(2)}) collective-permute-start(bf16[4,128,512]{2,1,0:T(8,128)(2,1)} %get-tuple-element.25), channel_id=1, source_target_pairs={{0,1},{1,0},{2,3},{3,2},{4,5},{5,4},{6,7},{7,6},{8,9},{9,8},{10,11... | collective-permute-start | bytes 1572872 | tf_op jit(solution)/shard_map/ppermute | solution.py:184
  36.2 13.7 %collective-permute-start.14 = (bf16[128,512]{1,0:T(8,128)(2,1)S(1)}, bf16[128,512]{1,0:T(8,128)(2,1)S(1)}, u32[]{:S(2)}, u32[]{:S(2)}) collective-permute-start(bf16[128,512]{1,0:T(8,128)(2,1)S(1)} %get-tuple-element.31), channel_id=1, source_target_pairs={{0,8},{1,9},{2,10},{3,11},{4,12},{5,13},{6,14},{7,15},{8,16},{9,17... | collective-permute-start | bytes 393224 | tf_op jit(solution)/shard_map/ppermute | solution.py:177
  41.4 9.8 %collective-permute-start.13 = (bf16[128,512]{1,0:T(8,128)(2,1)S(1)}, bf16[128,512]{1,0:T(8,128)(2,1)S(1)}, u32[]{:S(2)}, u32[]{:S(2)}) collective-permute-start(bf16[128,512]{1,0:T(8,128)(2,1)S(1)} %get-tuple-element.32), channel_id=1, source_target_pairs={{0,16},{1,17},{2,18},{3,19},{4,20},{5,21},{6,22},{7,23},{8,24},{9,... | collective-permute-start | bytes 393224 | tf_op jit(solution)/shard_map/ppermute | solution.py:177
  43.3 7.8 %collective-permute-start.12 = (bf16[128,512]{1,0:T(8,128)(2,1)S(1)}, bf16[128,512]{1,0:T(8,128)(2,1)S(1)}, u32[]{:S(2)}, u32[]{:S(2)}) collective-permute-start(bf16[128,512]{1,0:T(8,128)(2,1)S(1)} %get-tuple-element.33), channel_id=1, source_target_pairs={{0,24},{1,25},{2,26},{3,27},{4,28},{5,29},{6,30},{7,31}} | collective-permute-start | bytes 393224 | tf_op jit(solution)/shard_map/ppermute | solution.py:177
  47.7 5.9 %collective-permute-start.9 = (bf16[128,512]{1,0:T(8,128)(2,1)}, bf16[128,512]{1,0:T(8,128)(2,1)S(1)}, u32[]{:S(2)}, u32[]{:S(2)}) collective-permute-start(bf16[128,512]{1,0:T(8,128)(2,1)} %get-tuple-element.27), channel_id=1, source_target_pairs={{0,2},{1,3},{2,0},{3,1},{4,6},{5,7},{6,4},{7,5},{8,10},{9,11},{10,... | collective-permute-start | bytes 393224 | tf_op jit(solution)/shard_map/ppermute | solution.py:190
  49.2 8.1 %collective-permute-start.10 = (bf16[128,512]{1,0:T(8,128)(2,1)}, bf16[128,512]{1,0:T(8,128)(2,1)S(1)}, u32[]{:S(2)}, u32[]{:S(2)}) collective-permute-start(bf16[128,512]{1,0:T(8,128)(2,1)} %get-tuple-element.28), channel_id=1, source_target_pairs={{0,4},{1,5},{2,6},{3,7},{4,0},{5,1},{6,2},{7,3},{8,12},{9,13},{10,... | collective-permute-start | bytes 393224 | tf_op jit(solution)/shard_map/ppermute | solution.py:190
  49.9 7.4 %copy-start.10 = (bf16[128,512]{1,0:T(8,128)(2,1)}, bf16[128,512]{1,0:T(8,128)(2,1)S(1)}, u32[]{:S(2)}) copy-start(bf16[128,512]{1,0:T(8,128)(2,1)S(1)} %collective-permute-done.14.refs_5_) | copy-start | bytes 393220
  49.9 7.4 %collective-permute-start.11 = (bf16[128,512]{1,0:T(8,128)(2,1)}, bf16[128,512]{1,0:T(8,128)(2,1)S(1)}, u32[]{:S(2)}, u32[]{:S(2)}) collective-permute-start(bf16[128,512]{1,0:T(8,128)(2,1)} %get-tuple-element.29), channel_id=1, source_target_pairs={{0,6},{1,7},{2,4},{3,5},{4,2},{5,3},{6,0},{7,1},{8,14},{9,15},{10,... | collective-permute-start | bytes 393224 | tf_op jit(solution)/shard_map/ppermute | solution.py:190
  51.2 6.1 %copy-start.11 = (bf16[128,512]{1,0:T(8,128)(2,1)}, bf16[128,512]{1,0:T(8,128)(2,1)S(1)}, u32[]{:S(2)}) copy-start(bf16[128,512]{1,0:T(8,128)(2,1)S(1)} %collective-permute-done.13.refs_4_) | copy-start | bytes 393220
  51.2 6.1 %copy-start.12 = (bf16[128,512]{1,0:T(8,128)(2,1)}, bf16[128,512]{1,0:T(8,128)(2,1)S(1)}, u32[]{:S(2)}) copy-start(bf16[128,512]{1,0:T(8,128)(2,1)S(1)} %collective-permute-done.12.refs_3_) | copy-start | bytes 393220
  53.5 3.8 %copy-start.13 = (bf16[128,512]{1,0:T(8,128)(2,1)}, bf16[128,512]{1,0:T(8,128)(2,1)S(1)}, u32[]{:S(2)}) copy-start(bf16[128,512]{1,0:T(8,128)(2,1)S(1)} %collective-permute-done.9.refs_0_) | copy-start | bytes 393220
  (8 other events, 6.1 us)

commit v3 on v2

v3 whole, which is shorter than its diff:
```python
import functools
import math

import jax
import jax.numpy as jnp
from jax import lax
from jax.experimental import pallas as pl
from jax.experimental.pallas import tpu as pltpu
from jax.sharding import PartitionSpec as P

F32, BF16, I32 = jnp.float32, jnp.bfloat16, jnp.int32
ROOM = 12 * 1024 * 1024


def iota(shape, dim):
    return lax.broadcasted_iota(I32, shape, dim)


def call(kernel, outs, *args, hbm=(), scratch=()):
    spaces = [pltpu.HBM if i in hbm else pltpu.VMEM for i in range(len(args))]
    specs = [pl.BlockSpec(memory_space=m) for m in spaces]
    ops = [pltpu.with_memory_space_constraint(a, m) for a, m in zip(args, spaces)]
    held = sum(math.prod(m.shape) * jnp.dtype(m.dtype).itemsize for m in scratch if m.memory_space == pltpu.VMEM)
    return pl.pallas_call(
        kernel,
        out_shape=outs,
        in_specs=specs,
        out_specs=[pl.BlockSpec(memory_space=pltpu.VMEM)] * len(outs),
        scratch_shapes=list(scratch),
        cost_estimate=pl.CostEstimate(flops=1, bytes_accessed=1, transcendentals=0),
        compiler_params=pltpu.CompilerParams(vmem_limit_bytes=held + ROOM),
    )(*ops)


def tdot(a, b):
    return lax.dot_general(a, b, (((0,), (0,)), ((), ())), preferred_element_type=F32)


def dot(a, b):
    return jnp.dot(a, b, preferred_element_type=F32)


def where_am_i(ny, nk):
    r, c = lax.axis_index("row"), lax.axis_index("col")
    return r // ny, r % ny, c, c // nk, c % nk


def prep_kernel(u_hbm, comp_hbm, own, give, diag, scale, u, comp, raw, sems, *, nz, ny, nk, fine, rows):
    z, y, c, _, _ = where_am_i(ny, nk)
    ntiles = nz * ny
    take = 256 // ntiles
    parts = rows // (2 * take)
    get_comp = pltpu.make_async_copy(comp_hbm, comp, sems.at[0])
    get_u = pltpu.make_async_copy(u_hbm, u, sems.at[1])
    get_u.start()
    get_comp.start()
    j, m = iota((256, 256), 0), iota((256, 256), 1)
    slot, i = j // take, j % take
    d = slot % nz
    side = jnp.where(slot < nz, y, 1 - y)
    tile = ((z + d) % nz) * ny + side
    pick = jnp.where(m == i * ntiles + tile, 1.0, 0.0).astype(BF16)
    eye = iota((fine, fine), 0) == iota((fine, fine), 1)
    get_comp.wait()
    scale[0:1, :] = jnp.broadcast_to(comp[0:1, 0:1], (1, fine))
    scale[1:2, :] = jnp.broadcast_to(comp[0:1, 1:2], (1, fine))
    get_u.wait()
    for h in range(parts):
        x = jnp.concatenate([u[h * 512 : h * 512 + 256, :], u[h * 512 + 256 : h * 512 + 512, :]], axis=1)
        o = dot(pick, x)
        for g in range(2):
            r0 = h * 2 * take + g * take
            og = o[:, g * fine : (g + 1) * fine]
            for s in range(nz):
                part = og[s * take : (s + 1) * take]
                mirror = og[(nz + s) * take : (nz + s + 1) * take]
                if s == 0:
                    col = c * fine + iota((take, fine), 1)
                    row = r0 + iota((take, fine), 0)
                    raw[r0 : r0 + take, :] = part
                    own[r0 : r0 + take, 0:fine] = jnp.where(col > row, part, 0.0).astype(BF16)
                    own[r0 : r0 + take, nz * fine : (nz + 1) * fine] = jnp.where(y == 0, mirror, 0.0).astype(BF16)
                else:
                    own[r0 : r0 + take, s * fine : (s + 1) * fine] = part.astype(BF16)
                    give[r0 : r0 + take, (s - 1) * fine : s * fine] = mirror.astype(BF16)
    blk = raw[pl.ds(pl.multiple_of(c * fine, fine), fine), :]
    diag[...] = jnp.broadcast_to(jnp.sum(jnp.where(eye, blk, 0.0), axis=1, keepdims=True), (fine, fine))


def relay_kernel(probes, got, out, *, ny, nk):
    z = where_am_i(ny, nk)[0]

    @pl.when(z == 1)
    def _():
        out[...] = got[...]

    @pl.when(z != 1)
    def _():
        out[...] = probes[...]


def stack_kernel(*refs):
    for i, r in enumerate(refs[:-1]):
        refs[-1][i] = r[...]


def direct_kernel(own, oth, *refs, nz, ny, nx, nk, fine):
    ps, (keep, send, p, d) = refs[: nz + 1], refs[nz + 1 :]
    z, _, _, x, k = where_am_i(ny, nk)
    for n in range(nz + 1):
        p[n * fine : (n + 1) * fine, :] = ps[n][...]
    if nz == 4:
        @pl.when(z == 1)
        def _():
            p[fine : 2 * fine, :] = ps[3][...]
            p[3 * fine : 4 * fine, :] = jnp.zeros_like(ps[3][...])

    d[0] = dot(own[...], p[...])
    d[1] = dot(oth[...], p[fine : nz * fine, :])
    for s in range(ny):
        for e in range(nx):
            xx = (x + e) % nx
            i = s * nx + e
            keep[i] = d[s, pl.ds(pl.multiple_of((xx * nk + k) * fine, fine), fine), :]
            send[i] = d[s, pl.ds(pl.multiple_of((xx * nk + 1 - k) * fine, fine), fine), :].astype(BF16)


def mirror_kernel(own, oth, near, far, keep, m0, mx, *refs, nz, ny, nx, nk, fine):
    ms, q = refs[:-1], refs[-1]
    _, _, _, x, k = where_am_i(ny, nk)
    for s in range(ny):
        for e in range(nx):
            xx = (x + e) % nx
            i = s * nx + e
            q[s, pl.ds(pl.multiple_of((xx * nk + k) * fine, fine), fine), :] = near[i]
            q[s, pl.ds(pl.multiple_of((xx * nk + 1 - k) * fine, fine), fine), :] = far[i]
    q0, q1 = q[0], q[1]
    mo = tdot(own[...], q0)
    m0[...] = mo[:fine]
    mx[...] = mo[nz * fine :]
    md = (mo[fine : nz * fine] + tdot(oth[...], q1)).astype(BF16)
    for d in range(nz - 1):
        ms[d][...] = md[d * fine : (d + 1) * fine]


def fold_kernel(keep, got, mx, *refs, nx, ny, nz):
    near_ms, home, pieces, out_ms = refs[: nz - 2], refs[nz - 2], refs[nz - 1 : nz + nx * ny - 2], refs[nz + nx * ny - 2 :]
    home[...] = keep[0] + got[0].astype(F32)
    for i in range(1, nx * ny):
        total = keep[i] + got[i].astype(F32)
        if i == nx:
            total = total + mx[...]
        pieces[i - 1][...] = total.astype(BF16)
    for a, b in zip(near_ms, out_ms):
        b[...] = a[...]


def last_kernel(comp, probes, diag, m0, home, *refs):
    out = refs[-1]
    total = m0[...] + home[...]
    for r in refs[:-1]:
        total = total + r[...].astype(F32)
    pf = probes[...].astype(F32)
    total = total + diag[:, 0:1] * pf
    out[...] = comp[0:1, 0:1] * total + comp[1:2, 0:1] * pf


def solution(mesh):
    nrow, ncol = mesh.shape["row"], mesh.shape["col"]
    ny, nk = 2, 2
    nz, nx = nrow // ny, ncol // nk
    both = ("row", "col")

    def place(z, y, x, k):
        return ((z * ny + y) * nx + x) * nk + k

    spots = [(z, y, x, k) for z in range(nz) for y in range(ny) for x in range(nx) for k in range(nk)]

    def down(d):
        return [(place(z, y, x, k), place(z - d, y, x, k)) for z, y, x, k in spots if z >= d]

    def up(d):
        return [(place(z, y, x, k), place(z + d, y, x, k)) for z, y, x, k in spots if z + d < nz]

    def hop(*steps):
        return [(place(a, y, x, k), place(b, y, x, k)) for a, b in steps for z, y, x, k in spots if z == 0]

    def shift(s, e):
        return [(place(z, y, x, k), place(z, y ^ s, (x + e) % nx, k)) for z, y, x, k in spots]

    other_core = [(place(z, y, x, k), place(z, y, x, 1 - k)) for z, y, x, k in spots]
    away = [(s, e) for s in range(ny) for e in range(nx) if (s, e) != (0, 0)]

    def body(upper, signs, weights, components):
        rows, ntiles, _, fine = upper.shape
        npro = signs.shape[1]
        blk = (fine, npro)
        nblk = nx * ny

        probes = ((2 * signs - 1).astype(F32) * weights[:, None]).astype(BF16)
        if nz == 4:
            first = lax.ppermute(probes, both, hop((3, 0), (2, 1)))
        near = {(0, 0): probes}
        for s, e in reversed(away):
            near[s, e] = lax.ppermute(probes, both, shift(s, (nx - e) % nx))
        own, give, diag, scale = call(
            functools.partial(prep_kernel, nz=nz, ny=ny, nk=nk, fine=fine, rows=rows),
            [
                pltpu.VMEM((rows, (nz + 1) * fine), BF16),
                pltpu.VMEM((rows, (nz - 1) * fine), BF16),
                pltpu.VMEM((fine, fine), F32),
                pltpu.VMEM((2, fine), F32),
            ],
            upper.reshape(rows * ntiles, fine), components.reshape(1, 2),
            hbm=(0, 1),
            scratch=[
                pltpu.VMEM((rows * ntiles, fine), BF16),
                pltpu.VMEM((1, 2), F32),
                pltpu.VMEM((rows, fine), F32),
                pltpu.SemaphoreType.DMA((2,)),
            ],
        )
        oth = lax.ppermute(give, both, shift(1, 0))
        if nz == 4:
            downs = {1: lax.ppermute(probes, both, hop((3, 2), (1, 0))), 3: first}
            (later,) = call(functools.partial(relay_kernel, ny=ny, nk=nk), [pltpu.VMEM(blk, BF16)], probes, first)
            downs[2] = lax.ppermute(later, both, hop((3, 1), (1, 0)))
        else:
            downs = {d: lax.ppermute(probes, both, down(d)) for d in range(nz - 1, 0, -1)}
        (stack,) = call(
            stack_kernel, [pltpu.VMEM((nblk, *blk), BF16)], *[near[s, e] for s in range(ny) for e in range(nx)]
        )
        far = lax.ppermute(stack, both, other_core)
        oth, downs = lax.optimization_barrier((oth, downs))
        keep, send = call(
            functools.partial(direct_kernel, nz=nz, ny=ny, nx=nx, nk=nk, fine=fine),
            [pltpu.VMEM((nblk, *blk), F32), pltpu.VMEM((nblk, *blk), BF16)],
            own, oth, probes, *[downs[d] for d in range(1, nz)], near[1, 0],
            scratch=[pltpu.VMEM(((nz + 1) * fine, npro), BF16), pltpu.VMEM((ny, rows, npro), F32)],
        )
        got = lax.ppermute(send, both, other_core)
        m0, mx, *ms = call(
            functools.partial(mirror_kernel, nz=nz, ny=ny, nx=nx, nk=nk, fine=fine),
            [pltpu.VMEM(blk, F32), pltpu.VMEM(blk, F32)] + [pltpu.VMEM(blk, BF16)] * (nz - 1),
            own, oth, stack, far, keep,
            scratch=[pltpu.VMEM((ny, rows, npro), BF16)],
        )
        ups = [lax.ppermute(ms[nz - 2], both, up(nz - 1))]
        home, *rest = call(
            functools.partial(fold_kernel, nx=nx, ny=ny, nz=nz),
            [pltpu.VMEM(blk, F32)] + [pltpu.VMEM(blk, BF16)] * (nblk - 1 + nz - 2),
            keep, got, mx, *ms[: nz - 2],
        )
        pieces, ms = rest[: nblk - 1], rest[nblk - 1 :]
        cross = [lax.ppermute(p, both, shift(s, e)) for p, (s, e) in zip(pieces, away)]
        ups += [lax.ppermute(ms[d - 1], both, up(d)) for d in range(nz - 2, 0, -1)]
        (out,) = call(
            last_kernel, [jax.ShapeDtypeStruct(blk, F32)],
            scale, probes, diag, m0, home, *cross, *ups,
        )
        return out

    return jax.shard_map(
        body,
        mesh=mesh,
        in_specs=(P("row", None, "col", None), P(both, None), P(both), P()),
        out_specs=P(both, None),
        check_vma=False,
    )
```

time: 60.7 us -> 41 us (0.68)
  the two profiles are of different devices: /device:TPU:0 before, /device:TPU:18 now
where the time goes in v3:
time: 41 us; the launch traced here: 40.7 us
  starting transfers between devices  23.1 us (56%)
  waiting for transfers between devices  12.7 us (31%)
  Pallas kernels  4.63 us (11%)
    ppermute x2, starting transfers between devices, body(): ups += [lax.ppermute(ms[d - 1], both, up(d)) for d in range(nz - 2, 0, -1)]  8.83 us
    ppermute x2, waiting for transfers between devices, body(): ups += [lax.ppermute(ms[d - 1], both, up(d)) for d in range(nz - 2, 0, -1)]  5.45 us
    ppermute x3, waiting for transfers between devices, body(): near[s, e] = lax.ppermute(probes, both, shift(s, (nx - e) % nx))  5.24 us
    pallas_call x7, Pallas kernels, call(): pl.pallas_call(kernel, out_shape=outs, in_specs=specs, out_specs=[pl.Bloc...  4.63 us
    ppermute x3, starting transfers between devices, body(): lax.ppermute(p, both, shift(s, e))  3.55 us
    ppermute x3, starting transfers between devices, body(): near[s, e] = lax.ppermute(probes, both, shift(s, (nx - e) % nx))  3.55 us
    ppermute x1, starting transfers between devices, body(): first = lax.ppermute(probes, both, hop((3, 0), (2, 1)))  2.36 us
    ppermute x1, waiting for transfers between devices, body(): first = lax.ppermute(probes, both, hop((3, 0), (2, 1)))  1.7 us
  transfers between devices with their start and end apart: 15, of which 6 were waited for; matrix products, arithmetic and copies ran while one was open for 0% of the time, Pallas kernels for 5%

profile of v3, /device:TPU:18, one launch (start us, length us, event | category | flops | bytes accessed | tf_op | source)
XLA Modules:
  0.0 40.7 jit_solution(2072051580788967314)
XLA Ops:
  0.0 1.8 %shard_map.46 = (bf16[512,640]{1,0:T(8,128)(2,1)S(1)}, bf16[512,384]{1,0:T(8,128)(2,1)S(1)}, f32[128,128]{1,0:T(8,128)S(1)}, f32[2,128]{1,0:T(2,128)S(1)}) custom-call(bf16[4096,128]{1,0:T(8,128)(2,1)} %bitcast.2, f32[1,2]{1,0:T(1,128)} %bitcast.3), custom_call_target="tpu_custom_call" | custom-call | flops 1 | bytes 1 | tf_op jit(solution)/shard_map/pallas_call | solution.py:24
  1.8 1.6 %collective-permute-start = (bf16[512,384]{1,0:T(8,128)(2,1)S(1)}, bf16[512,384]{1,0:T(8,128)(2,1)S(1)}, u32[]{:S(2)}, u32[]{:S(2)}) collective-permute-start(bf16[512,384]{1,0:T(8,128)(2,1)S(1)} %get-tuple-element.29), channel_id=1, source_target_pairs={{0,4},{1,5},{2,6},{3,7},{4,0},{5,1},{6,2},{7,3},{8,12},{9,13},{10,... | collective-permute-start | bytes 1179656 | tf_op jit(solution)/shard_map/ppermute | solution.py:223
  3.5 2.4 %collective-permute-start.2 = (bf16[128,512]{1,0:T(8,128)(2,1)S(1)}, bf16[128,512]{1,0:T(8,128)(2,1)S(1)}, u32[]{:S(2)}, u32[]{:S(2)}) collective-permute-start(bf16[128,512]{1,0:T(8,128)(2,1)S(1)} %multiply_convert_fusion.probes.refs_0_), channel_id=1, source_target_pairs={{24,0},{25,1},{26,2},{27,3},{28,4},{29,5},{30,6},{31,7},{16,8},{17... | collective-permute-start | bytes 393224 | tf_op jit(solution)/shard_map/ppermute | solution.py:202
  5.8 0.6 %collective-permute-start.6 = (bf16[128,512]{1,0:T(8,128)(2,1)S(1)}, bf16[128,512]{1,0:T(8,128)(2,1)S(1)}, u32[]{:S(2)}, u32[]{:S(2)}) collective-permute-start(bf16[128,512]{1,0:T(8,128)(2,1)S(1)} %multiply_convert_fusion.probes.refs_0_), channel_id=1, source_target_pairs={{0,6},{1,7},{2,4},{3,5},{4,2},{5,3},{6,0},{7,1},{8,14},{9,15},{10,... | collective-permute-start | bytes 393224 | tf_op jit(solution)/shard_map/ppermute | solution.py:205
  6.5 1.5 %collective-permute-start.5 = (bf16[128,512]{1,0:T(8,128)(2,1)S(1)}, bf16[128,512]{1,0:T(8,128)(2,1)S(1)}, u32[]{:S(2)}, u32[]{:S(2)}) collective-permute-start(bf16[128,512]{1,0:T(8,128)(2,1)S(1)} %multiply_convert_fusion.probes.refs_0_), channel_id=1, source_target_pairs={{0,4},{1,5},{2,6},{3,7},{4,0},{5,1},{6,2},{7,3},{8,12},{9,13},{10,... | collective-permute-start | bytes 393224 | tf_op jit(solution)/shard_map/ppermute | solution.py:205
  7.9 1.5 %collective-permute-start.4 = (bf16[128,512]{1,0:T(8,128)(2,1)S(1)}, bf16[128,512]{1,0:T(8,128)(2,1)S(1)}, u32[]{:S(2)}, u32[]{:S(2)}) collective-permute-start(bf16[128,512]{1,0:T(8,128)(2,1)S(1)} %multiply_convert_fusion.probes.refs_0_), channel_id=1, source_target_pairs={{0,2},{1,3},{2,0},{3,1},{4,6},{5,7},{6,4},{7,5},{8,10},{9,11},{10,... | collective-permute-start | bytes 393224 | tf_op jit(solution)/shard_map/ppermute | solution.py:205
  9.4 1.7 %collective-permute-done.2.got.refs_3_ = bf16[128,512]{1,0:T(8,128)(2,1)S(1)} collective-permute-done((bf16[128,512]{1,0:T(8,128)(2,1)S(1)}, bf16[128,512]{1,0:T(8,128)(2,1)S(1)}, u32[]{:S(2)}, u32[]{:S(2)}) %collective-permute-start.2) | collective-permute-done | bytes 131104 | tf_op jit(solution)/shard_map/ppermute | solution.py:202
  11.1 1.3 %collective-permute-start.1 = (bf16[128,512]{1,0:T(8,128)(2,1)S(1)}, bf16[128,512]{1,0:T(8,128)(2,1)S(1)}, u32[]{:S(2)}, u32[]{:S(2)}) collective-permute-start(bf16[128,512]{1,0:T(8,128)(2,1)S(1)} %multiply_convert_fusion.probes.refs_0_), channel_id=1, source_target_pairs={{24,16},{25,17},{26,18},{27,19},{28,20},{29,21},{30,22},{31,23},{8... | collective-permute-start | bytes 393224 | tf_op jit(solution)/shard_map/ppermute | solution.py:225
  12.4 0.5 %collective-permute-done.6.refs_3_ = bf16[128,512]{1,0:T(8,128)(2,1)S(1)} collective-permute-done((bf16[128,512]{1,0:T(8,128)(2,1)S(1)}, bf16[128,512]{1,0:T(8,128)(2,1)S(1)}, u32[]{:S(2)}, u32[]{:S(2)}) %collective-permute-start.6) | collective-permute-done | bytes 131104 | tf_op jit(solution)/shard_map/ppermute | solution.py:205
  13.0 0.7 %collective-permute-start.3 = (bf16[128,512]{1,0:T(8,128)(2,1)S(1)}, bf16[128,512]{1,0:T(8,128)(2,1)S(1)}, u32[]{:S(2)}, u32[]{:S(2)}) collective-permute-start(bf16[128,512]{1,0:T(8,128)(2,1)S(1)} %shard_map.47), channel_id=1, source_target_pairs={{24,8},{25,9},{26,10},{27,11},{28,12},{29,13},{30,14},{31,15},{8,0... | collective-permute-start | bytes 393224 | tf_op jit(solution)/shard_map/ppermute | solution.py:227
  13.6 4.7 %collective-permute-done.5.refs_2_.refs_4_ = bf16[128,512]{1,0:T(8,128)(2,1)S(1)} collective-permute-done((bf16[128,512]{1,0:T(8,128)(2,1)S(1)}, bf16[128,512]{1,0:T(8,128)(2,1)S(1)}, u32[]{:S(2)}, u32[]{:S(2)}) %collective-permute-start.5) | collective-permute-done | bytes 131104 | tf_op jit(solution)/shard_map/ppermute | solution.py:205
  18.5 1.0 %shard_map.49 = (f32[4,128,512]{2,1,0:T(8,128)S(1)}, bf16[4,128,512]{2,1,0:T(8,128)(2,1)S(1)}) custom-call(bf16[512,640]{1,0:T(8,128)(2,1)S(1)} %get-tuple-element.28.own, bf16[512,384]{1,0:T(8,128)(2,1)S(1)} %collective-permute-done.oth, bf16[128,512]{1,0:T(8,128)(2,1)S(1)} %multiply_convert_fusion.probes.refs_0_, ...), custom_call_target="tpu_custom_call" | custom-call | flops 1 | bytes 1 | tf_op jit(solution)/shard_map/pallas_call | solution.py:24
  19.5 0.5 %collective-permute-start.8 = (bf16[4,128,512]{2,1,0:T(8,128)(2,1)S(1)}, bf16[4,128,512]{2,1,0:T(8,128)(2,1)S(1)}, u32[]{:S(2)}, u32[]{:S(2)}) collective-permute-start(bf16[4,128,512]{2,1,0:T(8,128)(2,1)S(1)} %get-tuple-element.36), channel_id=1, source_target_pairs={{0,1},{1,0},{2,3},{3,2},{4,5},{5,4},{6,7},{7,6},{8,9},{9,8},{10,11... | collective-permute-start | bytes 1572872 | tf_op jit(solution)/shard_map/ppermute | solution.py:241
  20.0 0.3 collective-permute-done.7.far
  20.4 0.8 %shard_map.50 = (f32[128,512]{1,0:T(8,128)S(1)}, f32[128,512]{1,0:T(8,128)S(1)}, bf16[128,512]{1,0:T(8,128)(2,1)S(1)}, bf16[128,512]{1,0:T(8,128)(2,1)S(1)}, bf16[128,512]{1,0:T(8,128)(2,1)S(1)}) custom-call(bf16[512,640]{1,0:T(8,128)(2,1)S(1)} %get-tuple-element.28.own, bf16[512,384]{1,0:T(8,128)(2,1)S(1)} %collective-permute-done.oth, ...), custom_call_target="tpu_custom_call" | custom-call | flops 1 | bytes 1 | tf_op jit(solution)/shard_map/pallas_call | solution.py:24
  21.2 0.7 %collective-permute-start.12 = (bf16[128,512]{1,0:T(8,128)(2,1)S(1)}, bf16[128,512]{1,0:T(8,128)(2,1)S(1)}, u32[]{:S(2)}, u32[]{:S(2)}) collective-permute-start(bf16[128,512]{1,0:T(8,128)(2,1)S(1)} %get-tuple-element.44), channel_id=1, source_target_pairs={{0,24},{1,25},{2,26},{3,27},{4,28},{5,29},{6,30},{7,31}} | collective-permute-start | bytes 393224 | tf_op jit(solution)/shard_map/ppermute | solution.py:248
  22.0 0.6 %collective-permute-start.9 = (bf16[128,512]{1,0:T(8,128)(2,1)S(1)}, bf16[128,512]{1,0:T(8,128)(2,1)S(1)}, u32[]{:S(2)}, u32[]{:S(2)}) collective-permute-start(bf16[128,512]{1,0:T(8,128)(2,1)S(1)} %get-tuple-element.41), channel_id=1, source_target_pairs={{0,2},{1,3},{2,0},{3,1},{4,6},{5,7},{6,4},{7,5},{8,10},{9,11},{10,... | collective-permute-start | bytes 393224 | tf_op jit(solution)/shard_map/ppermute | solution.py:255
  22.6 1.5 %collective-permute-start.10 = (bf16[128,512]{1,0:T(8,128)(2,1)S(1)}, bf16[128,512]{1,0:T(8,128)(2,1)S(1)}, u32[]{:S(2)}, u32[]{:S(2)}) collective-permute-start(bf16[128,512]{1,0:T(8,128)(2,1)S(1)} %get-tuple-element.42), channel_id=1, source_target_pairs={{0,4},{1,5},{2,6},{3,7},{4,0},{5,1},{6,2},{7,3},{8,12},{9,13},{10,... | collective-permute-start | bytes 393224 | tf_op jit(solution)/shard_map/ppermute | solution.py:255
  24.1 1.4 %collective-permute-start.11 = (bf16[128,512]{1,0:T(8,128)(2,1)S(1)}, bf16[128,512]{1,0:T(8,128)(2,1)S(1)}, u32[]{:S(2)}, u32[]{:S(2)}) collective-permute-start(bf16[128,512]{1,0:T(8,128)(2,1)S(1)} %get-tuple-element.43), channel_id=1, source_target_pairs={{0,6},{1,7},{2,4},{3,5},{4,2},{5,3},{6,0},{7,1},{8,14},{9,15},{10,... | collective-permute-start | bytes 393224 | tf_op jit(solution)/shard_map/ppermute | solution.py:255
  25.5 1.3 %collective-permute-start.13 = (bf16[128,512]{1,0:T(8,128)(2,1)S(1)}, bf16[128,512]{1,0:T(8,128)(2,1)S(1)}, u32[]{:S(2)}, u32[]{:S(2)}) collective-permute-start(bf16[128,512]{1,0:T(8,128)(2,1)S(1)} %get-tuple-element.45), channel_id=1, source_target_pairs={{0,16},{1,17},{2,18},{3,19},{4,20},{5,21},{6,22},{7,23},{8,24},{9,... | collective-permute-start | bytes 393224 | tf_op jit(solution)/shard_map/ppermute | solution.py:256
  26.8 7.5 %collective-permute-start.14 = (bf16[128,512]{1,0:T(8,128)(2,1)S(1)}, bf16[128,512]{1,0:T(8,128)(2,1)S(1)}, u32[]{:S(2)}, u32[]{:S(2)}) collective-permute-start(bf16[128,512]{1,0:T(8,128)(2,1)S(1)} %get-tuple-element.46), channel_id=1, source_target_pairs={{0,8},{1,9},{2,10},{3,11},{4,12},{5,13},{6,14},{7,15},{8,16},{9,17... | collective-permute-start | bytes 393224 | tf_op jit(solution)/shard_map/ppermute | solution.py:256
  34.4 1.4 %collective-permute-done.13.refs_4_ = bf16[128,512]{1,0:T(8,128)(2,1)S(1)} collective-permute-done((bf16[128,512]{1,0:T(8,128)(2,1)S(1)}, bf16[128,512]{1,0:T(8,128)(2,1)S(1)}, u32[]{:S(2)}, u32[]{:S(2)}) %collective-permute-start.13) | collective-permute-done | bytes 131104 | tf_op jit(solution)/shard_map/ppermute | solution.py:256
  35.8 4.0 %collective-permute-done.14.refs_5_ = bf16[128,512]{1,0:T(8,128)(2,1)S(1)} collective-permute-done((bf16[128,512]{1,0:T(8,128)(2,1)S(1)}, bf16[128,512]{1,0:T(8,128)(2,1)S(1)}, u32[]{:S(2)}, u32[]{:S(2)}) %collective-permute-start.14) | collective-permute-done | bytes 131104 | tf_op jit(solution)/shard_map/ppermute | solution.py:256
  39.9 0.9 %shard_map.52 = f32[128,512]{1,0:T(8,128)} custom-call(f32[2,128]{1,0:T(2,128)S(1)} %get-tuple-element.26.comp, bf16[128,512]{1,0:T(8,128)(2,1)S(1)} %multiply_convert_fusion.probes.refs_0_, f32[128,128]{1,0:T(8,128)S(1)} %get-tuple-element.27.diag, f32[128,512]{1,0:T(8,128)S(1)} %get-tuple-element.35.m0, f32[128,512]{1,0:T(8,128)S(1)} %get-tuple-element.40.home, ...), custom_call_target="tpu_custom_call" | custom-call | flops 1 | bytes 1 | tf_op jit(solution)/shard_map/pallas_call | solution.py:24
  (18 shorter events, 0.4 us)
Async XLA Ops:
  0.0 3.4 %copy-start = (s32[128,512]{1,0:T(8,128)S(1)}, s32[128,512]{1,0:T(8,128)}, u32[]{:S(2)}) copy-start(s32[128,512]{1,0:T(8,128)} %param.5) | copy-start | bytes 786436
  1.8 1.6 %copy-start.1 = (f32[128]{0:T(128)S(1)}, f32[128]{0:T(128)}, u32[]{:S(2)}) copy-start(f32[128]{0:T(128)} %param.6) | copy-start | bytes 1540
  1.8 16.7 %collective-permute-start = (bf16[512,384]{1,0:T(8,128)(2,1)S(1)}, bf16[512,384]{1,0:T(8,128)(2,1)S(1)}, u32[]{:S(2)}, u32[]{:S(2)}) collective-permute-start(bf16[512,384]{1,0:T(8,128)(2,1)S(1)} %get-tuple-element.29), channel_id=1, source_target_pairs={{0,4},{1,5},{2,6},{3,7},{4,0},{5,1},{6,2},{7,3},{8,12},{9,13},{10,... | collective-permute-start | bytes 1179656 | tf_op jit(solution)/shard_map/ppermute | solution.py:223
  3.5 7.6 %collective-permute-start.2 = (bf16[128,512]{1,0:T(8,128)(2,1)S(1)}, bf16[128,512]{1,0:T(8,128)(2,1)S(1)}, u32[]{:S(2)}, u32[]{:S(2)}) collective-permute-start(bf16[128,512]{1,0:T(8,128)(2,1)S(1)} %multiply_convert_fusion.probes.refs_0_), channel_id=1, source_target_pairs={{24,0},{25,1},{26,2},{27,3},{28,4},{29,5},{30,6},{31,7},{16,8},{17... | collective-permute-start | bytes 393224 | tf_op jit(solution)/shard_map/ppermute | solution.py:202
  5.8 7.1 %collective-permute-start.6 = (bf16[128,512]{1,0:T(8,128)(2,1)S(1)}, bf16[128,512]{1,0:T(8,128)(2,1)S(1)}, u32[]{:S(2)}, u32[]{:S(2)}) collective-permute-start(bf16[128,512]{1,0:T(8,128)(2,1)S(1)} %multiply_convert_fusion.probes.refs_0_), channel_id=1, source_target_pairs={{0,6},{1,7},{2,4},{3,5},{4,2},{5,3},{6,0},{7,1},{8,14},{9,15},{10,... | collective-permute-start | bytes 393224 | tf_op jit(solution)/shard_map/ppermute | solution.py:205
  6.5 11.9 %collective-permute-start.5 = (bf16[128,512]{1,0:T(8,128)(2,1)S(1)}, bf16[128,512]{1,0:T(8,128)(2,1)S(1)}, u32[]{:S(2)}, u32[]{:S(2)}) collective-permute-start(bf16[128,512]{1,0:T(8,128)(2,1)S(1)} %multiply_convert_fusion.probes.refs_0_), channel_id=1, source_target_pairs={{0,4},{1,5},{2,6},{3,7},{4,0},{5,1},{6,2},{7,3},{8,12},{9,13},{10,... | collective-permute-start | bytes 393224 | tf_op jit(solution)/shard_map/ppermute | solution.py:205
  7.9 10.4 %collective-permute-start.4 = (bf16[128,512]{1,0:T(8,128)(2,1)S(1)}, bf16[128,512]{1,0:T(8,128)(2,1)S(1)}, u32[]{:S(2)}, u32[]{:S(2)}) collective-permute-start(bf16[128,512]{1,0:T(8,128)(2,1)S(1)} %multiply_convert_fusion.probes.refs_0_), channel_id=1, source_target_pairs={{0,2},{1,3},{2,0},{3,1},{4,6},{5,7},{6,4},{7,5},{8,10},{9,11},{10,... | collective-permute-start | bytes 393224 | tf_op jit(solution)/shard_map/ppermute | solution.py:205
  11.1 7.4 %collective-permute-start.1 = (bf16[128,512]{1,0:T(8,128)(2,1)S(1)}, bf16[128,512]{1,0:T(8,128)(2,1)S(1)}, u32[]{:S(2)}, u32[]{:S(2)}) collective-permute-start(bf16[128,512]{1,0:T(8,128)(2,1)S(1)} %multiply_convert_fusion.probes.refs_0_), channel_id=1, source_target_pairs={{24,16},{25,17},{26,18},{27,19},{28,20},{29,21},{30,22},{31,23},{8... | collective-permute-start | bytes 393224 | tf_op jit(solution)/shard_map/ppermute | solution.py:225
  13.0 5.5 %collective-permute-start.3 = (bf16[128,512]{1,0:T(8,128)(2,1)S(1)}, bf16[128,512]{1,0:T(8,128)(2,1)S(1)}, u32[]{:S(2)}, u32[]{:S(2)}) collective-permute-start(bf16[128,512]{1,0:T(8,128)(2,1)S(1)} %shard_map.47), channel_id=1, source_target_pairs={{24,8},{25,9},{26,10},{27,11},{28,12},{29,13},{30,14},{31,15},{8,0... | collective-permute-start | bytes 393224 | tf_op jit(solution)/shard_map/ppermute | solution.py:227
  18.4 2.0 %collective-permute-start.7 = (bf16[4,128,512]{2,1,0:T(8,128)(2,1)S(1)}, bf16[4,128,512]{2,1,0:T(8,128)(2,1)S(1)}, u32[]{:S(2)}, u32[]{:S(2)}) collective-permute-start(bf16[4,128,512]{2,1,0:T(8,128)(2,1)S(1)} %shard_map.48.near), channel_id=1, source_target_pairs={{0,1},{1,0},{2,3},{3,2},{4,5},{5,4},{6,7},{7,6},{8,9},{9,8},{10,11... | collective-permute-start | bytes 1572872 | tf_op jit(solution)/shard_map/ppermute | solution.py:233
  19.5 2.3 %collective-permute-start.8 = (bf16[4,128,512]{2,1,0:T(8,128)(2,1)S(1)}, bf16[4,128,512]{2,1,0:T(8,128)(2,1)S(1)}, u32[]{:S(2)}, u32[]{:S(2)}) collective-permute-start(bf16[4,128,512]{2,1,0:T(8,128)(2,1)S(1)} %get-tuple-element.36), channel_id=1, source_target_pairs={{0,1},{1,0},{2,3},{3,2},{4,5},{5,4},{6,7},{7,6},{8,9},{9,8},{10,11... | collective-permute-start | bytes 1572872 | tf_op jit(solution)/shard_map/ppermute | solution.py:241
  21.2 5.7 %collective-permute-start.12 = (bf16[128,512]{1,0:T(8,128)(2,1)S(1)}, bf16[128,512]{1,0:T(8,128)(2,1)S(1)}, u32[]{:S(2)}, u32[]{:S(2)}) collective-permute-start(bf16[128,512]{1,0:T(8,128)(2,1)S(1)} %get-tuple-element.44), channel_id=1, source_target_pairs={{0,24},{1,25},{2,26},{3,27},{4,28},{5,29},{6,30},{7,31}} | collective-permute-start | bytes 393224 | tf_op jit(solution)/shard_map/ppermute | solution.py:248
  22.0 12.4 %collective-permute-start.9 = (bf16[128,512]{1,0:T(8,128)(2,1)S(1)}, bf16[128,512]{1,0:T(8,128)(2,1)S(1)}, u32[]{:S(2)}, u32[]{:S(2)}) collective-permute-start(bf16[128,512]{1,0:T(8,128)(2,1)S(1)} %get-tuple-element.41), channel_id=1, source_target_pairs={{0,2},{1,3},{2,0},{3,1},{4,6},{5,7},{6,4},{7,5},{8,10},{9,11},{10,... | collective-permute-start | bytes 393224 | tf_op jit(solution)/shard_map/ppermute | solution.py:255
  22.6 11.8 %collective-permute-start.10 = (bf16[128,512]{1,0:T(8,128)(2,1)S(1)}, bf16[128,512]{1,0:T(8,128)(2,1)S(1)}, u32[]{:S(2)}, u32[]{:S(2)}) collective-permute-start(bf16[128,512]{1,0:T(8,128)(2,1)S(1)} %get-tuple-element.42), channel_id=1, source_target_pairs={{0,4},{1,5},{2,6},{3,7},{4,0},{5,1},{6,2},{7,3},{8,12},{9,13},{10,... | collective-permute-start | bytes 393224 | tf_op jit(solution)/shard_map/ppermute | solution.py:255
  24.1 10.3 %collective-permute-start.11 = (bf16[128,512]{1,0:T(8,128)(2,1)S(1)}, bf16[128,512]{1,0:T(8,128)(2,1)S(1)}, u32[]{:S(2)}, u32[]{:S(2)}) collective-permute-start(bf16[128,512]{1,0:T(8,128)(2,1)S(1)} %get-tuple-element.43), channel_id=1, source_target_pairs={{0,6},{1,7},{2,4},{3,5},{4,2},{5,3},{6,0},{7,1},{8,14},{9,15},{10,... | collective-permute-start | bytes 393224 | tf_op jit(solution)/shard_map/ppermute | solution.py:255
  25.5 10.3 %collective-permute-start.13 = (bf16[128,512]{1,0:T(8,128)(2,1)S(1)}, bf16[128,512]{1,0:T(8,128)(2,1)S(1)}, u32[]{:S(2)}, u32[]{:S(2)}) collective-permute-start(bf16[128,512]{1,0:T(8,128)(2,1)S(1)} %get-tuple-element.45), channel_id=1, source_target_pairs={{0,16},{1,17},{2,18},{3,19},{4,20},{5,21},{6,22},{7,23},{8,24},{9,... | collective-permute-start | bytes 393224 | tf_op jit(solution)/shard_map/ppermute | solution.py:256
  26.8 13.0 %collective-permute-start.14 = (bf16[128,512]{1,0:T(8,128)(2,1)S(1)}, bf16[128,512]{1,0:T(8,128)(2,1)S(1)}, u32[]{:S(2)}, u32[]{:S(2)}) collective-permute-start(bf16[128,512]{1,0:T(8,128)(2,1)S(1)} %get-tuple-element.46), channel_id=1, source_target_pairs={{0,8},{1,9},{2,10},{3,11},{4,12},{5,13},{6,14},{7,15},{8,16},{9,17... | collective-permute-start | bytes 393224 | tf_op jit(solution)/shard_map/ppermute | solution.py:256

commit v4 on v3

v4 whole, which is shorter than its diff:
```python
import functools
import math

import jax
import jax.numpy as jnp
from jax import lax
from jax.experimental import pallas as pl
from jax.experimental.pallas import tpu as pltpu
from jax.sharding import PartitionSpec as P

F32, BF16, I32 = jnp.float32, jnp.bfloat16, jnp.int32
ROOM = 12 * 1024 * 1024


def iota(shape, dim):
    return lax.broadcasted_iota(I32, shape, dim)


def call(kernel, outs, *args, hbm=(), scratch=(), order=None):
    if order is not None:
        inner, place = kernel, [order.index(i) for i in range(len(args))]

        def kernel(*refs):
            inner(*[refs[i] for i in place], *refs[len(place) :])

        args = [args[i] for i in order]
    spaces = [pltpu.HBM if i in hbm else pltpu.VMEM for i in range(len(args))]
    specs = [pl.BlockSpec(memory_space=m) for m in spaces]
    ops = [pltpu.with_memory_space_constraint(a, m) for a, m in zip(args, spaces)]
    held = sum(math.prod(m.shape) * jnp.dtype(m.dtype).itemsize for m in scratch if m.memory_space == pltpu.VMEM)
    return pl.pallas_call(
        kernel,
        out_shape=outs,
        in_specs=specs,
        out_specs=[pl.BlockSpec(memory_space=pltpu.VMEM)] * len(outs),
        scratch_shapes=list(scratch),
        cost_estimate=pl.CostEstimate(flops=1, bytes_accessed=1, transcendentals=0),
        compiler_params=pltpu.CompilerParams(vmem_limit_bytes=held + ROOM),
    )(*ops)


def tdot(a, b):
    return lax.dot_general(a, b, (((0,), (0,)), ((), ())), preferred_element_type=F32)


def dot(a, b):
    return jnp.dot(a, b, preferred_element_type=F32)


def where_am_i(ny, nk):
    r, c = lax.axis_index("row"), lax.axis_index("col")
    return r // ny, r % ny, c, c // nk, c % nk


def packed(row, fine, wide):
    block = row // fine
    return (1 + block // wide) * fine + row % fine, block % wide * fine


def prep_kernel(
    u_hbm, signs_hbm, weights_hbm, comp_hbm,
    probes, own, give1, give2, diag, scale,
    u, signs, weights, comp, raw, sems,
    *, nz, ny, nk, fine, rows,
):
    z, y, c, _, _ = where_am_i(ny, nk)
    ntiles = nz * ny
    take = 256 // ntiles
    parts = rows // (2 * take)
    wide = probes.shape[1] // fine
    pairs = [(signs_hbm, signs), (weights_hbm, weights), (u_hbm, u), (comp_hbm, comp)]
    gets = [pltpu.make_async_copy(a, b, sems.at[n]) for n, (a, b) in enumerate(pairs)]
    for g in gets:
        g.start()
    j, m = iota((256, 256), 0), iota((256, 256), 1)
    slot, i = j // take, j % take
    d = slot % nz
    side = jnp.where(slot < nz, y, 1 - y)
    tile = ((z + d) % nz) * ny + side
    pick = jnp.where(m == i * ntiles + tile, 1.0, 0.0).astype(BF16)
    eye = iota((fine, fine), 0) == iota((fine, fine), 1)
    gets[0].wait()
    gets[1].wait()
    wcol = jnp.sum(jnp.where(eye, weights[...], 0.0), axis=1, keepdims=True)
    pv = ((2 * signs[...] - 1).astype(F32) * wcol).astype(BF16)
    probes[...] = pv
    give1[0:fine, :] = pv
    gets[3].wait()
    scale[0:1, :] = jnp.broadcast_to(comp[0:1, 0:1], (1, fine))
    scale[1:2, :] = jnp.broadcast_to(comp[0:1, 1:2], (1, fine))
    gets[2].wait()
    for h in range(parts):
        x = jnp.concatenate([u[h * 512 : h * 512 + 256, :], u[h * 512 + 256 : h * 512 + 512, :]], axis=1)
        o = dot(pick, x)
        for g in range(2):
            r0 = h * 2 * take + g * take
            og = o[:, g * fine : (g + 1) * fine]
            for s in range(nz):
                part = og[s * take : (s + 1) * take]
                mirror = og[(nz + s) * take : (nz + s + 1) * take]
                if s == 0:
                    col = c * fine + iota((take, fine), 1)
                    row = r0 + iota((take, fine), 0)
                    raw[r0 : r0 + take, :] = part
                    own[r0 : r0 + take, 0:fine] = jnp.where(col > row, part, 0.0).astype(BF16)
                    own[r0 : r0 + take, nz * fine : (nz + 1) * fine] = jnp.where(y == 0, mirror, 0.0).astype(BF16)
                else:
                    own[r0 : r0 + take, s * fine : (s + 1) * fine] = part.astype(BF16)
                    if s > 1:
                        give2[r0 : r0 + take, (s - 2) * fine : (s - 1) * fine] = mirror.astype(BF16)
                    else:
                        top, left = packed(r0, fine, wide)
                        give1[top : top + take, left : left + fine] = mirror.astype(BF16)
    blk = raw[pl.ds(pl.multiple_of(c * fine, fine), fine), :]
    diag[...] = jnp.broadcast_to(jnp.sum(jnp.where(eye, blk, 0.0), axis=1, keepdims=True), (fine, fine))


def relay_kernel(*refs):
    out = refs[-1]
    out[...] = refs[0][0 : out.shape[0], :]


def stack_kernel(*refs, order):
    for i, r in zip(order, refs[:-1]):
        refs[-1][i] = r[0 : refs[-1].shape[1], :]


def direct_kernel(own, oth1, oth2, *refs, nz, ny, nx, nk, fine):
    ps, (keep, send, oth, p, d) = refs[: nz + 1], refs[nz + 1 :]
    _, _, _, x, k = where_am_i(ny, nk)
    for n in range(nz + 1):
        p[n * fine : (n + 1) * fine, :] = ps[n][0:fine, :]
    d[0] = dot(own[...], p[...])
    for r0 in range(0, oth.shape[0], fine):
        top, left = packed(r0, fine, p.shape[1] // fine)
        oth[r0 : r0 + fine, 0:fine] = oth1[top : top + fine, left : left + fine]
    oth[:, fine:] = oth2[...]
    d[1] = dot(oth[...], p[fine : nz * fine, :])
    for s in range(ny):
        for e in range(nx):
            xx = (x + e) % nx
            i = s * nx + e
            keep[i] = d[s, pl.ds(pl.multiple_of((xx * nk + k) * fine, fine), fine), :]
            send[i] = d[s, pl.ds(pl.multiple_of((xx * nk + 1 - k) * fine, fine), fine), :].astype(BF16)


def mirror_kernel(near, far, keep, own, oth, m0, mx, *refs, nz, ny, nx, nk, fine):
    ms, q = refs[:-1], refs[-1]
    _, _, _, x, k = where_am_i(ny, nk)
    for s in range(ny):
        for e in range(nx):
            xx = (x + e) % nx
            i = s * nx + e
            q[s, pl.ds(pl.multiple_of((xx * nk + k) * fine, fine), fine), :] = near[i]
            q[s, pl.ds(pl.multiple_of((xx * nk + 1 - k) * fine, fine), fine), :] = far[i]
    q0, q1 = q[0], q[1]
    mo = tdot(own[...], q0)
    m0[...] = mo[:fine]
    mx[...] = mo[nz * fine :]
    md = (mo[fine : nz * fine] + tdot(oth[...], q1)).astype(BF16)
    for d in range(1, nz):
        ms[d - 1][...] = md[(d - 1) * fine : d * fine]


def fold_kernel(keep, got, mx, *refs, nx, ny):
    n = (len(refs) - nx * ny) // 2
    held, home, pieces, passed = refs[:n], refs[n], refs[n + 1 : n + nx * ny], refs[n + nx * ny :]
    home[...] = keep[0] + got[0].astype(F32)
    for i in range(1, nx * ny):
        total = keep[i] + got[i].astype(F32)
        if i == nx:
            total = total + mx[...]
        pieces[i - 1][...] = total.astype(BF16)
    for a, b in zip(held, passed):
        b[...] = a[...]


def last_kernel(scale, probes, diag, *refs):
    out = refs[-1]
    total = refs[0][...].astype(F32)
    for r in refs[1:-1]:
        total = total + r[...].astype(F32)
    pf = probes[...].astype(F32)
    total = total + diag[:, 0:1] * pf
    out[...] = scale[0:1, 0:1] * total + scale[1:2, 0:1] * pf


def solution(mesh):
    nrow, ncol = mesh.shape["row"], mesh.shape["col"]
    ny, nk = 2, 2
    nz, nx = nrow // ny, ncol // nk
    both = ("row", "col")

    def place(z, y, x, k):
        return ((z * ny + y) * nx + x) * nk + k

    spots = [(z, y, x, k) for z in range(nz) for y in range(ny) for x in range(nx) for k in range(nk)]

    def down(d):
        return [(place(z, y, x, k), place(z - d, y, x, k)) for z, y, x, k in spots if z >= d]

    def up(d):
        return [(place(z, y, x, k), place(z + d, y, x, k)) for z, y, x, k in spots if z + d < nz]

    def hop(*steps):
        return [(place(a, y, x, k), place(b, y, x, k)) for a, b in steps for z, y, x, k in spots if z == 0]

    def shift(s, e):
        return [(place(z, y, x, k), place(z, y ^ s, (x + e) % nx, k)) for z, y, x, k in spots]

    other_core = [(place(z, y, x, k), place(z, y, x, 1 - k)) for z, y, x, k in spots]
    away = [(s, e) for s in range(ny) for e in range(nx) if (s, e) != (0, 0)]

    def body(upper, signs, weights, components):
        rows, ntiles, _, fine = upper.shape
        npro = signs.shape[1]
        blk = (fine, npro)
        nblk = nx * ny

        probes, own, give1, give2, diag, scale = call(
            functools.partial(prep_kernel, nz=nz, ny=ny, nk=nk, fine=fine, rows=rows),
            [
                pltpu.VMEM(blk, BF16),
                pltpu.VMEM((rows, (nz + 1) * fine), BF16),
                pltpu.VMEM((fine + rows * fine // npro, npro), BF16),
                pltpu.VMEM((rows, (nz - 2) * fine), BF16),
                pltpu.VMEM((fine, fine), F32),
                pltpu.VMEM((2, fine), F32),
            ],
            upper.reshape(rows * ntiles, fine), signs, weights.reshape(1, fine), components.reshape(1, 2),
            hbm=(0, 1, 2, 3),
            scratch=[
                pltpu.VMEM((rows * ntiles, fine), BF16),
                pltpu.VMEM(blk, I32),
                pltpu.VMEM((1, fine), F32),
                pltpu.VMEM((1, 2), F32),
                pltpu.VMEM((rows, fine), F32),
                pltpu.SemaphoreType.DMA((4,)),
            ],
        )
        oth1 = lax.ppermute(give1, both, shift(1, 0))
        downs = {1: lax.ppermute(probes, both, down(1))}
        pairs = [(a, b) for a, b in shift(1, 0) if a // (ny * nx * nk) < nz - 2]
        oth2 = lax.ppermute(give2, both, pairs)
        if nz == 4:
            downs[3] = lax.ppermute(probes, both, down(3))
        near = {(0, 0): probes}
        for e in range(1, nx):
            near[0, e] = lax.ppermute(probes, both, shift(0, nx - e))
        have = {"a": downs[1], "x": near[0, 1], "y": oth1, "b": downs.get(3, downs[1])}
        (pad,) = call(
            relay_kernel, [pltpu.VMEM(blk, BF16)], oth1, *[have[n] for n in 'ax']
        )
        near[1, 0] = pad
        for e in range(1, nx):
            near[1, e] = lax.ppermute(pad, both, shift(0, nx - e))
        if nz == 4:
            handed = downs[1]
            if 'xyb':
                (handed,) = call(relay_kernel, [pltpu.VMEM(blk, BF16)], handed, *[have[n] for n in 'xyb'])
            downs[2] = lax.ppermute(handed, both, hop((2, 1), (1, 0)))
        else:
            downs |= {d: lax.ppermute(probes, both, down(d)) for d in range(2, nz)}
        order = [(s, e) for s in range(ny) for e in range(nx)]
        if nz == 4:
            order = [order[i] for i in [2, 0, 1, 3]]
        (stack,) = call(
            functools.partial(stack_kernel, order=[s * nx + e for s, e in order]),
            [pltpu.VMEM((nblk, *blk), BF16)],
            *[near[p] for p in order],
        )
        far = lax.ppermute(stack, both, other_core)
        oth2, downs = lax.optimization_barrier((oth2, downs))
        keep, send, oth = call(
            functools.partial(direct_kernel, nz=nz, ny=ny, nx=nx, nk=nk, fine=fine),
            [pltpu.VMEM((nblk, *blk), F32), pltpu.VMEM((nblk, *blk), BF16), pltpu.VMEM((rows, (nz - 1) * fine), BF16)],
            own, oth1, oth2, probes, *[downs[d] for d in range(1, nz)], near[1, 0],
            scratch=[pltpu.VMEM(((nz + 1) * fine, npro), BF16), pltpu.VMEM((ny, rows, npro), F32)],
            order=[0, 1, 2, 3, 4, 5, 6, 7] if nz == 4 else None,
        )
        got = lax.ppermute(send, both, other_core)
        m0, mx, *ms = call(
            functools.partial(mirror_kernel, nz=nz, ny=ny, nx=nx, nk=nk, fine=fine),
            [pltpu.VMEM(blk, F32), pltpu.VMEM(blk, F32)] + [pltpu.VMEM(blk, BF16)] * (nz - 1),
            stack, far, keep, own, oth,
            scratch=[pltpu.VMEM((ny, rows, npro), BF16)],
            order=[0, 1, 2, 3, 4] if nz == 4 else None,
        )
        steps = [1, 2, 3] if nz == 4 else list(range(1, nz))
        direct, chain = (1, 1) if nz == 4 else (1, False)
        climbs = [[(z, z + d) for z in range(nz - d)] for d in steps]
        ups = [lax.ppermute(ms[d - 1], both, hop(*climbs[i])) for i, d in enumerate(steps) if i < direct]
        home, *rest = call(
            functools.partial(fold_kernel, nx=nx, ny=ny),
            [pltpu.VMEM(blk, F32)] + [pltpu.VMEM(blk, BF16)] * (nblk - 1 + nz - 1 - direct),
            keep, got, mx, *[ms[d - 1] for d in steps[direct:]],
        )
        pieces, held = rest[: nblk - 1], rest[nblk - 1 :]
        cross = [lax.ppermute(p, both, shift(s, e)) for p, (s, e) in zip(pieces, away)]
        for n, h in enumerate(held):
            if chain and n == len(held) - 1:
                (h,) = call(relay_kernel, [pltpu.VMEM(blk, BF16)], h, ups[0])
            ups.append(lax.ppermute(h, both, hop(*climbs[direct + n])))
        tail = [scale, probes, diag, m0, home, *ups, *cross]
        (out,) = call(
            last_kernel, [jax.ShapeDtypeStruct(blk, F32)], *tail,
            order=[4, 1, 0, 5, 7, 2, 10, 6, 3, 8, 9] if nz == 4 else None,
        )
        return out

    return jax.shard_map(
        body,
        mesh=mesh,
        in_specs=(P("row", None, "col", None), P(both, None), P(both), P()),
        out_specs=P(both, None),
        check_vma=False,
    )
```

time: 41 us -> 37.9 us (0.924)
  the two profiles are of different devices: /device:TPU:18 before, /device:TPU:0 now
where the time goes in v4:
time: 37.9 us; the launch traced here: 37.3 us
  starting transfers between devices  20.2 us (53%)
  waiting for transfers between devices  12.3 us (32%)
  Pallas kernels  4.67 us (12%)
    ppermute x1, waiting for transfers between devices, body(): downs[2] = lax.ppermute(handed, both, hop((2, 1), (1, 0)))  5.09 us
    pallas_call x9, Pallas kernels, call(): pl.pallas_call(kernel, out_shape=outs, in_specs=specs, out_specs=[pl.Bloc...  4.67 us
    ppermute x3, starting transfers between devices, body(): lax.ppermute(p, both, shift(s, e))  3.45 us
    ppermute x1, waiting for transfers between devices, body(): downs[3] = lax.ppermute(probes, both, down(3))  3.3 us
    ppermute x3, waiting for transfers between devices, body(): lax.ppermute(p, both, shift(s, e))  3.22 us
    ppermute x1, starting transfers between devices, body(): oth1 = lax.ppermute(give1, both, shift(1, 0))  3.03 us
    ppermute x2, starting transfers between devices, body(): ups.append(lax.ppermute(h, both, hop(*climbs[direct + n])))  2.76 us
    ppermute x1, starting transfers between devices, body(): oth2 = lax.ppermute(give2, both, pairs)  2.41 us
  transfers between devices with their start and end apart: 15, of which 7 were waited for; matrix products, arithmetic and copies ran while one was open for 0% of the time, Pallas kernels for 5%

profile of v4, /device:TPU:0, one launch (start us, length us, event | category | flops | bytes accessed | tf_op | source)
XLA Modules:
  0.0 37.3 jit_solution(3716382712286777446)
XLA Ops:
  0.0 1.9 %shard_map.46 = (bf16[128,512]{1,0:T(8,128)(2,1)S(1)}, bf16[512,640]{1,0:T(8,128)(2,1)S(1)}, bf16[256,512]{1,0:T(8,128)(2,1)S(1)}, bf16[512,256]{1,0:T(8,128)(2,...) custom-call(bf16[4096,128]{1,0:T(8,128)(2,1)} %bitcast.3, s32[128,512]{1,0:T(8,128)} %signs_hbm.1, ...), custom_call_target="tpu_custom_call" | custom-call | flops 1 | bytes 1 | tf_op jit(solution)/shard_map/pallas_call | solution.py:31
  1.9 3.0 %collective-permute-start = (bf16[256,512]{1,0:T(8,128)(2,1)S(1)}, bf16[256,512]{1,0:T(8,128)(2,1)S(1)}, u32[]{:S(2)}, u32[]{:S(2)}) collective-permute-start(bf16[256,512]{1,0:T(8,128)(2,1)S(1)} %get-tuple-element.30), channel_id=1, source_target_pairs={{0,4},{1,5},{2,6},{3,7},{4,0},{5,1},{6,2},{7,3},{8,12},{9,13},{10,... | collective-permute-start | bytes 786440 | tf_op jit(solution)/shard_map/ppermute | solution.py:241
  4.9 1.3 %collective-permute-start.2 = (bf16[128,512]{1,0:T(8,128)(2,1)S(1)}, bf16[128,512]{1,0:T(8,128)(2,1)S(1)}, u32[]{:S(2)}, u32[]{:S(2)}) collective-permute-start(bf16[128,512]{1,0:T(8,128)(2,1)S(1)} %get-tuple-element.32.refs_3_.refs_1_), channel_id=1, source_target_pairs={{8,0},{9,1},{10,2},{11,3},{12,4},{13,5},{14,6},{15,7},{16,8},{17,9... | collective-permute-start | bytes 393224 | tf_op jit(solution)/shard_map/ppermute | solution.py:242
  6.2 1.6 %collective-permute-start.3 = (bf16[128,512]{1,0:T(8,128)(2,1)S(1)}, bf16[128,512]{1,0:T(8,128)(2,1)S(1)}, u32[]{:S(2)}, u32[]{:S(2)}) collective-permute-start(bf16[128,512]{1,0:T(8,128)(2,1)S(1)} %get-tuple-element.32.refs_3_.refs_1_), channel_id=1, source_target_pairs={{0,2},{1,3},{2,0},{3,1},{4,6},{5,7},{6,4},{7,5},{8,10},{9,11},{10,... | collective-permute-start | bytes 393224 | tf_op jit(solution)/shard_map/ppermute | solution.py:249
  7.7 1.3 %collective-permute-start.4 = (bf16[128,512]{1,0:T(8,128)(2,1)S(1)}, bf16[128,512]{1,0:T(8,128)(2,1)S(1)}, u32[]{:S(2)}, u32[]{:S(2)}) collective-permute-start(bf16[128,512]{1,0:T(8,128)(2,1)S(1)} %get-tuple-element.32.refs_3_.refs_1_), channel_id=1, source_target_pairs={{24,0},{25,1},{26,2},{27,3},{28,4},{29,5},{30,6},{31,7}} | collective-permute-start | bytes 393224 | tf_op jit(solution)/shard_map/ppermute | solution.py:246
  9.0 2.4 %collective-permute-start.1 = (bf16[512,256]{1,0:T(8,128)(2,1)S(1)}, bf16[512,256]{1,0:T(8,128)(2,1)S(1)}, u32[]{:S(2)}, u32[]{:S(2)}) collective-permute-start(bf16[512,256]{1,0:T(8,128)(2,1)S(1)} %get-tuple-element.31), channel_id=1, source_target_pairs={{0,4},{1,5},{2,6},{3,7},{4,0},{5,1},{6,2},{7,3},{8,12},{9,13},{10,... | collective-permute-start | bytes 786440 | tf_op jit(solution)/shard_map/ppermute | solution.py:244
  11.4 0.3 collective-permute-done.2.refs_0_.refs_1_.refs_4_
  11.8 1.6 %collective-permute-start.7 = (bf16[128,512]{1,0:T(8,128)(2,1)S(1)}, bf16[128,512]{1,0:T(8,128)(2,1)S(1)}, u32[]{:S(2)}, u32[]{:S(2)}) collective-permute-start(bf16[128,512]{1,0:T(8,128)(2,1)S(1)} %shard_map.48.refs_7_.refs_0_), channel_id=1, source_target_pairs={{0,2},{1,3},{2,0},{3,1},{4,6},{5,7},{6,4},{7,5},{8,10},{9,11},{10,... | collective-permute-start | bytes 393224 | tf_op jit(solution)/shard_map/ppermute | solution.py:256
  13.3 3.3 %collective-permute-done.4.refs_3_.refs_6_ = bf16[128,512]{1,0:T(8,128)(2,1)S(1)} collective-permute-done((bf16[128,512]{1,0:T(8,128)(2,1)S(1)}, bf16[128,512]{1,0:T(8,128)(2,1)S(1)}, u32[]{:S(2)}, u32[]{:S(2)}) %collective-permute-start.4) | collective-permute-done | bytes 131104 | tf_op jit(solution)/shard_map/ppermute | solution.py:246
  16.6 1.3 %collective-permute-start.5 = (bf16[128,512]{1,0:T(8,128)(2,1)S(1)}, bf16[128,512]{1,0:T(8,128)(2,1)S(1)}, u32[]{:S(2)}, u32[]{:S(2)}) collective-permute-start(bf16[128,512]{1,0:T(8,128)(2,1)S(1)} %shard_map.47), channel_id=1, source_target_pairs={{16,8},{17,9},{18,10},{19,11},{20,12},{21,13},{22,14},{23,15},{8,0... | collective-permute-start | bytes 393224 | tf_op jit(solution)/shard_map/ppermute | solution.py:261
  18.1 0.3 collective-permute-done.1.refs_2_
  18.4 5.1 %collective-permute-done.5.refs_5_ = bf16[128,512]{1,0:T(8,128)(2,1)S(1)} collective-permute-done((bf16[128,512]{1,0:T(8,128)(2,1)S(1)}, bf16[128,512]{1,0:T(8,128)(2,1)S(1)}, u32[]{:S(2)}, u32[]{:S(2)}) %collective-permute-start.5) | collective-permute-done | bytes 131104 | tf_op jit(solution)/shard_map/ppermute | solution.py:261
  23.5 1.0 %shard_map.49 = (f32[4,128,512]{2,1,0:T(8,128)S(1)}, bf16[4,128,512]{2,1,0:T(8,128)(2,1)S(1)}, bf16[512,384]{1,0:T(8,128)(2,1)S(1)}) custom-call(bf16[512,640]{1,0:T(8,128)(2,1)S(1)} %get-tuple-element.29.refs_0_.refs_3_, bf16[256,512]{1,0:T(8,128)(2,1)S(1)} %collective-permute-done.refs_2_.refs_0_.refs_1_, ...), custom_call_target="tpu_custom_call" | custom-call | flops 1 | bytes 1 | tf_op jit(solution)/shard_map/pallas_call | solution.py:31
  24.5 0.8 %shard_map.51 = (f32[128,512]{1,0:T(8,128)S(1)}, f32[128,512]{1,0:T(8,128)S(1)}, bf16[128,512]{1,0:T(8,128)(2,1)S(1)}, bf16[128,512]{1,0:T(8,128)(2,1)S(1)}, bf16[128,512]{1,0:T(8,128)(2,1)S(1)}) custom-call(bf16[4,128,512]{2,1,0:T(8,128)(2,1)S(1)} %shard_map.50.refs_0_, bf16[4,128,512]{2,1,0:T(8,128)(2,1)S(1)} %collective-permute-done.8.refs_1_, ...), custom_call_target="tpu_custom_call" | custom-call | flops 1 | bytes 1 | tf_op jit(solution)/shard_map/pallas_call | solution.py:31
  25.4 1.5 %collective-permute-start.9 = (bf16[128,512]{1,0:T(8,128)(2,1)S(1)}, bf16[128,512]{1,0:T(8,128)(2,1)S(1)}, u32[]{:S(2)}, u32[]{:S(2)}) collective-permute-start(bf16[128,512]{1,0:T(8,128)(2,1)S(1)} %get-tuple-element.45), channel_id=1, source_target_pairs={{0,8},{1,9},{2,10},{3,11},{4,12},{5,13},{6,14},{7,15},{8,16},{9,17... | collective-permute-start | bytes 393224 | tf_op jit(solution)/shard_map/ppermute | solution.py:292
  27.0 1.5 %collective-permute-start.11 = (bf16[128,512]{1,0:T(8,128)(2,1)S(1)}, bf16[128,512]{1,0:T(8,128)(2,1)S(1)}, u32[]{:S(2)}, u32[]{:S(2)}) collective-permute-start(bf16[128,512]{1,0:T(8,128)(2,1)S(1)} %get-tuple-element.48), channel_id=1, source_target_pairs={{0,6},{1,7},{2,4},{3,5},{4,2},{5,3},{6,0},{7,1},{8,14},{9,15},{10,... | collective-permute-start | bytes 393224 | tf_op jit(solution)/shard_map/ppermute | solution.py:299
  28.4 1.5 %collective-permute-start.12 = (bf16[128,512]{1,0:T(8,128)(2,1)S(1)}, bf16[128,512]{1,0:T(8,128)(2,1)S(1)}, u32[]{:S(2)}, u32[]{:S(2)}) collective-permute-start(bf16[128,512]{1,0:T(8,128)(2,1)S(1)} %get-tuple-element.49), channel_id=1, source_target_pairs={{0,16},{1,17},{2,18},{3,19},{4,20},{5,21},{6,22},{7,23},{8,24},{9,... | collective-permute-start | bytes 393224 | tf_op jit(solution)/shard_map/ppermute | solution.py:303
  29.9 0.6 %collective-permute-start.13 = (bf16[128,512]{1,0:T(8,128)(2,1)S(1)}, bf16[128,512]{1,0:T(8,128)(2,1)S(1)}, u32[]{:S(2)}, u32[]{:S(2)}) collective-permute-start(bf16[128,512]{1,0:T(8,128)(2,1)S(1)} %get-tuple-element.51), channel_id=1, source_target_pairs={{0,2},{1,3},{2,0},{3,1},{4,6},{5,7},{6,4},{7,5},{8,10},{9,11},{10,... | collective-permute-start | bytes 393224 | tf_op jit(solution)/shard_map/ppermute | solution.py:299
  30.5 1.4 %collective-permute-start.14 = (bf16[128,512]{1,0:T(8,128)(2,1)S(1)}, bf16[128,512]{1,0:T(8,128)(2,1)S(1)}, u32[]{:S(2)}, u32[]{:S(2)}) collective-permute-start(bf16[128,512]{1,0:T(8,128)(2,1)S(1)} %get-tuple-element.52), channel_id=1, source_target_pairs={{0,4},{1,5},{2,6},{3,7},{4,0},{5,1},{6,2},{7,3},{8,12},{9,13},{10,... | collective-permute-start | bytes 393224 | tf_op jit(solution)/shard_map/ppermute | solution.py:299
  31.9 1.3 %collective-permute-start.10 = (bf16[128,512]{1,0:T(8,128)(2,1)S(1)}, bf16[128,512]{1,0:T(8,128)(2,1)S(1)}, u32[]{:S(2)}, u32[]{:S(2)}) collective-permute-start(bf16[128,512]{1,0:T(8,128)(2,1)S(1)} %shard_map.53), channel_id=1, source_target_pairs={{0,24},{1,25},{2,26},{3,27},{4,28},{5,29},{6,30},{7,31}} | collective-permute-start | bytes 393224 | tf_op jit(solution)/shard_map/ppermute | solution.py:303
  33.2 0.6 %collective-permute-done.11.refs_6_ = bf16[128,512]{1,0:T(8,128)(2,1)S(1)} collective-permute-done((bf16[128,512]{1,0:T(8,128)(2,1)S(1)}, bf16[128,512]{1,0:T(8,128)(2,1)S(1)}, u32[]{:S(2)}, u32[]{:S(2)}) %collective-permute-start.11) | collective-permute-done | bytes 131104 | tf_op jit(solution)/shard_map/ppermute | solution.py:299
  33.9 1.6 %collective-permute-done.13.refs_9_ = bf16[128,512]{1,0:T(8,128)(2,1)S(1)} collective-permute-done((bf16[128,512]{1,0:T(8,128)(2,1)S(1)}, bf16[128,512]{1,0:T(8,128)(2,1)S(1)}, u32[]{:S(2)}, u32[]{:S(2)}) %collective-permute-start.13) | collective-permute-done | bytes 131104 | tf_op jit(solution)/shard_map/ppermute | solution.py:299
  35.5 1.0 %collective-permute-done.14.refs_10_ = bf16[128,512]{1,0:T(8,128)(2,1)S(1)} collective-permute-done((bf16[128,512]{1,0:T(8,128)(2,1)S(1)}, bf16[128,512]{1,0:T(8,128)(2,1)S(1)}, u32[]{:S(2)}, u32[]{:S(2)}) %collective-permute-start.14) | collective-permute-done | bytes 131104 | tf_op jit(solution)/shard_map/ppermute | solution.py:299
  36.5 0.9 %shard_map.54 = f32[128,512]{1,0:T(8,128)} custom-call(f32[128,512]{1,0:T(8,128)S(1)} %get-tuple-element.43.refs_0_, bf16[128,512]{1,0:T(8,128)(2,1)S(1)} %get-tuple-element.32.refs_3_.refs_1_, f32[2,128]{1,0:T(2,128)S(1)} %get-tuple-element.44.refs_2_, bf16[128,512]{1,0:T(8,128)(2,1)S(1)} %collective-permute-done.9.refs_1_.refs_3_, ...), custom_call_target="tpu_custom_call" | custom-call | flops 1 | bytes 1 | tf_op jit(solution)/shard_map/pallas_call | solution.py:31
  (15 shorter events, 0.3 us)
Async XLA Ops:
  1.9 9.9 %collective-permute-start = (bf16[256,512]{1,0:T(8,128)(2,1)S(1)}, bf16[256,512]{1,0:T(8,128)(2,1)S(1)}, u32[]{:S(2)}, u32[]{:S(2)}) collective-permute-start(bf16[256,512]{1,0:T(8,128)(2,1)S(1)} %get-tuple-element.30), channel_id=1, source_target_pairs={{0,4},{1,5},{2,6},{3,7},{4,0},{5,1},{6,2},{7,3},{8,12},{9,13},{10,... | collective-permute-start | bytes 786440 | tf_op jit(solution)/shard_map/ppermute | solution.py:241
  4.9 6.8 %collective-permute-start.2 = (bf16[128,512]{1,0:T(8,128)(2,1)S(1)}, bf16[128,512]{1,0:T(8,128)(2,1)S(1)}, u32[]{:S(2)}, u32[]{:S(2)}) collective-permute-start(bf16[128,512]{1,0:T(8,128)(2,1)S(1)} %get-tuple-element.32.refs_3_.refs_1_), channel_id=1, source_target_pairs={{8,0},{9,1},{10,2},{11,3},{12,4},{13,5},{14,6},{15,7},{16,8},{17,9... | collective-permute-start | bytes 393224 | tf_op jit(solution)/shard_map/ppermute | solution.py:242
  6.2 5.6 %collective-permute-start.3 = (bf16[128,512]{1,0:T(8,128)(2,1)S(1)}, bf16[128,512]{1,0:T(8,128)(2,1)S(1)}, u32[]{:S(2)}, u32[]{:S(2)}) collective-permute-start(bf16[128,512]{1,0:T(8,128)(2,1)S(1)} %get-tuple-element.32.refs_3_.refs_1_), channel_id=1, source_target_pairs={{0,2},{1,3},{2,0},{3,1},{4,6},{5,7},{6,4},{7,5},{8,10},{9,11},{10,... | collective-permute-start | bytes 393224 | tf_op jit(solution)/shard_map/ppermute | solution.py:249
  7.7 8.9 %collective-permute-start.4 = (bf16[128,512]{1,0:T(8,128)(2,1)S(1)}, bf16[128,512]{1,0:T(8,128)(2,1)S(1)}, u32[]{:S(2)}, u32[]{:S(2)}) collective-permute-start(bf16[128,512]{1,0:T(8,128)(2,1)S(1)} %get-tuple-element.32.refs_3_.refs_1_), channel_id=1, source_target_pairs={{24,0},{25,1},{26,2},{27,3},{28,4},{29,5},{30,6},{31,7}} | collective-permute-start | bytes 393224 | tf_op jit(solution)/shard_map/ppermute | solution.py:246
  9.0 9.4 %collective-permute-start.1 = (bf16[512,256]{1,0:T(8,128)(2,1)S(1)}, bf16[512,256]{1,0:T(8,128)(2,1)S(1)}, u32[]{:S(2)}, u32[]{:S(2)}) collective-permute-start(bf16[512,256]{1,0:T(8,128)(2,1)S(1)} %get-tuple-element.31), channel_id=1, source_target_pairs={{0,4},{1,5},{2,6},{3,7},{4,0},{5,1},{6,2},{7,3},{8,12},{9,13},{10,... | collective-permute-start | bytes 786440 | tf_op jit(solution)/shard_map/ppermute | solution.py:244
  11.8 6.2 %collective-permute-start.7 = (bf16[128,512]{1,0:T(8,128)(2,1)S(1)}, bf16[128,512]{1,0:T(8,128)(2,1)S(1)}, u32[]{:S(2)}, u32[]{:S(2)}) collective-permute-start(bf16[128,512]{1,0:T(8,128)(2,1)S(1)} %shard_map.48.refs_7_.refs_0_), channel_id=1, source_target_pairs={{0,2},{1,3},{2,0},{3,1},{4,6},{5,7},{6,4},{7,5},{8,10},{9,11},{10,... | collective-permute-start | bytes 393224 | tf_op jit(solution)/shard_map/ppermute | solution.py:256
  16.6 6.9 %collective-permute-start.5 = (bf16[128,512]{1,0:T(8,128)(2,1)S(1)}, bf16[128,512]{1,0:T(8,128)(2,1)S(1)}, u32[]{:S(2)}, u32[]{:S(2)}) collective-permute-start(bf16[128,512]{1,0:T(8,128)(2,1)S(1)} %shard_map.47), channel_id=1, source_target_pairs={{16,8},{17,9},{18,10},{19,11},{20,12},{21,13},{22,14},{23,15},{8,0... | collective-permute-start | bytes 393224 | tf_op jit(solution)/shard_map/ppermute | solution.py:261
  18.0 6.6 %collective-permute-start.8 = (bf16[4,128,512]{2,1,0:T(8,128)(2,1)S(1)}, bf16[4,128,512]{2,1,0:T(8,128)(2,1)S(1)}, u32[]{:S(2)}, u32[]{:S(2)}) collective-permute-start(bf16[4,128,512]{2,1,0:T(8,128)(2,1)S(1)} %shard_map.50.refs_0_), channel_id=1, source_target_pairs={{0,1},{1,0},{2,3},{3,2},{4,5},{5,4},{6,7},{7,6},{8,9},{9,8},{10,11... | collective-permute-start | bytes 1572872 | tf_op jit(solution)/shard_map/ppermute | solution.py:272
  24.5 2.4 %collective-permute-start.6 = (bf16[4,128,512]{2,1,0:T(8,128)(2,1)S(1)}, bf16[4,128,512]{2,1,0:T(8,128)(2,1)S(1)}, u32[]{:S(2)}, u32[]{:S(2)}) collective-permute-start(bf16[4,128,512]{2,1,0:T(8,128)(2,1)S(1)} %get-tuple-element.38), channel_id=1, source_target_pairs={{0,1},{1,0},{2,3},{3,2},{4,5},{5,4},{6,7},{7,6},{8,9},{9,8},{10,11... | collective-permute-start | bytes 1572872 | tf_op jit(solution)/shard_map/ppermute | solution.py:281
  25.4 6.5 %collective-permute-start.9 = (bf16[128,512]{1,0:T(8,128)(2,1)S(1)}, bf16[128,512]{1,0:T(8,128)(2,1)S(1)}, u32[]{:S(2)}, u32[]{:S(2)}) collective-permute-start(bf16[128,512]{1,0:T(8,128)(2,1)S(1)} %get-tuple-element.45), channel_id=1, source_target_pairs={{0,8},{1,9},{2,10},{3,11},{4,12},{5,13},{6,14},{7,15},{8,16},{9,17... | collective-permute-start | bytes 393224 | tf_op jit(solution)/shard_map/ppermute | solution.py:292
  27.0 6.9 %collective-permute-start.11 = (bf16[128,512]{1,0:T(8,128)(2,1)S(1)}, bf16[128,512]{1,0:T(8,128)(2,1)S(1)}, u32[]{:S(2)}, u32[]{:S(2)}) collective-permute-start(bf16[128,512]{1,0:T(8,128)(2,1)S(1)} %get-tuple-element.48), channel_id=1, source_target_pairs={{0,6},{1,7},{2,4},{3,5},{4,2},{5,3},{6,0},{7,1},{8,14},{9,15},{10,... | collective-permute-start | bytes 393224 | tf_op jit(solution)/shard_map/ppermute | solution.py:299
  28.4 5.4 %collective-permute-start.12 = (bf16[128,512]{1,0:T(8,128)(2,1)S(1)}, bf16[128,512]{1,0:T(8,128)(2,1)S(1)}, u32[]{:S(2)}, u32[]{:S(2)}) collective-permute-start(bf16[128,512]{1,0:T(8,128)(2,1)S(1)} %get-tuple-element.49), channel_id=1, source_target_pairs={{0,16},{1,17},{2,18},{3,19},{4,20},{5,21},{6,22},{7,23},{8,24},{9,... | collective-permute-start | bytes 393224 | tf_op jit(solution)/shard_map/ppermute | solution.py:303
  29.9 5.6 %collective-permute-start.13 = (bf16[128,512]{1,0:T(8,128)(2,1)S(1)}, bf16[128,512]{1,0:T(8,128)(2,1)S(1)}, u32[]{:S(2)}, u32[]{:S(2)}) collective-permute-start(bf16[128,512]{1,0:T(8,128)(2,1)S(1)} %get-tuple-element.51), channel_id=1, source_target_pairs={{0,2},{1,3},{2,0},{3,1},{4,6},{5,7},{6,4},{7,5},{8,10},{9,11},{10,... | collective-permute-start | bytes 393224 | tf_op jit(solution)/shard_map/ppermute | solution.py:299
  30.5 5.9 %collective-permute-start.14 = (bf16[128,512]{1,0:T(8,128)(2,1)S(1)}, bf16[128,512]{1,0:T(8,128)(2,1)S(1)}, u32[]{:S(2)}, u32[]{:S(2)}) collective-permute-start(bf16[128,512]{1,0:T(8,128)(2,1)S(1)} %get-tuple-element.52), channel_id=1, source_target_pairs={{0,4},{1,5},{2,6},{3,7},{4,0},{5,1},{6,2},{7,3},{8,12},{9,13},{10,... | collective-permute-start | bytes 393224 | tf_op jit(solution)/shard_map/ppermute | solution.py:299
  31.9 4.5 %collective-permute-start.10 = (bf16[128,512]{1,0:T(8,128)(2,1)S(1)}, bf16[128,512]{1,0:T(8,128)(2,1)S(1)}, u32[]{:S(2)}, u32[]{:S(2)}) collective-permute-start(bf16[128,512]{1,0:T(8,128)(2,1)S(1)} %shard_map.53), channel_id=1, source_target_pairs={{0,24},{1,25},{2,26},{3,27},{4,28},{5,29},{6,30},{7,31}} | collective-permute-start | bytes 393224 | tf_op jit(solution)/shard_map/ppermute | solution.py:303

commit v5 on v4

--- a/solution.py
+++ b/solution.py
@@ -249,7 +249,7 @@
             near[0, e] = lax.ppermute(probes, both, shift(0, nx - e))
         have = {"a": downs[1], "x": near[0, 1], "y": oth1, "b": downs.get(3, downs[1])}
         (pad,) = call(
-            relay_kernel, [pltpu.VMEM(blk, BF16)], oth1, *[have[n] for n in 'ax']
+            relay_kernel, [pltpu.VMEM(blk, BF16)], oth1
         )
         near[1, 0] = pad
         for e in range(1, nx):
@@ -257,7 +257,7 @@
         if nz == 4:
             handed = downs[1]
             if 'xyb':
-                (handed,) = call(relay_kernel, [pltpu.VMEM(blk, BF16)], handed, *[have[n] for n in 'xyb'])
+                (handed,) = call(relay_kernel, [pltpu.VMEM(blk, BF16)], handed, *[have[n] for n in 'yb'])
             downs[2] = lax.ppermute(handed, both, hop((2, 1), (1, 0)))
         else:
             downs |= {d: lax.ppermute(probes, both, down(d)) for d in range(2, nz)}

time: 37.9 us -> 37.9 us (level)
    ppermute x1, starting transfers between devices: 2.41 us -> 1.93 us  [body(): oth2 = lax.ppermute(give2, both, pairs)]
    ppermute x1, starting transfers between devices: 1.56 us -> 2.04 us  [body(): near[0, e] = lax.ppermute(probes, both, shift(0, nx - e))]
  transfers between devices with their start and end apart: 15 -> 15, of which waited for: 7 -> 5; matrix products, arithmetic and copies ran while one was open for 0% -> 0% of each run, Pallas kernels for 5% -> 5%
where the time goes in v5:
time: 37.9 us; the launch traced here: 37.3 us
  starting transfers between devices  20.2 us (53%)
  waiting for transfers between devices  12.3 us (32%)
  Pallas kernels  4.67 us (12%)
    ppermute x1, waiting for transfers between devices, body(): downs[2] = lax.ppermute(handed, both, hop((2, 1), (1, 0)))  5.41 us
    pallas_call x9, Pallas kernels, call(): pl.pallas_call(kernel, out_shape=outs, in_specs=specs, out_specs=[pl.Bloc...  4.67 us
    ppermute x1, waiting for transfers between devices, body(): downs[3] = lax.ppermute(probes, both, down(3))  3.57 us
    ppermute x3, starting transfers between devices, body(): lax.ppermute(p, both, shift(s, e))  3.43 us
    ppermute x3, waiting for transfers between devices, body(): lax.ppermute(p, both, shift(s, e))  3.22 us
    ppermute x1, starting transfers between devices, body(): oth1 = lax.ppermute(give1, both, shift(1, 0))  3.03 us
    ppermute x2, starting transfers between devices, body(): ups.append(lax.ppermute(h, both, hop(*climbs[direct + n])))  2.77 us
    ppermute x1, starting transfers between devices, body(): near[0, e] = lax.ppermute(probes, both, shift(0, nx - e))  2.04 us
  transfers between devices with their start and end apart: 15, of which 5 were waited for; matrix products, arithmetic and copies ran while one was open for 0% of the time, Pallas kernels for 5%

profile of v5, /device:TPU:0, one launch (start us, length us, event | category | flops | bytes accessed | tf_op | source)
XLA Modules:
  0.0 37.3 jit_solution(2198032605453819858)
XLA Ops:
  0.0 1.9 %shard_map.46 = (bf16[128,512]{1,0:T(8,128)(2,1)S(1)}, bf16[512,640]{1,0:T(8,128)(2,1)S(1)}, bf16[256,512]{1,0:T(8,128)(2,1)S(1)}, bf16[512,256]{1,0:T(8,128)(2,...) custom-call(bf16[4096,128]{1,0:T(8,128)(2,1)} %bitcast.3, s32[128,512]{1,0:T(8,128)} %signs_hbm.1, ...), custom_call_target="tpu_custom_call" | custom-call | flops 1 | bytes 1 | tf_op jit(solution)/shard_map/pallas_call | solution.py:31
  1.9 3.0 %collective-permute-start = (bf16[256,512]{1,0:T(8,128)(2,1)S(1)}, bf16[256,512]{1,0:T(8,128)(2,1)S(1)}, u32[]{:S(2)}, u32[]{:S(2)}) collective-permute-start(bf16[256,512]{1,0:T(8,128)(2,1)S(1)} %get-tuple-element.30), channel_id=1, source_target_pairs={{0,4},{1,5},{2,6},{3,7},{4,0},{5,1},{6,2},{7,3},{8,12},{9,13},{10,... | collective-permute-start | bytes 786440 | tf_op jit(solution)/shard_map/ppermute | solution.py:241
  4.9 1.3 %collective-permute-start.2 = (bf16[128,512]{1,0:T(8,128)(2,1)S(1)}, bf16[128,512]{1,0:T(8,128)(2,1)S(1)}, u32[]{:S(2)}, u32[]{:S(2)}) collective-permute-start(bf16[128,512]{1,0:T(8,128)(2,1)S(1)} %get-tuple-element.32.refs_3_.refs_1_), channel_id=1, source_target_pairs={{8,0},{9,1},{10,2},{11,3},{12,4},{13,5},{14,6},{15,7},{16,8},{17,9... | collective-permute-start | bytes 393224 | tf_op jit(solution)/shard_map/ppermute | solution.py:242
  6.2 1.3 %collective-permute-start.3 = (bf16[128,512]{1,0:T(8,128)(2,1)S(1)}, bf16[128,512]{1,0:T(8,128)(2,1)S(1)}, u32[]{:S(2)}, u32[]{:S(2)}) collective-permute-start(bf16[128,512]{1,0:T(8,128)(2,1)S(1)} %get-tuple-element.32.refs_3_.refs_1_), channel_id=1, source_target_pairs={{24,0},{25,1},{26,2},{27,3},{28,4},{29,5},{30,6},{31,7}} | collective-permute-start | bytes 393224 | tf_op jit(solution)/shard_map/ppermute | solution.py:246
  7.5 1.9 %collective-permute-start.1 = (bf16[512,256]{1,0:T(8,128)(2,1)S(1)}, bf16[512,256]{1,0:T(8,128)(2,1)S(1)}, u32[]{:S(2)}, u32[]{:S(2)}) collective-permute-start(bf16[512,256]{1,0:T(8,128)(2,1)S(1)} %get-tuple-element.31), channel_id=1, source_target_pairs={{0,4},{1,5},{2,6},{3,7},{4,0},{5,1},{6,2},{7,3},{8,12},{9,13},{10,... | collective-permute-start | bytes 786440 | tf_op jit(solution)/shard_map/ppermute | solution.py:244
  9.4 2.0 %collective-permute-start.6 = (bf16[128,512]{1,0:T(8,128)(2,1)S(1)}, bf16[128,512]{1,0:T(8,128)(2,1)S(1)}, u32[]{:S(2)}, u32[]{:S(2)}) collective-permute-start(bf16[128,512]{1,0:T(8,128)(2,1)S(1)} %get-tuple-element.32.refs_3_.refs_1_), channel_id=1, source_target_pairs={{0,2},{1,3},{2,0},{3,1},{4,6},{5,7},{6,4},{7,5},{8,10},{9,11},{10,... | collective-permute-start | bytes 393224 | tf_op jit(solution)/shard_map/ppermute | solution.py:249
  11.5 1.5 %collective-permute-start.7 = (bf16[128,512]{1,0:T(8,128)(2,1)S(1)}, bf16[128,512]{1,0:T(8,128)(2,1)S(1)}, u32[]{:S(2)}, u32[]{:S(2)}) collective-permute-start(bf16[128,512]{1,0:T(8,128)(2,1)S(1)} %shard_map.48.refs_7_.refs_0_), channel_id=1, source_target_pairs={{0,2},{1,3},{2,0},{3,1},{4,6},{5,7},{6,4},{7,5},{8,10},{9,11},{10,... | collective-permute-start | bytes 393224 | tf_op jit(solution)/shard_map/ppermute | solution.py:256
  13.0 3.6 %collective-permute-done.3.refs_2_.refs_6_ = bf16[128,512]{1,0:T(8,128)(2,1)S(1)} collective-permute-done((bf16[128,512]{1,0:T(8,128)(2,1)S(1)}, bf16[128,512]{1,0:T(8,128)(2,1)S(1)}, u32[]{:S(2)}, u32[]{:S(2)}) %collective-permute-start.3) | collective-permute-done | bytes 131104 | tf_op jit(solution)/shard_map/ppermute | solution.py:246
  16.6 1.3 %collective-permute-start.4 = (bf16[128,512]{1,0:T(8,128)(2,1)S(1)}, bf16[128,512]{1,0:T(8,128)(2,1)S(1)}, u32[]{:S(2)}, u32[]{:S(2)}) collective-permute-start(bf16[128,512]{1,0:T(8,128)(2,1)S(1)} %shard_map.47), channel_id=1, source_target_pairs={{16,8},{17,9},{18,10},{19,11},{20,12},{21,13},{22,14},{23,15},{8,0... | collective-permute-start | bytes 393224 | tf_op jit(solution)/shard_map/ppermute | solution.py:261
  17.9 0.1 collective-permute-start.8
  18.0 5.4 %collective-permute-done.4.refs_5_ = bf16[128,512]{1,0:T(8,128)(2,1)S(1)} collective-permute-done((bf16[128,512]{1,0:T(8,128)(2,1)S(1)}, bf16[128,512]{1,0:T(8,128)(2,1)S(1)}, u32[]{:S(2)}, u32[]{:S(2)}) %collective-permute-start.4) | collective-permute-done | bytes 131104 | tf_op jit(solution)/shard_map/ppermute | solution.py:261
  23.4 1.0 %shard_map.49 = (f32[4,128,512]{2,1,0:T(8,128)S(1)}, bf16[4,128,512]{2,1,0:T(8,128)(2,1)S(1)}, bf16[512,384]{1,0:T(8,128)(2,1)S(1)}) custom-call(bf16[512,640]{1,0:T(8,128)(2,1)S(1)} %get-tuple-element.29.refs_0_.refs_3_, bf16[256,512]{1,0:T(8,128)(2,1)S(1)} %collective-permute-done.refs_1_.refs_0_, bf16[512,256]{1,0:T(8,128)(2,1)S(1)} %collective-permute-done.1.refs_2_, ...), custom_call_target="tpu_custom_call" | custom-call | flops 1 | bytes 1 | tf_op jit(solution)/shard_map/pallas_call | solution.py:31
  24.5 0.8 %shard_map.51 = (f32[128,512]{1,0:T(8,128)S(1)}, f32[128,512]{1,0:T(8,128)S(1)}, bf16[128,512]{1,0:T(8,128)(2,1)S(1)}, bf16[128,512]{1,0:T(8,128)(2,1)S(1)}, bf16[128,512]{1,0:T(8,128)(2,1)S(1)}) custom-call(bf16[4,128,512]{2,1,0:T(8,128)(2,1)S(1)} %shard_map.50.refs_0_, bf16[4,128,512]{2,1,0:T(8,128)(2,1)S(1)} %collective-permute-done.8.refs_1_, ...), custom_call_target="tpu_custom_call" | custom-call | flops 1 | bytes 1 | tf_op jit(solution)/shard_map/pallas_call | solution.py:31
  25.3 1.5 %collective-permute-start.9 = (bf16[128,512]{1,0:T(8,128)(2,1)S(1)}, bf16[128,512]{1,0:T(8,128)(2,1)S(1)}, u32[]{:S(2)}, u32[]{:S(2)}) collective-permute-start(bf16[128,512]{1,0:T(8,128)(2,1)S(1)} %get-tuple-element.45), channel_id=1, source_target_pairs={{0,8},{1,9},{2,10},{3,11},{4,12},{5,13},{6,14},{7,15},{8,16},{9,17... | collective-permute-start | bytes 393224 | tf_op jit(solution)/shard_map/ppermute | solution.py:292
  26.8 0.1 shard_map.52
  26.9 1.5 %collective-permute-start.11 = (bf16[128,512]{1,0:T(8,128)(2,1)S(1)}, bf16[128,512]{1,0:T(8,128)(2,1)S(1)}, u32[]{:S(2)}, u32[]{:S(2)}) collective-permute-start(bf16[128,512]{1,0:T(8,128)(2,1)S(1)} %get-tuple-element.48), channel_id=1, source_target_pairs={{0,6},{1,7},{2,4},{3,5},{4,2},{5,3},{6,0},{7,1},{8,14},{9,15},{10,... | collective-permute-start | bytes 393224 | tf_op jit(solution)/shard_map/ppermute | solution.py:299
  28.4 1.5 %collective-permute-start.12 = (bf16[128,512]{1,0:T(8,128)(2,1)S(1)}, bf16[128,512]{1,0:T(8,128)(2,1)S(1)}, u32[]{:S(2)}, u32[]{:S(2)}) collective-permute-start(bf16[128,512]{1,0:T(8,128)(2,1)S(1)} %get-tuple-element.49), channel_id=1, source_target_pairs={{0,16},{1,17},{2,18},{3,19},{4,20},{5,21},{6,22},{7,23},{8,24},{9,... | collective-permute-start | bytes 393224 | tf_op jit(solution)/shard_map/ppermute | solution.py:303
  29.9 0.6 %collective-permute-start.13 = (bf16[128,512]{1,0:T(8,128)(2,1)S(1)}, bf16[128,512]{1,0:T(8,128)(2,1)S(1)}, u32[]{:S(2)}, u32[]{:S(2)}) collective-permute-start(bf16[128,512]{1,0:T(8,128)(2,1)S(1)} %get-tuple-element.51), channel_id=1, source_target_pairs={{0,2},{1,3},{2,0},{3,1},{4,6},{5,7},{6,4},{7,5},{8,10},{9,11},{10,... | collective-permute-start | bytes 393224 | tf_op jit(solution)/shard_map/ppermute | solution.py:299
  30.5 1.3 %collective-permute-start.14 = (bf16[128,512]{1,0:T(8,128)(2,1)S(1)}, bf16[128,512]{1,0:T(8,128)(2,1)S(1)}, u32[]{:S(2)}, u32[]{:S(2)}) collective-permute-start(bf16[128,512]{1,0:T(8,128)(2,1)S(1)} %get-tuple-element.52), channel_id=1, source_target_pairs={{0,4},{1,5},{2,6},{3,7},{4,0},{5,1},{6,2},{7,3},{8,12},{9,13},{10,... | collective-permute-start | bytes 393224 | tf_op jit(solution)/shard_map/ppermute | solution.py:299
  31.9 1.3 %collective-permute-start.10 = (bf16[128,512]{1,0:T(8,128)(2,1)S(1)}, bf16[128,512]{1,0:T(8,128)(2,1)S(1)}, u32[]{:S(2)}, u32[]{:S(2)}) collective-permute-start(bf16[128,512]{1,0:T(8,128)(2,1)S(1)} %shard_map.53), channel_id=1, source_target_pairs={{0,24},{1,25},{2,26},{3,27},{4,28},{5,29},{6,30},{7,31}} | collective-permute-start | bytes 393224 | tf_op jit(solution)/shard_map/ppermute | solution.py:303
  33.2 0.6 %collective-permute-done.11.refs_6_ = bf16[128,512]{1,0:T(8,128)(2,1)S(1)} collective-permute-done((bf16[128,512]{1,0:T(8,128)(2,1)S(1)}, bf16[128,512]{1,0:T(8,128)(2,1)S(1)}, u32[]{:S(2)}, u32[]{:S(2)}) %collective-permute-start.11) | collective-permute-done | bytes 131104 | tf_op jit(solution)/shard_map/ppermute | solution.py:299
  33.8 1.7 %collective-permute-done.13.refs_9_ = bf16[128,512]{1,0:T(8,128)(2,1)S(1)} collective-permute-done((bf16[128,512]{1,0:T(8,128)(2,1)S(1)}, bf16[128,512]{1,0:T(8,128)(2,1)S(1)}, u32[]{:S(2)}, u32[]{:S(2)}) %collective-permute-start.13) | collective-permute-done | bytes 131104 | tf_op jit(solution)/shard_map/ppermute | solution.py:299
  35.5 0.9 %collective-permute-done.14.refs_10_ = bf16[128,512]{1,0:T(8,128)(2,1)S(1)} collective-permute-done((bf16[128,512]{1,0:T(8,128)(2,1)S(1)}, bf16[128,512]{1,0:T(8,128)(2,1)S(1)}, u32[]{:S(2)}, u32[]{:S(2)}) %collective-permute-start.14) | collective-permute-done | bytes 131104 | tf_op jit(solution)/shard_map/ppermute | solution.py:299
  36.4 0.9 %shard_map.54 = f32[128,512]{1,0:T(8,128)} custom-call(f32[128,512]{1,0:T(8,128)S(1)} %get-tuple-element.43.refs_0_, bf16[128,512]{1,0:T(8,128)(2,1)S(1)} %get-tuple-element.32.refs_3_.refs_1_, f32[2,128]{1,0:T(2,128)S(1)} %get-tuple-element.44.refs_2_, bf16[128,512]{1,0:T(8,128)(2,1)S(1)} %collective-permute-done.9.refs_1_.refs_3_, ...), custom_call_target="tpu_custom_call" | custom-call | flops 1 | bytes 1 | tf_op jit(solution)/shard_map/pallas_call | solution.py:31
  (15 shorter events, 0.2 us)
Async XLA Ops:
  1.9 9.6 %collective-permute-start = (bf16[256,512]{1,0:T(8,128)(2,1)S(1)}, bf16[256,512]{1,0:T(8,128)(2,1)S(1)}, u32[]{:S(2)}, u32[]{:S(2)}) collective-permute-start(bf16[256,512]{1,0:T(8,128)(2,1)S(1)} %get-tuple-element.30), channel_id=1, source_target_pairs={{0,4},{1,5},{2,6},{3,7},{4,0},{5,1},{6,2},{7,3},{8,12},{9,13},{10,... | collective-permute-start | bytes 786440 | tf_op jit(solution)/shard_map/ppermute | solution.py:241
  4.9 8.1 %collective-permute-start.2 = (bf16[128,512]{1,0:T(8,128)(2,1)S(1)}, bf16[128,512]{1,0:T(8,128)(2,1)S(1)}, u32[]{:S(2)}, u32[]{:S(2)}) collective-permute-start(bf16[128,512]{1,0:T(8,128)(2,1)S(1)} %get-tuple-element.32.refs_3_.refs_1_), channel_id=1, source_target_pairs={{8,0},{9,1},{10,2},{11,3},{12,4},{13,5},{14,6},{15,7},{16,8},{17,9... | collective-permute-start | bytes 393224 | tf_op jit(solution)/shard_map/ppermute | solution.py:242
  6.2 10.4 %collective-permute-start.3 = (bf16[128,512]{1,0:T(8,128)(2,1)S(1)}, bf16[128,512]{1,0:T(8,128)(2,1)S(1)}, u32[]{:S(2)}, u32[]{:S(2)}) collective-permute-start(bf16[128,512]{1,0:T(8,128)(2,1)S(1)} %get-tuple-element.32.refs_3_.refs_1_), channel_id=1, source_target_pairs={{24,0},{25,1},{26,2},{27,3},{28,4},{29,5},{30,6},{31,7}} | collective-permute-start | bytes 393224 | tf_op jit(solution)/shard_map/ppermute | solution.py:246
  7.5 10.5 %collective-permute-start.1 = (bf16[512,256]{1,0:T(8,128)(2,1)S(1)}, bf16[512,256]{1,0:T(8,128)(2,1)S(1)}, u32[]{:S(2)}, u32[]{:S(2)}) collective-permute-start(bf16[512,256]{1,0:T(8,128)(2,1)S(1)} %get-tuple-element.31), channel_id=1, source_target_pairs={{0,4},{1,5},{2,6},{3,7},{4,0},{5,1},{6,2},{7,3},{8,12},{9,13},{10,... | collective-permute-start | bytes 786440 | tf_op jit(solution)/shard_map/ppermute | solution.py:244
  9.4 8.5 %collective-permute-start.6 = (bf16[128,512]{1,0:T(8,128)(2,1)S(1)}, bf16[128,512]{1,0:T(8,128)(2,1)S(1)}, u32[]{:S(2)}, u32[]{:S(2)}) collective-permute-start(bf16[128,512]{1,0:T(8,128)(2,1)S(1)} %get-tuple-element.32.refs_3_.refs_1_), channel_id=1, source_target_pairs={{0,2},{1,3},{2,0},{3,1},{4,6},{5,7},{6,4},{7,5},{8,10},{9,11},{10,... | collective-permute-start | bytes 393224 | tf_op jit(solution)/shard_map/ppermute | solution.py:249
  11.5 6.4 %collective-permute-start.7 = (bf16[128,512]{1,0:T(8,128)(2,1)S(1)}, bf16[128,512]{1,0:T(8,128)(2,1)S(1)}, u32[]{:S(2)}, u32[]{:S(2)}) collective-permute-start(bf16[128,512]{1,0:T(8,128)(2,1)S(1)} %shard_map.48.refs_7_.refs_0_), channel_id=1, source_target_pairs={{0,2},{1,3},{2,0},{3,1},{4,6},{5,7},{6,4},{7,5},{8,10},{9,11},{10,... | collective-permute-start | bytes 393224 | tf_op jit(solution)/shard_map/ppermute | solution.py:256
  16.6 6.9 %collective-permute-start.4 = (bf16[128,512]{1,0:T(8,128)(2,1)S(1)}, bf16[128,512]{1,0:T(8,128)(2,1)S(1)}, u32[]{:S(2)}, u32[]{:S(2)}) collective-permute-start(bf16[128,512]{1,0:T(8,128)(2,1)S(1)} %shard_map.47), channel_id=1, source_target_pairs={{16,8},{17,9},{18,10},{19,11},{20,12},{21,13},{22,14},{23,15},{8,0... | collective-permute-start | bytes 393224 | tf_op jit(solution)/shard_map/ppermute | solution.py:261
  17.9 6.5 %collective-permute-start.8 = (bf16[4,128,512]{2,1,0:T(8,128)(2,1)S(1)}, bf16[4,128,512]{2,1,0:T(8,128)(2,1)S(1)}, u32[]{:S(2)}, u32[]{:S(2)}) collective-permute-start(bf16[4,128,512]{2,1,0:T(8,128)(2,1)S(1)} %shard_map.50.refs_0_), channel_id=1, source_target_pairs={{0,1},{1,0},{2,3},{3,2},{4,5},{5,4},{6,7},{7,6},{8,9},{9,8},{10,11... | collective-permute-start | bytes 1572872 | tf_op jit(solution)/shard_map/ppermute | solution.py:272
  24.4 2.4 %collective-permute-start.5 = (bf16[4,128,512]{2,1,0:T(8,128)(2,1)S(1)}, bf16[4,128,512]{2,1,0:T(8,128)(2,1)S(1)}, u32[]{:S(2)}, u32[]{:S(2)}) collective-permute-start(bf16[4,128,512]{2,1,0:T(8,128)(2,1)S(1)} %get-tuple-element.38), channel_id=1, source_target_pairs={{0,1},{1,0},{2,3},{3,2},{4,5},{5,4},{6,7},{7,6},{8,9},{9,8},{10,11... | collective-permute-start | bytes 1572872 | tf_op jit(solution)/shard_map/ppermute | solution.py:281
  25.3 6.5 %collective-permute-start.9 = (bf16[128,512]{1,0:T(8,128)(2,1)S(1)}, bf16[128,512]{1,0:T(8,128)(2,1)S(1)}, u32[]{:S(2)}, u32[]{:S(2)}) collective-permute-start(bf16[128,512]{1,0:T(8,128)(2,1)S(1)} %get-tuple-element.45), channel_id=1, source_target_pairs={{0,8},{1,9},{2,10},{3,11},{4,12},{5,13},{6,14},{7,15},{8,16},{9,17... | collective-permute-start | bytes 393224 | tf_op jit(solution)/shard_map/ppermute | solution.py:292
  26.9 6.8 %collective-permute-start.11 = (bf16[128,512]{1,0:T(8,128)(2,1)S(1)}, bf16[128,512]{1,0:T(8,128)(2,1)S(1)}, u32[]{:S(2)}, u32[]{:S(2)}) collective-permute-start(bf16[128,512]{1,0:T(8,128)(2,1)S(1)} %get-tuple-element.48), channel_id=1, source_target_pairs={{0,6},{1,7},{2,4},{3,5},{4,2},{5,3},{6,0},{7,1},{8,14},{9,15},{10,... | collective-permute-start | bytes 393224 | tf_op jit(solution)/shard_map/ppermute | solution.py:299
  28.4 5.3 %collective-permute-start.12 = (bf16[128,512]{1,0:T(8,128)(2,1)S(1)}, bf16[128,512]{1,0:T(8,128)(2,1)S(1)}, u32[]{:S(2)}, u32[]{:S(2)}) collective-permute-start(bf16[128,512]{1,0:T(8,128)(2,1)S(1)} %get-tuple-element.49), channel_id=1, source_target_pairs={{0,16},{1,17},{2,18},{3,19},{4,20},{5,21},{6,22},{7,23},{8,24},{9,... | collective-permute-start | bytes 393224 | tf_op jit(solution)/shard_map/ppermute | solution.py:303
  29.9 5.6 %collective-permute-start.13 = (bf16[128,512]{1,0:T(8,128)(2,1)S(1)}, bf16[128,512]{1,0:T(8,128)(2,1)S(1)}, u32[]{:S(2)}, u32[]{:S(2)}) collective-permute-start(bf16[128,512]{1,0:T(8,128)(2,1)S(1)} %get-tuple-element.51), channel_id=1, source_target_pairs={{0,2},{1,3},{2,0},{3,1},{4,6},{5,7},{6,4},{7,5},{8,10},{9,11},{10,... | collective-permute-start | bytes 393224 | tf_op jit(solution)/shard_map/ppermute | solution.py:299
  30.5 5.9 %collective-permute-start.14 = (bf16[128,512]{1,0:T(8,128)(2,1)S(1)}, bf16[128,512]{1,0:T(8,128)(2,1)S(1)}, u32[]{:S(2)}, u32[]{:S(2)}) collective-permute-start(bf16[128,512]{1,0:T(8,128)(2,1)S(1)} %get-tuple-element.52), channel_id=1, source_target_pairs={{0,4},{1,5},{2,6},{3,7},{4,0},{5,1},{6,2},{7,3},{8,12},{9,13},{10,... | collective-permute-start | bytes 393224 | tf_op jit(solution)/shard_map/ppermute | solution.py:299
  31.9 4.5 %collective-permute-start.10 = (bf16[128,512]{1,0:T(8,128)(2,1)S(1)}, bf16[128,512]{1,0:T(8,128)(2,1)S(1)}, u32[]{:S(2)}, u32[]{:S(2)}) collective-permute-start(bf16[128,512]{1,0:T(8,128)(2,1)S(1)} %shard_map.53), channel_id=1, source_target_pairs={{0,24},{1,25},{2,26},{3,27},{4,28},{5,29},{6,30},{7,31}} | collective-permute-start | bytes 393224 | tf_op jit(solution)/shard_map/ppermute | solution.py:303

commit v6 on v5

--- a/solution.py
+++ b/solution.py
@@ -16,7 +16,7 @@
     return lax.broadcasted_iota(I32, shape, dim)
 
 
-def call(kernel, outs, *args, hbm=(), scratch=(), order=None):
+def call(kernel, outs, *args, hbm=(), scratch=(), order=None, to=pltpu.VMEM):
     if order is not None:
         inner, place = kernel, [order.index(i) for i in range(len(args))]
 
@@ -32,7 +32,7 @@
         kernel,
         out_shape=outs,
         in_specs=specs,
-        out_specs=[pl.BlockSpec(memory_space=pltpu.VMEM)] * len(outs),
+        out_specs=[pl.BlockSpec(memory_space=to)] * len(outs),
         scratch_shapes=list(scratch),
         cost_estimate=pl.CostEstimate(flops=1, bytes_accessed=1, transcendentals=0),
         compiler_params=pltpu.CompilerParams(vmem_limit_bytes=held + ROOM),
@@ -176,13 +176,21 @@
 
 
 def last_kernel(scale, probes, diag, *refs):
-    out = refs[-1]
-    total = refs[0][...].astype(F32)
-    for r in refs[1:-1]:
-        total = total + r[...].astype(F32)
-    pf = probes[...].astype(F32)
-    total = total + diag[:, 0:1] * pf
-    out[...] = scale[0:1, 0:1] * total + scale[1:2, 0:1] * pf
+    out, hold, sems = refs[-3:]
+    step = hold.shape[0] // 4
+    puts = []
+    for n in range(4):
+        at = pl.ds(n * step, step)
+        total = refs[0][at, :].astype(F32)
+        for r in refs[1:-3]:
+            total = total + r[at, :].astype(F32)
+        pf = probes[at, :].astype(F32)
+        total = total + diag[at, 0:1] * pf
+        hold[at, :] = scale[0:1, 0:1] * total + scale[1:2, 0:1] * pf
+        puts.append(pltpu.make_async_copy(hold.at[at, :], out.at[at, :], sems.at[n]))
+        puts[n].start()
+    for p in puts:
+        p.wait()
 
 
 def solution(mesh):
@@ -287,7 +295,7 @@
             order=[0, 1, 2, 3, 4] if nz == 4 else None,
         )
         steps = [1, 2, 3] if nz == 4 else list(range(1, nz))
-        direct, chain = (1, 1) if nz == 4 else (1, False)
+        direct, chain = (2, 1) if nz == 4 else (1, False)
         climbs = [[(z, z + d) for z in range(nz - d)] for d in steps]
         ups = [lax.ppermute(ms[d - 1], both, hop(*climbs[i])) for i, d in enumerate(steps) if i < direct]
         home, *rest = call(
@@ -303,7 +311,8 @@
             ups.append(lax.ppermute(h, both, hop(*climbs[direct + n])))
         tail = [scale, probes, diag, m0, home, *ups, *cross]
         (out,) = call(
-            last_kernel, [jax.ShapeDtypeStruct(blk, F32)], *tail,
+            last_kernel, [jax.ShapeDtypeStruct(blk, F32)], *tail, to=pl.ANY,
+            scratch=[pltpu.VMEM(blk, F32), pltpu.SemaphoreType.DMA((4,))],
             order=[4, 1, 0, 5, 7, 2, 10, 6, 3, 8, 9] if nz == 4 else None,
         )
         return out

time: 37.9 us -> 37.9 us (level)
    ppermute x1 -> x2, starting transfers between devices: 1.49 us -> 2.96 us  [body(): lax.ppermute(ms[d - 1], both, hop(*climbs[i]))]
    ppermute x2 -> x1, starting transfers between devices: 2.77 us -> 1.3 us  [body(): ups.append(lax.ppermute(h, both, hop(*climbs[direct + n])))]
where the time goes in v6:
time: 37.9 us; the launch traced here: 37.3 us
  starting transfers between devices  20.2 us (53%)
  waiting for transfers between devices  12.3 us (32%)
  Pallas kernels  4.64 us (12%)
    ppermute x1, waiting for transfers between devices, body(): downs[2] = lax.ppermute(handed, both, hop((2, 1), (1, 0)))  5.41 us
    pallas_call x9, Pallas kernels, call(): pl.pallas_call(kernel, out_shape=outs, in_specs=specs, out_specs=[pl.Bloc...  4.64 us
    ppermute x1, waiting for transfers between devices, body(): downs[3] = lax.ppermute(probes, both, down(3))  3.57 us
    ppermute x3, starting transfers between devices, body(): lax.ppermute(p, both, shift(s, e))  3.43 us
    ppermute x3, waiting for transfers between devices, body(): lax.ppermute(p, both, shift(s, e))  3.22 us
    ppermute x1, starting transfers between devices, body(): oth1 = lax.ppermute(give1, both, shift(1, 0))  3.03 us
    ppermute x2, starting transfers between devices, body(): lax.ppermute(ms[d - 1], both, hop(*climbs[i]))  2.96 us
    ppermute x1, starting transfers between devices, body(): near[0, e] = lax.ppermute(probes, both, shift(0, nx - e))  2.04 us
  transfers between devices with their start and end apart: 15, of which 5 were waited for; matrix products, arithmetic and copies ran while one was open for 0% of the time, Pallas kernels for 5%

profile of v6, /device:TPU:0, one launch (start us, length us, event | category | flops | bytes accessed | tf_op | source)
XLA Modules:
  0.0 37.3 jit_solution(1262143155748056517)
XLA Ops:
  0.0 1.9 %shard_map.46 = (bf16[128,512]{1,0:T(8,128)(2,1)S(1)}, bf16[512,640]{1,0:T(8,128)(2,1)S(1)}, bf16[256,512]{1,0:T(8,128)(2,1)S(1)}, bf16[512,256]{1,0:T(8,128)(2,...) custom-call(bf16[4096,128]{1,0:T(8,128)(2,1)} %bitcast.3, s32[128,512]{1,0:T(8,128)} %signs_hbm.1, ...), custom_call_target="tpu_custom_call" | custom-call | flops 1 | bytes 1 | tf_op jit(solution)/shard_map/pallas_call | solution.py:31
  1.9 3.0 %collective-permute-start = (bf16[256,512]{1,0:T(8,128)(2,1)S(1)}, bf16[256,512]{1,0:T(8,128)(2,1)S(1)}, u32[]{:S(2)}, u32[]{:S(2)}) collective-permute-start(bf16[256,512]{1,0:T(8,128)(2,1)S(1)} %get-tuple-element.29), channel_id=1, source_target_pairs={{0,4},{1,5},{2,6},{3,7},{4,0},{5,1},{6,2},{7,3},{8,12},{9,13},{10,... | collective-permute-start | bytes 786440 | tf_op jit(solution)/shard_map/ppermute | solution.py:249
  4.9 1.3 %collective-permute-start.2 = (bf16[128,512]{1,0:T(8,128)(2,1)S(1)}, bf16[128,512]{1,0:T(8,128)(2,1)S(1)}, u32[]{:S(2)}, u32[]{:S(2)}) collective-permute-start(bf16[128,512]{1,0:T(8,128)(2,1)S(1)} %get-tuple-element.31.refs_3_.refs_1_), channel_id=1, source_target_pairs={{8,0},{9,1},{10,2},{11,3},{12,4},{13,5},{14,6},{15,7},{16,8},{17,9... | collective-permute-start | bytes 393224 | tf_op jit(solution)/shard_map/ppermute | solution.py:250
  6.2 1.3 %collective-permute-start.3 = (bf16[128,512]{1,0:T(8,128)(2,1)S(1)}, bf16[128,512]{1,0:T(8,128)(2,1)S(1)}, u32[]{:S(2)}, u32[]{:S(2)}) collective-permute-start(bf16[128,512]{1,0:T(8,128)(2,1)S(1)} %get-tuple-element.31.refs_3_.refs_1_), channel_id=1, source_target_pairs={{24,0},{25,1},{26,2},{27,3},{28,4},{29,5},{30,6},{31,7}} | collective-permute-start | bytes 393224 | tf_op jit(solution)/shard_map/ppermute | solution.py:254
  7.5 1.9 %collective-permute-start.1 = (bf16[512,256]{1,0:T(8,128)(2,1)S(1)}, bf16[512,256]{1,0:T(8,128)(2,1)S(1)}, u32[]{:S(2)}, u32[]{:S(2)}) collective-permute-start(bf16[512,256]{1,0:T(8,128)(2,1)S(1)} %get-tuple-element.30), channel_id=1, source_target_pairs={{0,4},{1,5},{2,6},{3,7},{4,0},{5,1},{6,2},{7,3},{8,12},{9,13},{10,... | collective-permute-start | bytes 786440 | tf_op jit(solution)/shard_map/ppermute | solution.py:252
  9.4 2.0 %collective-permute-start.6 = (bf16[128,512]{1,0:T(8,128)(2,1)S(1)}, bf16[128,512]{1,0:T(8,128)(2,1)S(1)}, u32[]{:S(2)}, u32[]{:S(2)}) collective-permute-start(bf16[128,512]{1,0:T(8,128)(2,1)S(1)} %get-tuple-element.31.refs_3_.refs_1_), channel_id=1, source_target_pairs={{0,2},{1,3},{2,0},{3,1},{4,6},{5,7},{6,4},{7,5},{8,10},{9,11},{10,... | collective-permute-start | bytes 393224 | tf_op jit(solution)/shard_map/ppermute | solution.py:257
  11.5 1.5 %collective-permute-start.7 = (bf16[128,512]{1,0:T(8,128)(2,1)S(1)}, bf16[128,512]{1,0:T(8,128)(2,1)S(1)}, u32[]{:S(2)}, u32[]{:S(2)}) collective-permute-start(bf16[128,512]{1,0:T(8,128)(2,1)S(1)} %shard_map.48.refs_7_.refs_0_), channel_id=1, source_target_pairs={{0,2},{1,3},{2,0},{3,1},{4,6},{5,7},{6,4},{7,5},{8,10},{9,11},{10,... | collective-permute-start | bytes 393224 | tf_op jit(solution)/shard_map/ppermute | solution.py:264
  13.0 3.6 %collective-permute-done.3.refs_2_.refs_6_ = bf16[128,512]{1,0:T(8,128)(2,1)S(1)} collective-permute-done((bf16[128,512]{1,0:T(8,128)(2,1)S(1)}, bf16[128,512]{1,0:T(8,128)(2,1)S(1)}, u32[]{:S(2)}, u32[]{:S(2)}) %collective-permute-start.3) | collective-permute-done | bytes 131104 | tf_op jit(solution)/shard_map/ppermute | solution.py:254
  16.6 1.3 %collective-permute-start.4 = (bf16[128,512]{1,0:T(8,128)(2,1)S(1)}, bf16[128,512]{1,0:T(8,128)(2,1)S(1)}, u32[]{:S(2)}, u32[]{:S(2)}) collective-permute-start(bf16[128,512]{1,0:T(8,128)(2,1)S(1)} %shard_map.47), channel_id=1, source_target_pairs={{16,8},{17,9},{18,10},{19,11},{20,12},{21,13},{22,14},{23,15},{8,0... | collective-permute-start | bytes 393224 | tf_op jit(solution)/shard_map/ppermute | solution.py:269
  17.9 0.1 collective-permute-start.8
  18.0 5.4 %collective-permute-done.4.refs_5_ = bf16[128,512]{1,0:T(8,128)(2,1)S(1)} collective-permute-done((bf16[128,512]{1,0:T(8,128)(2,1)S(1)}, bf16[128,512]{1,0:T(8,128)(2,1)S(1)}, u32[]{:S(2)}, u32[]{:S(2)}) %collective-permute-start.4) | collective-permute-done | bytes 131104 | tf_op jit(solution)/shard_map/ppermute | solution.py:269
  23.4 1.0 %shard_map.49 = (f32[4,128,512]{2,1,0:T(8,128)S(1)}, bf16[4,128,512]{2,1,0:T(8,128)(2,1)S(1)}, bf16[512,384]{1,0:T(8,128)(2,1)S(1)}) custom-call(bf16[512,640]{1,0:T(8,128)(2,1)S(1)} %get-tuple-element.28.refs_0_.refs_3_, bf16[256,512]{1,0:T(8,128)(2,1)S(1)} %collective-permute-done.refs_1_.refs_0_, bf16[512,256]{1,0:T(8,128)(2,1)S(1)} %collective-permute-done.1.refs_2_, ...), custom_call_target="tpu_custom_call" | custom-call | flops 1 | bytes 1 | tf_op jit(solution)/shard_map/pallas_call | solution.py:31
  24.5 0.8 %shard_map.51 = (f32[128,512]{1,0:T(8,128)S(1)}, f32[128,512]{1,0:T(8,128)S(1)}, bf16[128,512]{1,0:T(8,128)(2,1)S(1)}, bf16[128,512]{1,0:T(8,128)(2,1)S(1)}, bf16[128,512]{1,0:T(8,128)(2,1)S(1)}) custom-call(bf16[4,128,512]{2,1,0:T(8,128)(2,1)S(1)} %shard_map.50.refs_0_, bf16[4,128,512]{2,1,0:T(8,128)(2,1)S(1)} %collective-permute-done.8.refs_1_, ...), custom_call_target="tpu_custom_call" | custom-call | flops 1 | bytes 1 | tf_op jit(solution)/shard_map/pallas_call | solution.py:31
  25.3 1.5 %collective-permute-start.9 = (bf16[128,512]{1,0:T(8,128)(2,1)S(1)}, bf16[128,512]{1,0:T(8,128)(2,1)S(1)}, u32[]{:S(2)}, u32[]{:S(2)}) collective-permute-start(bf16[128,512]{1,0:T(8,128)(2,1)S(1)} %get-tuple-element.43), channel_id=1, source_target_pairs={{0,8},{1,9},{2,10},{3,11},{4,12},{5,13},{6,14},{7,15},{8,16},{9,17... | collective-permute-start | bytes 393224 | tf_op jit(solution)/shard_map/ppermute | solution.py:300
  26.8 0.1 shard_map.52
  26.9 1.5 %collective-permute-start.11 = (bf16[128,512]{1,0:T(8,128)(2,1)S(1)}, bf16[128,512]{1,0:T(8,128)(2,1)S(1)}, u32[]{:S(2)}, u32[]{:S(2)}) collective-permute-start(bf16[128,512]{1,0:T(8,128)(2,1)S(1)} %get-tuple-element.46), channel_id=1, source_target_pairs={{0,6},{1,7},{2,4},{3,5},{4,2},{5,3},{6,0},{7,1},{8,14},{9,15},{10,... | collective-permute-start | bytes 393224 | tf_op jit(solution)/shard_map/ppermute | solution.py:307
  28.4 1.5 %collective-permute-start.12 = (bf16[128,512]{1,0:T(8,128)(2,1)S(1)}, bf16[128,512]{1,0:T(8,128)(2,1)S(1)}, u32[]{:S(2)}, u32[]{:S(2)}) collective-permute-start(bf16[128,512]{1,0:T(8,128)(2,1)S(1)} %get-tuple-element.47), channel_id=1, source_target_pairs={{0,16},{1,17},{2,18},{3,19},{4,20},{5,21},{6,22},{7,23},{8,24},{9,... | collective-permute-start | bytes 393224 | tf_op jit(solution)/shard_map/ppermute | solution.py:300
  29.9 0.6 %collective-permute-start.13 = (bf16[128,512]{1,0:T(8,128)(2,1)S(1)}, bf16[128,512]{1,0:T(8,128)(2,1)S(1)}, u32[]{:S(2)}, u32[]{:S(2)}) collective-permute-start(bf16[128,512]{1,0:T(8,128)(2,1)S(1)} %get-tuple-element.49), channel_id=1, source_target_pairs={{0,2},{1,3},{2,0},{3,1},{4,6},{5,7},{6,4},{7,5},{8,10},{9,11},{10,... | collective-permute-start | bytes 393224 | tf_op jit(solution)/shard_map/ppermute | solution.py:307
  30.5 1.3 %collective-permute-start.14 = (bf16[128,512]{1,0:T(8,128)(2,1)S(1)}, bf16[128,512]{1,0:T(8,128)(2,1)S(1)}, u32[]{:S(2)}, u32[]{:S(2)}) collective-permute-start(bf16[128,512]{1,0:T(8,128)(2,1)S(1)} %get-tuple-element.50), channel_id=1, source_target_pairs={{0,4},{1,5},{2,6},{3,7},{4,0},{5,1},{6,2},{7,3},{8,12},{9,13},{10,... | collective-permute-start | bytes 393224 | tf_op jit(solution)/shard_map/ppermute | solution.py:307
  31.9 1.3 %collective-permute-start.10 = (bf16[128,512]{1,0:T(8,128)(2,1)S(1)}, bf16[128,512]{1,0:T(8,128)(2,1)S(1)}, u32[]{:S(2)}, u32[]{:S(2)}) collective-permute-start(bf16[128,512]{1,0:T(8,128)(2,1)S(1)} %shard_map.53), channel_id=1, source_target_pairs={{0,24},{1,25},{2,26},{3,27},{4,28},{5,29},{6,30},{7,31}} | collective-permute-start | bytes 393224 | tf_op jit(solution)/shard_map/ppermute | solution.py:311
  33.2 0.6 %collective-permute-done.11.refs_6_ = bf16[128,512]{1,0:T(8,128)(2,1)S(1)} collective-permute-done((bf16[128,512]{1,0:T(8,128)(2,1)S(1)}, bf16[128,512]{1,0:T(8,128)(2,1)S(1)}, u32[]{:S(2)}, u32[]{:S(2)}) %collective-permute-start.11) | collective-permute-done | bytes 131104 | tf_op jit(solution)/shard_map/ppermute | solution.py:307
  33.8 1.7 %collective-permute-done.13.refs_9_ = bf16[128,512]{1,0:T(8,128)(2,1)S(1)} collective-permute-done((bf16[128,512]{1,0:T(8,128)(2,1)S(1)}, bf16[128,512]{1,0:T(8,128)(2,1)S(1)}, u32[]{:S(2)}, u32[]{:S(2)}) %collective-permute-start.13) | collective-permute-done | bytes 131104 | tf_op jit(solution)/shard_map/ppermute | solution.py:307
  35.5 0.9 %collective-permute-done.14.refs_10_ = bf16[128,512]{1,0:T(8,128)(2,1)S(1)} collective-permute-done((bf16[128,512]{1,0:T(8,128)(2,1)S(1)}, bf16[128,512]{1,0:T(8,128)(2,1)S(1)}, u32[]{:S(2)}, u32[]{:S(2)}) %collective-permute-start.14) | collective-permute-done | bytes 131104 | tf_op jit(solution)/shard_map/ppermute | solution.py:307
  36.4 0.9 %shard_map.54 = f32[128,512]{1,0:T(8,128)} custom-call(f32[128,512]{1,0:T(8,128)S(1)} %get-tuple-element.41.refs_0_, bf16[128,512]{1,0:T(8,128)(2,1)S(1)} %get-tuple-element.31.refs_3_.refs_1_, f32[2,128]{1,0:T(2,128)S(1)} %get-tuple-element.42.refs_2_, bf16[128,512]{1,0:T(8,128)(2,1)S(1)} %collective-permute-done.9.refs_1_.refs_3_, ...), custom_call_target="tpu_custom_call" | custom-call | flops 1 | bytes 1 | tf_op jit(solution)/shard_map/pallas_call | solution.py:31
  (15 shorter events, 0.2 us)
Async XLA Ops:
  1.9 9.6 %collective-permute-start = (bf16[256,512]{1,0:T(8,128)(2,1)S(1)}, bf16[256,512]{1,0:T(8,128)(2,1)S(1)}, u32[]{:S(2)}, u32[]{:S(2)}) collective-permute-start(bf16[256,512]{1,0:T(8,128)(2,1)S(1)} %get-tuple-element.29), channel_id=1, source_target_pairs={{0,4},{1,5},{2,6},{3,7},{4,0},{5,1},{6,2},{7,3},{8,12},{9,13},{10,... | collective-permute-start | bytes 786440 | tf_op jit(solution)/shard_map/ppermute | solution.py:249
  4.9 8.1 %collective-permute-start.2 = (bf16[128,512]{1,0:T(8,128)(2,1)S(1)}, bf16[128,512]{1,0:T(8,128)(2,1)S(1)}, u32[]{:S(2)}, u32[]{:S(2)}) collective-permute-start(bf16[128,512]{1,0:T(8,128)(2,1)S(1)} %get-tuple-element.31.refs_3_.refs_1_), channel_id=1, source_target_pairs={{8,0},{9,1},{10,2},{11,3},{12,4},{13,5},{14,6},{15,7},{16,8},{17,9... | collective-permute-start | bytes 393224 | tf_op jit(solution)/shard_map/ppermute | solution.py:250
  6.2 10.4 %collective-permute-start.3 = (bf16[128,512]{1,0:T(8,128)(2,1)S(1)}, bf16[128,512]{1,0:T(8,128)(2,1)S(1)}, u32[]{:S(2)}, u32[]{:S(2)}) collective-permute-start(bf16[128,512]{1,0:T(8,128)(2,1)S(1)} %get-tuple-element.31.refs_3_.refs_1_), channel_id=1, source_target_pairs={{24,0},{25,1},{26,2},{27,3},{28,4},{29,5},{30,6},{31,7}} | collective-permute-start | bytes 393224 | tf_op jit(solution)/shard_map/ppermute | solution.py:254
  7.5 10.5 %collective-permute-start.1 = (bf16[512,256]{1,0:T(8,128)(2,1)S(1)}, bf16[512,256]{1,0:T(8,128)(2,1)S(1)}, u32[]{:S(2)}, u32[]{:S(2)}) collective-permute-start(bf16[512,256]{1,0:T(8,128)(2,1)S(1)} %get-tuple-element.30), channel_id=1, source_target_pairs={{0,4},{1,5},{2,6},{3,7},{4,0},{5,1},{6,2},{7,3},{8,12},{9,13},{10,... | collective-permute-start | bytes 786440 | tf_op jit(solution)/shard_map/ppermute | solution.py:252
  9.4 8.5 %collective-permute-start.6 = (bf16[128,512]{1,0:T(8,128)(2,1)S(1)}, bf16[128,512]{1,0:T(8,128)(2,1)S(1)}, u32[]{:S(2)}, u32[]{:S(2)}) collective-permute-start(bf16[128,512]{1,0:T(8,128)(2,1)S(1)} %get-tuple-element.31.refs_3_.refs_1_), channel_id=1, source_target_pairs={{0,2},{1,3},{2,0},{3,1},{4,6},{5,7},{6,4},{7,5},{8,10},{9,11},{10,... | collective-permute-start | bytes 393224 | tf_op jit(solution)/shard_map/ppermute | solution.py:257
  11.5 6.4 %collective-permute-start.7 = (bf16[128,512]{1,0:T(8,128)(2,1)S(1)}, bf16[128,512]{1,0:T(8,128)(2,1)S(1)}, u32[]{:S(2)}, u32[]{:S(2)}) collective-permute-start(bf16[128,512]{1,0:T(8,128)(2,1)S(1)} %shard_map.48.refs_7_.refs_0_), channel_id=1, source_target_pairs={{0,2},{1,3},{2,0},{3,1},{4,6},{5,7},{6,4},{7,5},{8,10},{9,11},{10,... | collective-permute-start | bytes 393224 | tf_op jit(solution)/shard_map/ppermute | solution.py:264
  16.6 6.9 %collective-permute-start.4 = (bf16[128,512]{1,0:T(8,128)(2,1)S(1)}, bf16[128,512]{1,0:T(8,128)(2,1)S(1)}, u32[]{:S(2)}, u32[]{:S(2)}) collective-permute-start(bf16[128,512]{1,0:T(8,128)(2,1)S(1)} %shard_map.47), channel_id=1, source_target_pairs={{16,8},{17,9},{18,10},{19,11},{20,12},{21,13},{22,14},{23,15},{8,0... | collective-permute-start | bytes 393224 | tf_op jit(solution)/shard_map/ppermute | solution.py:269
  17.9 6.5 %collective-permute-start.8 = (bf16[4,128,512]{2,1,0:T(8,128)(2,1)S(1)}, bf16[4,128,512]{2,1,0:T(8,128)(2,1)S(1)}, u32[]{:S(2)}, u32[]{:S(2)}) collective-permute-start(bf16[4,128,512]{2,1,0:T(8,128)(2,1)S(1)} %shard_map.50.refs_0_), channel_id=1, source_target_pairs={{0,1},{1,0},{2,3},{3,2},{4,5},{5,4},{6,7},{7,6},{8,9},{9,8},{10,11... | collective-permute-start | bytes 1572872 | tf_op jit(solution)/shard_map/ppermute | solution.py:280
  24.4 2.4 %collective-permute-start.5 = (bf16[4,128,512]{2,1,0:T(8,128)(2,1)S(1)}, bf16[4,128,512]{2,1,0:T(8,128)(2,1)S(1)}, u32[]{:S(2)}, u32[]{:S(2)}) collective-permute-start(bf16[4,128,512]{2,1,0:T(8,128)(2,1)S(1)} %get-tuple-element.37), channel_id=1, source_target_pairs={{0,1},{1,0},{2,3},{3,2},{4,5},{5,4},{6,7},{7,6},{8,9},{9,8},{10,11... | collective-permute-start | bytes 1572872 | tf_op jit(solution)/shard_map/ppermute | solution.py:289
  25.3 6.5 %collective-permute-start.9 = (bf16[128,512]{1,0:T(8,128)(2,1)S(1)}, bf16[128,512]{1,0:T(8,128)(2,1)S(1)}, u32[]{:S(2)}, u32[]{:S(2)}) collective-permute-start(bf16[128,512]{1,0:T(8,128)(2,1)S(1)} %get-tuple-element.43), channel_id=1, source_target_pairs={{0,8},{1,9},{2,10},{3,11},{4,12},{5,13},{6,14},{7,15},{8,16},{9,17... | collective-permute-start | bytes 393224 | tf_op jit(solution)/shard_map/ppermute | solution.py:300
  26.9 6.8 %collective-permute-start.11 = (bf16[128,512]{1,0:T(8,128)(2,1)S(1)}, bf16[128,512]{1,0:T(8,128)(2,1)S(1)}, u32[]{:S(2)}, u32[]{:S(2)}) collective-permute-start(bf16[128,512]{1,0:T(8,128)(2,1)S(1)} %get-tuple-element.46), channel_id=1, source_target_pairs={{0,6},{1,7},{2,4},{3,5},{4,2},{5,3},{6,0},{7,1},{8,14},{9,15},{10,... | collective-permute-start | bytes 393224 | tf_op jit(solution)/shard_map/ppermute | solution.py:307
  28.4 5.3 %collective-permute-start.12 = (bf16[128,512]{1,0:T(8,128)(2,1)S(1)}, bf16[128,512]{1,0:T(8,128)(2,1)S(1)}, u32[]{:S(2)}, u32[]{:S(2)}) collective-permute-start(bf16[128,512]{1,0:T(8,128)(2,1)S(1)} %get-tuple-element.47), channel_id=1, source_target_pairs={{0,16},{1,17},{2,18},{3,19},{4,20},{5,21},{6,22},{7,23},{8,24},{9,... | collective-permute-start | bytes 393224 | tf_op jit(solution)/shard_map/ppermute | solution.py:300
  29.9 5.6 %collective-permute-start.13 = (bf16[128,512]{1,0:T(8,128)(2,1)S(1)}, bf16[128,512]{1,0:T(8,128)(2,1)S(1)}, u32[]{:S(2)}, u32[]{:S(2)}) collective-permute-start(bf16[128,512]{1,0:T(8,128)(2,1)S(1)} %get-tuple-element.49), channel_id=1, source_target_pairs={{0,2},{1,3},{2,0},{3,1},{4,6},{5,7},{6,4},{7,5},{8,10},{9,11},{10,... | collective-permute-start | bytes 393224 | tf_op jit(solution)/shard_map/ppermute | solution.py:307
  30.5 5.9 %collective-permute-start.14 = (bf16[128,512]{1,0:T(8,128)(2,1)S(1)}, bf16[128,512]{1,0:T(8,128)(2,1)S(1)}, u32[]{:S(2)}, u32[]{:S(2)}) collective-permute-start(bf16[128,512]{1,0:T(8,128)(2,1)S(1)} %get-tuple-element.50), channel_id=1, source_target_pairs={{0,4},{1,5},{2,6},{3,7},{4,0},{5,1},{6,2},{7,3},{8,12},{9,13},{10,... | collective-permute-start | bytes 393224 | tf_op jit(solution)/shard_map/ppermute | solution.py:307
  31.9 4.5 %collective-permute-start.10 = (bf16[128,512]{1,0:T(8,128)(2,1)S(1)}, bf16[128,512]{1,0:T(8,128)(2,1)S(1)}, u32[]{:S(2)}, u32[]{:S(2)}) collective-permute-start(bf16[128,512]{1,0:T(8,128)(2,1)S(1)} %shard_map.53), channel_id=1, source_target_pairs={{0,24},{1,25},{2,26},{3,27},{4,28},{5,29},{6,30},{7,31}} | collective-permute-start | bytes 393224 | tf_op jit(solution)/shard_map/ppermute | solution.py:311
